TPU v7x, 32 devices: a whole 2x2x4 slice. The times are simulated.
32 devices in a mesh: region: 8 (over z, y), member: 4 (over x, core).
Axes of the slice: x: 2, y: 2, z: 4, core: 2. Of those that a mesh axis runs over, the one named last changes fastest.
Arguments:
- latent: bfloat16 [4, 2048, 512], P('member', 'region'), may hold values from -6 to 6
- node_gain: float32 [512], replicated, may hold values from 0.1 to 1.9
- w_qkv: bfloat16 [512, 1536], replicated, may hold values from -0.25 to 0.25
- w_out: bfloat16 [512, 512], replicated, may hold values from -0.25 to 0.25
- edge_bias: float32 [2048, 128], P('region'), may hold values from -6 to 400
- edge_source: int32 [2048, 8], P('region'), may hold values from 0 to 511, as said below
- boundary: int32 [8, 256], P('region'), may hold values from 0 to 255, as said below
- node_count: int32 [8], P('region'), may hold values from 128 to 256, as said below
- decoder_projection_weight: bfloat16 [512, 98], replicated, may hold values from -0.25 to 0.25
- dec_source: int32 [3, 8192], P(None, 'region'), may hold values from 0 to 511, as said below
- dec_weight: float32 [3, 8192], P(None, 'region'), may hold values from 0.2 to 1
- state: float32 [98, 8192], P(None, 'region'), may hold values from -6 to 6
- target: float32 [98, 8192], P(None, 'region'), may hold values from -6 to 6
- area: float32 [8192], P('region'), may hold values from 0.3 to 9
- var_weight: float32 [98], replicated, may hold values from 0.3 to 3
Outputs:
- loss: float32 [], replicated
- grad_qkv: float32 [512, 1536], P('region')
- grad_out: float32 [512, 512], P('region')
- decoder_weight_gradient: float32 [512, 98], P('region')
- grad_latent: bfloat16 [4, 2048, 512], P('member', 'region')
Inputs may be any that keep to these rules, and one draw needn't show every extreme that they name: Row n of edge_source belongs to region r = n // 256; each entry is below node_count[r], or is 256 + i with i below 256. Row r of boundary holds node slots below node_count[r]. `node_count`: equals 256 in at least one region. `dec_source`: column p belongs to region r = p // 1024; each entry is below node_count[r], or is 256 + i with i below 256.
All inputs are finite; a program needn't handle non-finite values.
Results may differ from a plain program's by a relative error of at most 0.02.
Values may be sent and summed in bfloat16 or wider, within the bound.
No kernel may reach another device: no remote copies, remote signals or barrier semaphores. Data moves between devices by JAX's collectives and lax.ppermute only.
A program may use at most 128 MiB of HBM per device.

v0:
```python
import math

import jax
import jax.numpy as jnp
from jax import lax
from jax.sharding import PartitionSpec as P

ALPHA = 0.95
NORM_EPS = 1e-05
SMOOTH_SQ = 0.25
SMOOTH_ROOT = 0.5


def padded(cells, sides, width):
    for axis, dim in sides:
        count = lax.axis_size(axis)
        head = lax.slice_in_dim(cells, 0, width, axis=dim)
        tail = lax.slice_in_dim(cells, cells.shape[dim] - width, cells.shape[dim], axis=dim)
        cells = jnp.concatenate(
            [
                lax.ppermute(tail, axis, [(i, (i + 1) % count) for i in range(count)]),
                cells,
                lax.ppermute(head, axis, [((i + 1) % count, i) for i in range(count)]),
            ],
            axis=dim,
        )
    return cells


def layer_norm(latent_rows, gain):
    values = latent_rows.astype(jnp.float32)
    center = values - jnp.mean(values, axis=-1, keepdims=True)
    inverse = lax.rsqrt(jnp.mean(center * center, axis=-1, keepdims=True) + NORM_EPS)
    return (center * inverse * gain).astype(jnp.bfloat16)


def norm_backward(latent_rows, gain, grad_rows):
    values = latent_rows.astype(jnp.float32)
    center = values - jnp.mean(values, axis=-1, keepdims=True)
    inverse = lax.rsqrt(jnp.mean(center * center, axis=-1, keepdims=True) + NORM_EPS)
    scaled = center * inverse
    scaled_grad = grad_rows * gain
    return inverse * (
        scaled_grad
        - jnp.mean(scaled_grad, axis=-1, keepdims=True)
        - scaled * jnp.mean(scaled_grad * scaled, axis=-1, keepdims=True)
    )


def attend(queries, key_value, bias_rows, edge_src):
    node_cap, edge_count = edge_src.shape
    feature_width = queries.shape[1]
    head_count = bias_rows.shape[1] // edge_count
    head_size = feature_width // head_count
    picked_rows = key_value[edge_src]
    key_rows = picked_rows[:, :, :feature_width].reshape(
        node_cap, edge_count, head_count, head_size
    )
    value_rows = picked_rows[:, :, feature_width:].reshape(
        node_cap, edge_count, head_count, head_size
    )
    query_heads = queries.reshape(node_cap, head_count, head_size)
    scores = jnp.einsum(
        "nhd,nehd->nhe", query_heads, key_rows, preferred_element_type=jnp.float32
    ) / math.sqrt(head_size)
    scores = scores + bias_rows.reshape(node_cap, head_count, edge_count)
    shifted = jnp.exp(scores - jnp.max(scores, axis=-1, keepdims=True))
    attn_probs = shifted / jnp.sum(shifted, axis=-1, keepdims=True)
    rounded = attn_probs.astype(jnp.bfloat16)
    attended = jnp.einsum("nhe,nehd->nhd", rounded, value_rows, preferred_element_type=jnp.float32)
    kept_values = (query_heads, key_rows, value_rows, attn_probs, rounded)
    return (attended.reshape(node_cap, feature_width).astype(jnp.bfloat16), kept_values)


def attend_backward(grad_mixed, kept_values, edge_src, table_rows):
    query_heads, key_rows, value_rows, attn_probs, rounded = kept_values
    node_cap, head_count, head_size = query_heads.shape
    edge_count = edge_src.shape[1]
    feature_width = head_count * head_size
    grad_heads = grad_mixed.reshape(node_cap, head_count, head_size)
    grad_probs = jnp.einsum(
        "nhd,nehd->nhe", grad_heads, value_rows, preferred_element_type=jnp.float32
    )
    grad_scores = (
        attn_probs * (grad_probs - jnp.sum(attn_probs * grad_probs, axis=-1, keepdims=True))
    ).astype(jnp.bfloat16)
    inv_root = 1.0 / math.sqrt(head_size)
    grad_query = (
        jnp.einsum("nhe,nehd->nhd", grad_scores, key_rows, preferred_element_type=jnp.float32)
        * inv_root
    )
    grad_query = grad_query.reshape(node_cap, feature_width).astype(jnp.bfloat16)
    grad_keys = (
        jnp.einsum("nhe,nhd->nehd", grad_scores, query_heads, preferred_element_type=jnp.float32)
        * inv_root
    )
    grad_values = jnp.einsum(
        "nhe,nhd->nehd", rounded, grad_heads, preferred_element_type=jnp.float32
    )
    grad_edges = jnp.concatenate(
        [
            grad_keys.reshape(node_cap * edge_count, feature_width),
            grad_values.reshape(node_cap * edge_count, feature_width),
        ],
        axis=1,
    )
    grad_key_value = jax.ops.segment_sum(grad_edges, edge_src.reshape(-1), num_segments=table_rows)
    return (grad_query, grad_key_value.astype(jnp.bfloat16))


def smooth_abs(values):
    return jnp.sqrt(values * values + SMOOTH_SQ) - SMOOTH_ROOT


def smooth_slope(values):
    return values * lax.rsqrt(values * values + SMOOTH_SQ)


def ensemble_score_parts(own_block, every_member_output, target_rows, weight_rows):
    member_score_sum = every_member_output.shape[0]
    fair_scale = 1.0 - (1.0 - ALPHA) / member_score_sum
    pair_scale = fair_scale / (2.0 * member_score_sum * (member_score_sum - 1))
    spread = jnp.zeros_like(own_block)
    slope_sum = jnp.zeros_like(own_block)
    for peer_index in range(member_score_sum):
        member_gap = own_block - every_member_output[peer_index][None]
        spread = spread + smooth_abs(member_gap)
        slope_sum = slope_sum + smooth_slope(member_gap)
    target_gap = own_block - target_rows[None]
    crps_term = smooth_abs(target_gap) / member_score_sum - pair_scale * spread
    grad_rows = (
        smooth_slope(target_gap) / member_score_sum - 2.0 * pair_scale * slope_sum
    ) * weight_rows[None]
    return (jnp.sum(crps_term * weight_rows[None]), grad_rows.astype(jnp.bfloat16))


def rows_dot(left, right):
    return lax.dot_general(
        left, right, (((0,), (0,)), ((), ())), preferred_element_type=jnp.float32
    )


def cols_dot(left, right):
    return lax.dot_general(
        left, right, (((1,), (1,)), ((), ())), preferred_element_type=jnp.float32
    )


def body(
    latent,
    node_gain,
    w_qkv,
    w_out,
    edge_bias,
    edge_source,
    boundary,
    node_count,
    decoder_projection_weight,
    dec_source,
    dec_weight,
    state,
    target,
    area,
    var_weight,
):
    hidden = latent[0]
    node_cap, feature_width = hidden.shape
    border = boundary[0]
    rim_size = border.shape[0] // 2
    table_rows = node_cap + 2 * rim_size
    live_rows = (jnp.arange(node_cap) < node_count[0])[:, None]
    features = layer_norm(hidden, node_gain)
    w_key_value = w_qkv[:, feature_width:]
    queries = jnp.dot(
        features, w_qkv[:, :feature_width], preferred_element_type=jnp.float32
    ).astype(jnp.bfloat16)
    arrived = padded(features[border], (("region", 0),), rim_size)
    node_table = jnp.concatenate([features, arrived[:rim_size], arrived[-rim_size:]], axis=0)
    key_value = jnp.dot(node_table, w_key_value, preferred_element_type=jnp.float32).astype(
        jnp.bfloat16
    )
    attended, kept_values = attend(queries, key_value, edge_bias, edge_source)
    update = hidden.astype(jnp.float32) + jnp.dot(
        attended, w_out, preferred_element_type=jnp.float32
    )
    node_out = jnp.where(live_rows, update, 0.0).astype(jnp.bfloat16)
    arrived_out = padded(node_out[border], (("region", 0),), rim_size)
    grid_table = jnp.concatenate(
        [node_out, arrived_out[:rim_size], arrived_out[-rim_size:]], axis=0
    )
    picked_rows = grid_table[dec_source]
    edge_signal = jnp.sum(dec_weight[:, :, None] * picked_rows.astype(jnp.float32), axis=0).astype(
        jnp.bfloat16
    )
    predicted_fields = state + lax.dot_general(
        decoder_projection_weight,
        edge_signal,
        (((0,), (1,)), ((), ())),
        preferred_element_type=jnp.float32,
    )
    weight_factor = area[None, :] * var_weight[:, None] / var_weight.shape[0]
    total_points = state.shape[1] * lax.axis_size("region")
    every_member_output = lax.all_gather(
        predicted_fields[None].astype(jnp.bfloat16), "member", axis=0, tiled=True
    ).astype(jnp.float32)
    partial_loss_value, gradient_block_local = ensemble_score_parts(
        predicted_fields[None], every_member_output, target, weight_factor
    )
    prediction_gradient = gradient_block_local[0]
    partial_loss_value = partial_loss_value / total_points
    decoder_weight_gradient = lax.dot_general(
        edge_signal,
        prediction_gradient,
        (((0,), (1,)), ((), ())),
        preferred_element_type=jnp.float32,
    )
    grad_message = lax.dot_general(
        prediction_gradient,
        decoder_projection_weight,
        (((0,), (1,)), ((), ())),
        preferred_element_type=jnp.float32,
    )
    spread_rows = (dec_weight[:, :, None] * grad_message[None]).reshape(-1, feature_width)
    grad_table = jax.ops.segment_sum(spread_rows, dec_source.reshape(-1), num_segments=table_rows)
    came_back = padded(
        grad_table[node_cap:].astype(jnp.bfloat16), (("region", 0),), rim_size
    ).astype(jnp.float32)
    returned = jnp.concatenate([came_back[:rim_size], came_back[-rim_size:]], axis=0)
    grad_node = jnp.where(live_rows, grad_table[:node_cap].at[border].add(returned), 0.0)
    grad_node_b = grad_node.astype(jnp.bfloat16)
    grad_out = rows_dot(attended, grad_node_b)
    grad_mixed = cols_dot(grad_node_b, w_out).astype(jnp.bfloat16)
    grad_query, grad_key_value = attend_backward(grad_mixed, kept_values, edge_source, table_rows)
    grad_q = rows_dot(features, grad_query)
    own_grads = jnp.concatenate([grad_query, grad_key_value[:node_cap]], axis=1)
    grad_features = cols_dot(own_grads, w_qkv)
    grad_kv = rows_dot(node_table, grad_key_value)
    grad_rim = cols_dot(grad_key_value[node_cap:], w_key_value)
    came_rim = padded(grad_rim.astype(jnp.bfloat16), (("region", 0),), rim_size).astype(
        grad_rim.dtype
    )
    grad_features = grad_features.at[border].add(
        jnp.concatenate([came_rim[:rim_size], came_rim[-rim_size:]], axis=0)
    )
    grad_qkv = jnp.concatenate([grad_q, grad_kv], axis=1)
    grad_latent = (grad_node + norm_backward(hidden, node_gain, grad_features)).astype(
        jnp.bfloat16
    )[None]
    rows_each = feature_width // lax.axis_size("region")
    total_qkv, total_out, total_dec, loss = lax.psum(
        (grad_qkv, grad_out, decoder_weight_gradient, partial_loss_value), ("region", "member")
    )
    offset_rows = lax.axis_index("region") * rows_each
    share_qkv = lax.dynamic_slice_in_dim(total_qkv, offset_rows, rows_each, 0)
    share_out = lax.dynamic_slice_in_dim(total_out, offset_rows, rows_each, 0)
    share_dec = lax.dynamic_slice_in_dim(total_dec, offset_rows, rows_each, 0)
    return (loss, share_qkv, share_out, share_dec, grad_latent)


def solution(mesh):
    placed = (
        P("member", "region", None),
        P(),
        P(),
        P(),
        P("region", None),
        P("region", None),
        P("region", None),
        P("region"),
        P(),
        P(None, "region"),
        P(None, "region"),
        P(None, "region"),
        P(None, "region"),
        P("region"),
        P(),
    )
    return jax.shard_map(
        body,
        mesh=mesh,
        in_specs=placed,
        out_specs=(
            P(),
            P("region", None),
            P("region", None),
            P("region", None),
            P("member", "region", None),
        ),
        check_vma=False,
    )
```

profile of v0, /device:TPU:0, one launch (start us, length us, event | category | flops | bytes accessed | tf_op | source)
XLA Modules:
  0.0 365.6 jit_solution(3375841454523531865)
XLA Ops:
  9.1 1.2 fusion.37
  12.7 3.0 collective-permute-start
  15.7 3.1 collective-permute-start.1
  19.1 1.3 convolution_convert_fusion.3
  24.7 2.4 copy.43
  27.8 2.0 convolution_convert_fusion
  29.8 9.6 %gather_fusion.1 = bf16[2048,1024]{1,0:T(8,128)(2,1)} fusion(bf16[512,1024]{1,0:T(8,128)(2,1)S(1)} %convolution_convert_fusion, s32[2048]{0:T(1024)S(1)} %broadcast_clamp_fusion.1), kind=kCustom, calls=%fused_computation.1 | custom fusion | bytes 8396800 | tf_op jit(solution)/shard_map/gather | solution.py:55
  39.4 4.5 %fusion.88 = (bf16[256,8,512]{2,1,0:T(8,128)(2,1)}, bf16[256,8,512]{2,1,0:T(8,128)(2,1)}) fusion(bf16[256,8,1024]{2,1,0:T(8,128)(2,1)} %bitcast.181), kind=kLoop, calls=%fused_computation.157 | loop fusion | bytes 8388608 | tf_op jit(solution)/shard_map/slice | solution.py:56
  43.9 3.0 copy.76
  46.9 1.5 multiply_reduce_fusion.3
  48.4 1.8 convert_convert_fusion
  50.2 4.4 %copy.77 = bf16[256,8,512]{0,2,1:T(8,128)(2,1)} copy(bf16[256,8,512]{2,1,0:T(8,128)(2,1)} %get-tuple-element.11) | data formatting | bytes 4194304
  54.6 2.1 multiply_reduce_fusion.2
  58.4 1.3 gather_fusion.2
  59.8 4.7 %collective-permute-start.3 = (bf16[128,512]{1,0:T(8,128)(2,1)S(1)}, bf16[128,512]{1,0:T(8,128)(2,1)S(1)}, u32[]{:S(2)}, u32[]{:S(2)}) collective-permute-start(bf16[128,512]{1,0:T(8,128)(2,1)S(1)} %get-tuple-element.23), channel_id=1, source_target_pairs={{4,0},{8,4},{12,8},{16,12},{20,16},{24,20},{28,24},{0,28},{5,1},{9... | collective-permute-start | bytes 393224 | tf_op jit(solution)/shard_map/ppermute | solution.py:23
  64.5 1.4 copy.46
  65.9 1.7 collective-permute-done.2
  67.7 13.3 %gather_fusion.3 = bf16[3072,512]{1,0:T(8,128)(2,1)} fusion(bf16[512,512]{1,0:T(8,128)(2,1)S(1)} %pad_maximum_fusion.2, s32[3072]{0:T(1024)S(1)} %broadcast_clamp_fusion), kind=kCustom, calls=%fused_computation.3 | custom fusion | bytes 6303744 | tf_op jit(solution)/shard_map/gather | solution.py:191
  81.0 2.5 fusion.7
  84.1 9.2 %all-gather.1 = bf16[4,98,1024]{2,1,0:T(8,128)(2,1)S(1)} all-gather(bf16[1,98,1024]{2,1,0:T(8,128)(2,1)S(1)} %convert_bitcast_fusion.1), channel_id=2, replica_groups=mesh['region'=8,'member'=4] {'member'}, dimensions={0}, use_global_device_ids=true | all-gather | bytes 1003520 | tf_op jit(solution)/shard_map/all_gather | solution.py:203
  93.5 1.8 fusion.65
  95.8 3.1 bitcast_multiply_fusion
  98.9 19.5 %scatter_custom_fusion = f32[512,512]{1,0:T(8,128)S(1)} fusion(s32[3072]{0:T(1024)} %reshape.215, f32[3072,512]{1,0:T(8,128)} %bitcast_multiply_fusion, f32[]{:T(128)} %constant.17.clone.1), kind=kCustom, calls=%fused_computation.79 | custom fusion | flops 1572864 | bytes 1049088 | tf_op jit(solution)/shard_map/scatter-add | solution.py:224
  118.7 4.6 %collective-permute-start.5 = (bf16[128,512]{1,0:T(8,128)(2,1)S(1)}, bf16[128,512]{1,0:T(8,128)(2,1)S(1)}, u32[]{:S(2)}, u32[]{:S(2)}) collective-permute-start(bf16[128,512]{1,0:T(8,128)(2,1)S(1)} %get-tuple-element.19), channel_id=1, source_target_pairs={{4,0},{8,4},{12,8},{16,12},{20,16},{24,20},{28,24},{0,28},{5,1},{9... | collective-permute-start | bytes 393224 | tf_op jit(solution)/shard_map/ppermute | solution.py:23
  123.3 1.2 fusion.52
  124.6 2.7 collective-permute-done.4
  127.3 2.7 scatter_custom_fusion.1
  130.4 2.4 fusion.87
  133.0 2.6 multiply_reduce_fusion.1
  136.7 1.4 copy.44
  138.1 2.5 copy.45
  141.2 1.4 fusion.69
  142.7 6.5 %multiply_bitcast_fusion = f32[256,8,16,32]{3,2,1,0:T(8,128)} fusion(f32[256,16,8]{1,2,0:T(8,128)S(1)} %copy-done.11, f32[256,16,32]{2,1,0:T(8,128)S(1)} %copy-done.6), kind=kLoop, calls=%fused_computation.11 | loop fusion | flops 1048576 | bytes 4849664 | tf_op jit(solution)/shard_map/nhe,nhd->nehd/transpose | solution.py:97
  149.2 13.1 %reshape.180 = f32[2048,512]{1,0:T(8,128)} reshape(f32[256,8,16,32]{3,2,1,0:T(8,128)} %multiply_bitcast_fusion) | data formatting | bytes 8388608 | tf_op jit(solution)/shard_map/reshape | solution.py:103
  162.3 7.9 %multiply_bitcast_fusion.1 = f32[256,8,16,32]{3,2,1,0:T(8,128)} fusion(f32[256,16,8]{1,2,0:T(8,128)} %copy.44, f32[256,16,32]{2,1,0:T(8,128)S(1)} %copy-done.5), kind=kLoop, calls=%fused_computation.12 | loop fusion | flops 2097152 | bytes 4849664 | tf_op jit(solution)/shard_map/mul | solution.py:94
  170.2 13.0 %reshape.179 = f32[2048,512]{1,0:T(8,128)} reshape(f32[256,8,16,32]{3,2,1,0:T(8,128)} %multiply_bitcast_fusion.1) | data formatting | bytes 8388608 | tf_op jit(solution)/shard_map/reshape | solution.py:102
  183.1 18.9 %scatter_custom_fusion.2 = f32[512,1024]{1,0:T(8,128)S(1)} fusion(s32[2048]{0:T(1024)} %reshape.231, f32[2048,512]{1,0:T(8,128)} %reshape.180, f32[]{:T(128)} %constant.24.clone.1, f32[2048,512]{1,0:T(8,128)} %reshape.179, f32[]{:T(128)} %constant.17.clone.1), kind=kCustom, calls=%fused_computation.13 | custom fusion | flops 4194304 | bytes 10486784 | tf_op jit(solution)/shard_map/scatter-add | solution.py:107
  204.0 1.9 pad_maximum_fusion
  206.8 39.7 %psum.28 = f32[]{:T(128)} all-reduce(f32[]{:T(128)S(6)} %div.57), channel_id=1, replica_groups=mesh['region'=8,'member'=4] {'region','member'}, use_global_device_ids=true, to_apply=%region_6.7 | all-reduce | flops 1 | bytes 8 | tf_op jit(solution)/shard_map/psum | solution.py:250
  246.7 1.8 convolution_convert_fusion.1
  248.5 2.5 collective-permute-start.6
  251.0 2.3 collective-permute-start.7
  253.9 3.1 collective-permute-done.6
  258.0 2.5 scatter_custom_fusion.3
  261.8 92.3 %all-reduce.3.cloned.1.call-done = (f32[512,1536]{1,0:T(8,128)}, f32[512,512]{1,0:T(8,128)}, f32[512,98]{1,0:T(8,128)}) async-done(((f32[512,1536]{1,0:T(8,128)}, f32[512,512]{1,0:T(8,128)}, f32[512,98]{1,0:T(8,128)}), (f32[512,1536]{1,0:T(8,128)}, f32[512,512]{1,0:T(8,128)}, f32[512,98]{1,0:T(8,128)})) %all-reduce.3.cloned.1.call-update) | async-done | bytes 4395024 | tf_op jit(solution)/shard_map/psum | solution.py:250
  354.1 1.8 constant_dynamic-slice_fusion.2
  355.8 1.4 constant_dynamic-slice_fusion
  357.2 1.6 constant_dynamic-slice_fusion.1
  (137 shorter events, 19.3 us)
Async XLA Ops:
  7.2 50.2 %copy-start = (bf16[512,512]{1,0:T(8,128)(2,1)S(1)}, bf16[512,512]{1,0:T(8,128)(2,1)}, u32[]{:S(2)}) copy-start(bf16[512,512]{1,0:T(8,128)(2,1)} %param.18) | copy-start | bytes 1572868
  7.2 11.6 %copy-start.28 = (s32[256,8]{0,1:T(8,128)S(1)}, s32[256,8]{0,1:T(8,128)}, u32[]{:S(2)}) copy-start(s32[256,8]{0,1:T(8,128)} %param.20) | copy-start | bytes 24580
  7.2 11.6 %copy-start.22 = (s32[3,1024]{1,0:T(4,128)S(1)}, s32[3,1024]{1,0:T(4,128)}, u32[]{:S(2)}) copy-start(s32[3,1024]{1,0:T(4,128)} %param.24) | copy-start | bytes 36868
  7.2 346.8 %all-reduce.3.cloned.1.call-start = ((), (), s32[]{:S(2)}) async-start(), calls=%async_computation | async-start | bytes 8912896 | tf_op jit(solution)/shard_map/psum | solution.py:250
  8.0 10.8 %copy-start.34 = (s32[256,1]{0,1:T(1,128)}, s32[256,1]{0,1:T(1,128)S(1)}, u32[]{:S(2)}) copy-start(s32[256,1]{0,1:T(1,128)S(1)} %compare_select_fusion.2) | copy-start | bytes 3076
  9.1 2.4 copy-start.25
  10.2 8.6 %copy-start.29 = (f32[256]{0:T(256)}, f32[256]{0:T(256)S(1)}, u32[]{:S(2)}) copy-start(f32[256]{0:T(256)S(1)} %add_rsqrt_fusion) | copy-start | bytes 3076
  10.3 8.5 %copy-start.31 = (s32[1024]{0:T(1024)}, s32[1024]{0:T(1024)S(1)}, u32[]{:S(2)}) copy-start(s32[1024]{0:T(1024)S(1)} %pad_clamp_fusion) | copy-start | bytes 12292
  10.3 11.8 %copy-start.21 = (f32[3,1024]{1,0:T(4,128)S(1)}, f32[3,1024]{1,0:T(4,128)}, u32[]{:S(2)}) copy-start(f32[3,1024]{1,0:T(4,128)} %param.25) | copy-start | bytes 36868
  10.3 13.0 %copy-start.20 = (f32[256,128]{1,0:T(8,128)S(1)}, f32[256,128]{1,0:T(8,128)}, u32[]{:S(2)}) copy-start(f32[256,128]{1,0:T(8,128)} %param.19) | copy-start | bytes 393220
  12.7 15.1 %collective-permute-start = (bf16[128,512]{1,0:T(8,128)(2,1)S(1)}, bf16[128,512]{1,0:T(8,128)(2,1)S(1)}, u32[]{:S(2)}, u32[]{:S(2)}) collective-permute-start(bf16[128,512]{1,0:T(8,128)(2,1)S(1)} %get-tuple-element.24), channel_id=1, source_target_pairs={{0,4},{4,8},{8,12},{12,16},{16,20},{20,24},{24,28},{28,0},{1,5},{5... | collective-permute-start | bytes 393224 | tf_op jit(solution)/shard_map/ppermute | solution.py:21
  15.7 12.1 %collective-permute-start.1 = (bf16[128,512]{1,0:T(8,128)(2,1)S(1)}, bf16[128,512]{1,0:T(8,128)(2,1)S(1)}, u32[]{:S(2)}, u32[]{:S(2)}) collective-permute-start(bf16[128,512]{1,0:T(8,128)(2,1)S(1)} %get-tuple-element.25), channel_id=1, source_target_pairs={{4,0},{8,4},{12,8},{16,12},{20,16},{24,20},{28,24},{0,28},{5,1},{9... | collective-permute-start | bytes 393224 | tf_op jit(solution)/shard_map/ppermute | solution.py:23
  27.8 11.6 %copy-start.17 = (bf16[128,512]{1,0:T(8,128)(2,1)}, bf16[128,512]{1,0:T(8,128)(2,1)S(1)}, u32[]{:S(2)}) copy-start(bf16[128,512]{1,0:T(8,128)(2,1)S(1)} %collective-permute-done.1) | copy-start | bytes 393220
  46.9 7.7 %copy-start.2 = (bf16[256,8,512]{0,2,1:T(8,128)(2,1)}, bf16[256,8,512]{0,2,1:T(8,128)(2,1)S(1)}, u32[]{:S(2)}) copy-start(bf16[256,8,512]{0,2,1:T(8,128)(2,1)S(1)} %copy.76) | copy-start | bytes 6291460
  50.2 7.2 %copy-start.4 = (bf16[1,256,512]{2,1,0:T(8,128)(2,1)S(1)}, bf16[1,256,512]{2,1,0:T(8,128)(2,1)}, u32[]{:S(2)}) copy-start(bf16[1,256,512]{2,1,0:T(8,128)(2,1)} %param.15) | copy-start | bytes 786436
  54.6 9.9 %copy-start.24 = (s32[3072]{0:T(1024)S(1)}, s32[3072]{0:T(1024)}, u32[]{:S(2)}) copy-start(s32[3072]{0:T(1024)} %reshape.207) | copy-start | bytes 36868
  56.7 0.7 copy-start.13
  59.7 7.8 %collective-permute-start.2 = (bf16[128,512]{1,0:T(8,128)(2,1)S(1)}, bf16[128,512]{1,0:T(8,128)(2,1)S(1)}, u32[]{:S(2)}, u32[]{:S(2)}) collective-permute-start(bf16[128,512]{1,0:T(8,128)(2,1)S(1)} %get-tuple-element.22), channel_id=1, source_target_pairs={{0,4},{4,8},{8,12},{12,16},{16,20},{20,24},{24,28},{28,0},{1,5},{5... | collective-permute-start | bytes 393224 | tf_op jit(solution)/shard_map/ppermute | solution.py:21
  59.8 7.8 %collective-permute-start.3 = (bf16[128,512]{1,0:T(8,128)(2,1)S(1)}, bf16[128,512]{1,0:T(8,128)(2,1)S(1)}, u32[]{:S(2)}, u32[]{:S(2)}) collective-permute-start(bf16[128,512]{1,0:T(8,128)(2,1)S(1)} %get-tuple-element.23), channel_id=1, source_target_pairs={{4,0},{8,4},{12,8},{16,12},{20,16},{24,20},{28,24},{0,28},{5,1},{9... | collective-permute-start | bytes 393224 | tf_op jit(solution)/shard_map/ppermute | solution.py:23
  81.0 2.5 copy-start.15
  81.0 2.6 copy-start.16
  83.5 10.0 %copy-start.14 = (f32[98,1024]{1,0:T(8,128)S(1)}, f32[98,1024]{1,0:T(8,128)}, u32[]{:S(2)}) copy-start(f32[98,1024]{1,0:T(8,128)} %param.27) | copy-start | bytes 1204228
  83.5 10.0 %copy-start.33 = (f32[1024]{0:T(1024)S(1)}, f32[1024]{0:T(1024)}, u32[]{:S(2)}) copy-start(f32[1024]{0:T(1024)} %param.28) | copy-start | bytes 12292
  83.5 9.9 %copy-start.35 = (f32[98]{0:T(128)S(1)}, f32[98]{0:T(128)}, u32[]{:S(2)}) copy-start(f32[98]{0:T(128)} %param.29) | copy-start | bytes 1180
  93.5 2.3 copy-start.23
  118.5 11.5 %copy-start.32 = (pred[256]{0:T(512)(128)(4,1)S(1)}, pred[256]{0:T(512)(128)(4,1)}, u32[]{:S(2)}) copy-start(pred[256]{0:T(512)(128)(4,1)} %iota_compare_fusion) | copy-start | bytes 772
  118.5 8.7 %collective-permute-start.4 = (bf16[128,512]{1,0:T(8,128)(2,1)S(1)}, bf16[128,512]{1,0:T(8,128)(2,1)S(1)}, u32[]{:S(2)}, u32[]{:S(2)}) collective-permute-start(bf16[128,512]{1,0:T(8,128)(2,1)S(1)} %get-tuple-element.18), channel_id=1, source_target_pairs={{0,4},{4,8},{8,12},{12,16},{16,20},{20,24},{24,28},{28,0},{1,5},{5... | collective-permute-start | bytes 393224 | tf_op jit(solution)/shard_map/ppermute | solution.py:21
  118.7 8.5 %collective-permute-start.5 = (bf16[128,512]{1,0:T(8,128)(2,1)S(1)}, bf16[128,512]{1,0:T(8,128)(2,1)S(1)}, u32[]{:S(2)}, u32[]{:S(2)}) collective-permute-start(bf16[128,512]{1,0:T(8,128)(2,1)S(1)} %get-tuple-element.19), channel_id=1, source_target_pairs={{4,0},{8,4},{12,8},{16,12},{20,16},{24,20},{28,24},{0,28},{5,1},{9... | collective-permute-start | bytes 393224 | tf_op jit(solution)/shard_map/ppermute | solution.py:23
  130.0 2.9 copy-start.7
  130.4 5.2 %copy-start.19 = (f32[256,16,8]{0,2,1:T(8,128)S(1)}, f32[256,16,8]{0,2,1:T(8,128)}, u32[]{:S(2)}) copy-start(f32[256,16,8]{0,2,1:T(8,128)} %get-tuple-element.27) | copy-start | bytes 393220
  133.0 7.6 %copy-start.3 = (bf16[256,8,512]{0,2,1:T(8,128)(2,1)S(1)}, bf16[256,8,512]{0,2,1:T(8,128)(2,1)}, u32[]{:S(2)}) copy-start(bf16[256,8,512]{0,2,1:T(8,128)(2,1)} %copy-done.2) | copy-start | bytes 6291460
  138.1 3.1 copy-start.26
  138.1 3.1 copy-start.27
  138.1 3.1 copy-start.30
  140.6 2.1 copy-start.6
  140.6 2.1 copy-start.11
  149.2 13.1 %copy-start.5 = (f32[256,16,32]{2,1,0:T(8,128)S(1)}, f32[256,16,32]{2,1,0:T(8,128)}, u32[]{:S(2)}) copy-start(f32[256,16,32]{2,1,0:T(8,128)} %copy.43) | copy-start | bytes 1572868
  202.1 1.2 copy-start.18
  202.1 1.9 copy-start.12
  202.2 1.0 copy-start.9
  206.0 40.7 %copy-start.10 = (bf16[512,1024]{1,0:T(8,128)(2,1)S(1)}, bf16[512,1024]{1,0:T(8,128)(2,1)}, u32[]{:S(2)}) copy-start(bf16[512,1024]{1,0:T(8,128)(2,1)} %copy-done.9) | copy-start | bytes 3145732
  206.0 47.3 %slice-start = ((bf16[512,1024]{1,0:T(8,128)(2,1)}), bf16[256,1024]{1,0:T(8,128)(2,1)S(1)}, s32[]{:S(2)}) async-start(bf16[512,1024]{1,0:T(8,128)(2,1)} %copy-done.9), calls=%async_computation.1 | async-start | bytes 1048576 | tf_op jit(solution)/shard_map/slice | solution.py:235
  246.6 6.7 %copy-start.36 = (bf16[512,1536]{1,0:T(8,128)(2,1)S(1)}, bf16[512,1536]{1,0:T(8,128)(2,1)}, u32[]{:S(2)}) copy-start(bf16[512,1536]{1,0:T(8,128)(2,1)} %param.17) | copy-start | bytes 4718596
  248.5 8.5 %collective-permute-start.6 = (bf16[128,512]{1,0:T(8,128)(2,1)S(1)}, bf16[128,512]{1,0:T(8,128)(2,1)S(1)}, u32[]{:S(2)}, u32[]{:S(2)}) collective-permute-start(bf16[128,512]{1,0:T(8,128)(2,1)S(1)} %get-tuple-element.20), channel_id=1, source_target_pairs={{0,4},{4,8},{8,12},{12,16},{16,20},{20,24},{24,28},{28,0},{1,5},{5... | collective-permute-start | bytes 393224 | tf_op jit(solution)/shard_map/ppermute | solution.py:21
  251.0 9.8 %copy-start.8 = (f32[256,512]{1,0:T(8,128)S(1)}, f32[256,512]{1,0:T(8,128)}, u32[]{:S(2)}) copy-start(f32[256,512]{1,0:T(8,128)} %copy-done.7) | copy-start | bytes 1572868
  251.0 7.0 %collective-permute-start.7 = (bf16[128,512]{1,0:T(8,128)(2,1)S(1)}, bf16[128,512]{1,0:T(8,128)(2,1)S(1)}, u32[]{:S(2)}, u32[]{:S(2)}) collective-permute-start(bf16[128,512]{1,0:T(8,128)(2,1)S(1)} %get-tuple-element.21), channel_id=1, source_target_pairs={{4,0},{8,4},{12,8},{16,12},{20,16},{24,20},{28,24},{0,28},{5,1},{9... | collective-permute-start | bytes 393224 | tf_op jit(solution)/shard_map/ppermute | solution.py:23
  253.3 105.5 %copy-start.1 = (bf16[512,512]{1,0:T(8,128)(2,1)S(1)}, bf16[512,512]{1,0:T(8,128)(2,1)}, u32[]{:S(2)}) copy-start(bf16[512,512]{1,0:T(8,128)(2,1)} %param.18) | copy-start | bytes 1572868
Sparse Core Ops, SparseCore 0:
  206.1 147.8 all-reduce.2
where the time goes:
time: 367 us; the launch traced here: 366 us
  waiting for transfers between devices  101 us (28%)
  other arithmetic  83.6 us (23%)
  local copies, waits for them, and re-layouts  81.8 us (22%)
  blocking collectives  49 us (13%)
  starting transfers between devices  20.5 us (6%)
  between operations  16.2 us (4%)
  matrix products  13.8 us (4%)
    psum x1, waiting for transfers between devices, body(): lax.psum((grad_qkv, grad_out, decoder_weight_gradient, partial_loss_value...  92.3 us
    psum x1, blocking collectives, body(): lax.psum((grad_qkv, grad_out, decoder_weight_gradient, partial_loss_value...  39.7 us
    scatter-add x1, other arithmetic, body(): jax.ops.segment_sum(spread_rows, dec_source.reshape(-1), num_segments=tab...  19.5 us
    scatter-add x1, other arithmetic, attend_backward(): jax.ops.segment_sum(grad_edges, edge_src.reshape(-1), num_segments=table_...  18.9 us
    ppermute x4, starting transfers between devices, padded(): lax.ppermute(head, axis, [((i + 1) % count, i) for i in range(count)])  14.7 us
    gather x1, local copies, waits for them, and re-layouts, body(): picked_rows = grid_table[dec_source]  13.3 us
    reshape x1, local copies, waits for them, and re-layouts, attend_backward(): grad_values.reshape(node_cap * edge_count, feature_width)  13.1 us
    reshape x1, local copies, waits for them, and re-layouts, attend_backward(): grad_keys.reshape(node_cap * edge_count, feature_width)  13 us
  transfers between devices with their start and end apart: 9, of which 6 were waited for; matrix products, arithmetic and copies ran while one was open for 5% of the time, Pallas kernels for 0%

commit v1 on v0

v1 whole, which is shorter than its diff:
```python
import functools
import math

import jax
import jax.numpy as jnp
from jax import lax
from jax.experimental import pallas as pl
from jax.experimental.pallas import tpu as pltpu
from jax.sharding import PartitionSpec as P

ALPHA = 0.95
NORM_EPS = 1e-05
SMOOTH_SQ = 0.25
SMOOTH_ROOT = 0.5
F32 = jnp.float32
BF16 = jnp.bfloat16
LANES = 128


def nn(left, right):
    return lax.dot_general(left, right, (((1,), (0,)), ((), ())), preferred_element_type=F32)


def nt(left, right):
    return lax.dot_general(left, right, (((1,), (1,)), ((), ())), preferred_element_type=F32)


def tn(left, right):
    return lax.dot_general(left, right, (((0,), (0,)), ((), ())), preferred_element_type=F32)


def on_core(name, kernel, outs, *args, scalars=(), scratch=()):
    return pl.pallas_call(
        kernel,
        name=name,
        out_shape=[jax.ShapeDtypeStruct(s, d) for s, d in outs],
        in_specs=[pl.BlockSpec(memory_space=pltpu.SMEM)] * len(scalars)
        + [pl.BlockSpec(memory_space=pltpu.VMEM)] * len(args),
        out_specs=[pl.BlockSpec(memory_space=pltpu.VMEM)] * len(outs),
        scratch_shapes=list(scratch),
        compiler_params=pltpu.CompilerParams(vmem_limit_bytes=48 * 1024 * 1024),
    )(*scalars, *args)


def iota(shape, dim):
    return lax.broadcasted_iota(jnp.int32, shape, dim)


def ones_where(mask):
    return jnp.where(mask, 1.0, 0.0).astype(BF16)


def shift_of(size):
    assert size & (size - 1) == 0
    return size.bit_length() - 1


def head_map(rows, cols, row_size, col_size):
    return ones_where(
        (iota((rows, cols), 0) >> shift_of(row_size)) == (iota((rows, cols), 1) >> shift_of(col_size))
    )


def group_reduce(values, size, op):
    lanes = values.shape[1]
    lane = iota(values.shape, 1)
    step = 1
    while step < size:
        partner = jnp.where(
            (lane & step) == 0,
            pltpu.roll(values, lanes - step, 1),
            pltpu.roll(values, step, 1),
        )
        values = op(values, partner)
        step *= 2
    return values


def norm_parts(hidden):
    values = hidden.astype(F32)
    center = values - jnp.mean(values, axis=-1, keepdims=True)
    inverse = lax.rsqrt(jnp.mean(center * center, axis=-1, keepdims=True) + NORM_EPS)
    return center * inverse, inverse


def picked(border_row, table):
    mask = ones_where(iota((table.shape[0], border_row.shape[1]), 0) == border_row)
    return tn(mask, table)


def norm_kernel(hidden_ref, gain_ref, border_ref, features_ref, head_ref, tail_ref):
    scaled, _ = norm_parts(hidden_ref[...])
    features = (scaled * gain_ref[...]).astype(BF16)
    features_ref[...] = features
    rows = picked(border_ref[...], features).astype(BF16)
    rim = head_ref.shape[0]
    head_ref[...] = rows[:rim]
    tail_ref[...] = rows[rim:]


def project_kernel(features_ref, w_ref, src_ref, weight_ref, q_ref, kv_ref, mix_ref):
    width = features_ref.shape[1]
    qkv = nn(features_ref[...], w_ref[...]).astype(BF16)
    q_ref[...] = qkv[:, :width]
    kv_ref[...] = qkv[:, width:]
    rows = iota(mix_ref.shape, 0)
    total = jnp.zeros(mix_ref.shape, F32)
    for j in range(src_ref.shape[0]):
        total += jnp.where(rows == src_ref[j : j + 1, :], weight_ref[j : j + 1, :], 0.0)
    mix_ref[...] = total.astype(BF16)


def attend_kernel(
    count_ref, hidden_ref, left_ref, right_ref, q_ref, kv_ref, w_ref, w_out_ref, bias_ref, src_ref,
    border_ref, out_ref, head_ref, tail_ref, probs_ref, attended_ref, keys_ref, values_ref, table_ref,
):
    nodes, width = hidden_ref.shape
    rim = left_ref.shape[0]
    edges = src_ref.shape[1]
    columns = bias_ref.shape[1]
    head_size = width // (columns // edges)
    w_kv = w_ref[:, width:]
    table_ref[:nodes] = kv_ref[...]
    table_ref[nodes : nodes + rim] = nn(left_ref[...], w_kv).astype(BF16)
    table_ref[nodes + rim :] = nn(right_ref[...], w_kv).astype(BF16)
    table = table_ref[...]
    queries = q_ref[...].astype(F32)
    squeeze = head_map(width, columns, head_size, edges)
    expand = head_map(columns, width, edges, head_size)
    lane = iota((nodes, columns), 1) & (edges - 1)
    slot = iota((nodes, table.shape[0]), 1)
    scores = jnp.zeros((nodes, columns), F32)
    for e in range(edges):
        rows = nn(ones_where(slot == src_ref[:, e : e + 1]), table)
        keys_ref[e] = rows[:, :width].astype(BF16)
        values_ref[e] = rows[:, width:].astype(BF16)
        part = nn((queries * rows[:, :width]).astype(BF16), squeeze)
        scores = jnp.where(lane == e, part, scores)
    scores = scores / math.sqrt(head_size) + bias_ref[...]
    shifted = jnp.exp(scores - group_reduce(scores, edges, jnp.maximum))
    probs = shifted / group_reduce(shifted, edges, jnp.add)
    probs_ref[...] = probs
    total = jnp.zeros((nodes, width), F32)
    for e in range(edges):
        share = nn(jnp.where(lane == e, probs, 0.0).astype(BF16), expand)
        total += share * values_ref[e].astype(F32)
    attended = total.astype(BF16)
    attended_ref[...] = attended
    update = hidden_ref[...].astype(F32) + nn(attended, w_out_ref[...])
    live = iota((nodes, width), 0) < count_ref[0]
    node_out = jnp.where(live, update, 0.0).astype(BF16)
    out_ref[...] = node_out
    rows = picked(border_ref[...], node_out).astype(BF16)
    head_ref[...] = rows[:rim]
    tail_ref[...] = rows[rim:]


def decode_kernel(
    own_ref, left_ref, right_ref, mix_ref, w_ref, message_ref, change_ref, sent_ref, table_ref
):
    nodes = own_ref.shape[0]
    rim = left_ref.shape[0]
    table_ref[:nodes] = own_ref[...]
    table_ref[nodes : nodes + rim] = left_ref[...]
    table_ref[nodes + rim :] = right_ref[...]
    message = tn(table_ref[...], mix_ref[...]).astype(BF16)
    message_ref[...] = message
    change = tn(w_ref[...], message)
    change_ref[...] = change
    sent_ref[...] = change.astype(BF16)


def smooth_root(values):
    return values * values + SMOOTH_SQ


def score_kernel(
    change_ref, every_ref, state_ref, target_ref, area_ref, var_ref, mix_ref, w_ref, rank_ref,
    grad_ref, message_ref, head_ref, tail_ref, loss_ref, *, points,
):
    members = every_ref.shape[0]
    fair = 1.0 - (1.0 - ALPHA) / members
    pair = fair / (2.0 * members * (members - 1))
    own = change_ref[...]
    variables = own.shape[0]
    spread = jnp.zeros_like(own)
    slope = jnp.zeros_like(own)
    me = rank_ref[0]
    for n in range(members):
        other = jnp.where(me == n, own, every_ref[n].astype(F32))
        gap = own - other
        square = smooth_root(gap)
        inverse = lax.rsqrt(square)
        spread += square * inverse - SMOOTH_ROOT
        slope += gap * inverse
    gap = state_ref[...] + own - target_ref[...]
    square = smooth_root(gap)
    inverse = lax.rsqrt(square)
    weight = area_ref[...] * var_ref[...] / variables
    term = (square * inverse - SMOOTH_ROOT) / members - pair * spread
    loss_ref[...] = jnp.full(loss_ref.shape, jnp.sum(term * weight) / points, F32)
    grad = ((gap * inverse / members - 2.0 * pair * slope) * weight).astype(BF16)
    grad_ref[...] = grad
    message = nn(w_ref[...], grad).astype(BF16)
    message_ref[...] = message
    rim = head_ref.shape[0]
    nodes = mix_ref.shape[0] - 2 * rim
    rows = nt(mix_ref[nodes:, :], message).astype(BF16)
    head_ref[...] = rows[:rim]
    tail_ref[...] = rows[rim:]


def score_call(rank, *args, outs, points):
    kernel = functools.partial(score_kernel, points=points)

    def ordered(rank_ref, change, every, state, target, area, var, mix, w, *out_refs):
        kernel(change, every, state, target, area, var, mix, w, rank_ref, *out_refs)

    return on_core("score", ordered, outs, *args, scalars=(rank,))


def own_rows_kernel(mix_ref, grad_message_ref, message_ref, grad_ref, own_ref, dec_ref):
    nodes = own_ref.shape[0]
    own_ref[...] = nt(mix_ref[:nodes, :], grad_message_ref[...])
    dec_ref[...] = nt(message_ref[...], grad_ref[...])


def node_grad_kernel(
    count_ref, own_ref, from_left_ref, from_right_ref, border_ref, attended_ref, w_out_ref,
    grad_ref, mixed_ref, out_ref, rows_ref,
):
    nodes, width = own_ref.shape
    rim = from_left_ref.shape[0]
    rows_ref[:rim] = from_left_ref[...]
    rows_ref[rim:] = from_right_ref[...]
    mask = ones_where(iota((nodes, 2 * rim), 0) == border_ref[...])
    total = own_ref[...] + nn(mask, rows_ref[...])
    total = jnp.where(iota((nodes, width), 0) < count_ref[0], total, 0.0)
    grad_ref[...] = total
    rounded = total.astype(BF16)
    mixed_ref[...] = nt(rounded, w_out_ref[...]).astype(BF16)
    out_ref[...] = tn(attended_ref[...], rounded)


def attend_back_kernel(
    mixed_ref, q_ref, probs_ref, keys_ref, values_ref, src_ref, w_ref,
    grad_query_ref, grad_kv_ref, head_ref, tail_ref, edge_ref, hot_ref,
):
    nodes, width = mixed_ref.shape
    edges = src_ref.shape[0]
    columns = probs_ref.shape[1]
    head_size = width // (columns // edges)
    inv_root = 1.0 / math.sqrt(head_size)
    squeeze = head_map(width, columns, head_size, edges)
    expand = head_map(columns, width, edges, head_size)
    lane = iota((nodes, columns), 1) & (edges - 1)
    mixed = mixed_ref[...].astype(F32)
    probs = probs_ref[...]
    grad_probs = jnp.zeros((nodes, columns), F32)
    for e in range(edges):
        part = nn((mixed * values_ref[e].astype(F32)).astype(BF16), squeeze)
        grad_probs = jnp.where(lane == e, part, grad_probs)
    grad_scores = probs * (grad_probs - group_reduce(probs * grad_probs, edges, jnp.add))
    query = q_ref[...].astype(F32) * inv_root
    total = jnp.zeros((nodes, width), F32)
    table_rows = hot_ref.shape[0]
    slot = iota((table_rows, nodes), 0)
    for e in range(edges):
        at = pl.ds(e * nodes, nodes)
        hot_ref[:, at] = ones_where(slot == src_ref[e : e + 1, :])
        share = nn(jnp.where(lane == e, grad_scores, 0.0).astype(BF16), expand)
        total += share * keys_ref[e].astype(F32)
        edge_ref[at, :width] = (share * query).astype(BF16)
        share = nn(jnp.where(lane == e, probs, 0.0).astype(BF16), expand)
        edge_ref[at, width:] = (share * mixed).astype(BF16)
    grad_query_ref[...] = (total * inv_root).astype(BF16)
    grad_kv = nn(hot_ref[...], edge_ref[...]).astype(BF16)
    grad_kv_ref[...] = grad_kv
    rim = head_ref.shape[0]
    rows = nt(grad_kv[nodes:], w_ref[:, width:]).astype(BF16)
    head_ref[...] = rows[:rim]
    tail_ref[...] = rows[rim:]


def split_rows(bits_ref, which, source, send_ref, keep_ref):
    mine = bits_ref[which]
    for i in range(send_ref.shape[0]):
        send_ref[i] = source[i, 1 - mine].astype(BF16)
        keep_ref[i] = source[i, mine]


def weight_grad_kernel(
    bits_ref, features_ref, left_ref, right_ref, grad_query_ref, grad_kv_ref, out_ref, dec_ref,
    loss_ref, send_ref, keep_ref, full_ref,
):
    nodes, width = features_ref.shape
    rim = left_ref.shape[0]
    variables = dec_ref.shape[1]
    pairs, _, rows, _ = full_ref.shape
    shape = (pairs, 2, rows)
    features = features_ref[...]

    def put(start, values):
        full_ref[:, :, :, start : start + values.shape[1]] = values.reshape(*shape, values.shape[1])

    put(0, tn(features, grad_query_ref[...]))
    total = tn(features, grad_kv_ref[:nodes, :])
    total += tn(left_ref[...], grad_kv_ref[nodes : nodes + rim, :])
    total += tn(right_ref[...], grad_kv_ref[nodes + rim :, :])
    put(width, total)
    put(3 * width, out_ref[...])
    dec = dec_ref[...]
    pad = jnp.concatenate([dec, jnp.zeros((width, LANES - variables), F32)], axis=1)
    loss = jnp.broadcast_to(loss_ref[0:1, 0:1], (width, LANES))
    high = loss.astype(BF16).astype(F32)
    lane = iota((width, LANES), 1)
    pad = jnp.where(lane == variables, high, pad)
    pad = jnp.where(lane == variables + 1, loss - high, pad)
    put(4 * width, pad)
    split_rows(bits_ref, 0, full_ref, send_ref, keep_ref)


def joined(keep, arrived, variables):
    total = keep + arrived.astype(F32)
    last = total[..., -LANES:]
    lane = iota(last.shape, last.ndim - 1)
    loss = last[..., variables : variables + 1] + last[..., variables + 1 : variables + 2]
    high = loss.astype(BF16).astype(F32)
    last = jnp.where(lane == variables, high, last)
    last = jnp.where(lane == variables + 1, loss - high, last)
    return total[..., :-LANES], last


def combine_kernel(bits_ref, keep_in_ref, arrived_ref, send_ref, keep_ref, *, which, variables):
    mine = bits_ref[which]
    for i in range(send_ref.shape[0]):
        for half in (0, 1):
            at = mine if half else 1 - mine
            body, last = joined(keep_in_ref[i, at], arrived_ref[i, at], variables)
            to = keep_ref if half else send_ref
            to[i, :, :-LANES] = body.astype(to.dtype)
            to[i, :, -LANES:] = last.astype(to.dtype)


def last_kernel(keep_ref, arrived_ref, sum_ref, *, variables):
    body, last = joined(keep_ref[...], arrived_ref[...], variables)
    sum_ref[:, :-LANES] = body.astype(BF16)
    sum_ref[:, -LANES:] = last.astype(BF16)


def unpack_kernel(sums_ref, qkv_ref, out_ref, dec_ref, loss_ref):
    width = out_ref.shape[1]
    variables = dec_ref.shape[1]
    qkv_ref[...] = sums_ref[:, : 3 * width].astype(F32)
    out_ref[...] = sums_ref[:, 3 * width : 4 * width].astype(F32)
    last = sums_ref[:, 4 * width :].astype(F32)
    dec_ref[...] = last[:, :variables]
    loss = last[0:1, variables : variables + 1] + last[0:1, variables + 1 : variables + 2]
    loss_ref[...] = jnp.broadcast_to(loss, loss_ref.shape)


def own_feature_kernel(grad_query_ref, grad_kv_ref, w_ref, grad_ref):
    nodes, width = grad_query_ref.shape
    grad_ref[...] = nt(grad_query_ref[...], w_ref[:, :width]) + nt(
        grad_kv_ref[:nodes, :], w_ref[:, width:]
    )


def latent_grad_kernel(
    hidden_ref, gain_ref, own_ref, from_left_ref, from_right_ref, border_ref, node_ref, grad_ref, rows_ref
):
    nodes = hidden_ref.shape[0]
    rim = from_left_ref.shape[0]
    rows_ref[:rim] = from_left_ref[...]
    rows_ref[rim:] = from_right_ref[...]
    mask = ones_where(iota((nodes, 2 * rim), 0) == border_ref[...])
    grad_rows = own_ref[...] + nn(mask, rows_ref[...])
    scaled, inverse = norm_parts(hidden_ref[...])
    scaled_grad = grad_rows * gain_ref[...]
    back = inverse * (
        scaled_grad
        - jnp.mean(scaled_grad, axis=-1, keepdims=True)
        - scaled * jnp.mean(scaled_grad * scaled, axis=-1, keepdims=True)
    )
    grad_ref[...] = (node_ref[...] + back).astype(BF16)


def swap_rims(head, tail):
    count = lax.axis_size("region")
    from_left = lax.ppermute(tail, "region", [(i, (i + 1) % count) for i in range(count)])
    from_right = lax.ppermute(head, "region", [((i + 1) % count, i) for i in range(count)])
    return from_left, from_right


def exchange_order(regions, members):
    order = [("member", 1 << b) for b in range(shift_of(members))]
    bits = [1 << b for b in range(shift_of(regions))]
    return order + [("region", b) for b in bits[:1] + bits[:0:-1]]


def body(
    latent,
    node_gain,
    w_qkv,
    w_out,
    edge_bias,
    edge_source,
    boundary,
    node_count,
    decoder_projection_weight,
    dec_source,
    dec_weight,
    state,
    target,
    area,
    var_weight,
):
    hidden = latent[0]
    nodes, width = hidden.shape
    rim = boundary.shape[1] // 2
    table_rows = nodes + 2 * rim
    edges = edge_source.shape[1]
    columns = edge_bias.shape[1]
    variables, points = state.shape
    regions, members = lax.axis_size("region"), lax.axis_size("member")
    total_points = points * regions
    gain = node_gain[None]
    rim_rows = ((rim, width), BF16)
    order = exchange_order(regions, members)
    where = {"region": lax.axis_index("region"), "member": lax.axis_index("member")}
    bits = jnp.stack([(where[axis] & bit) // bit for axis, bit in order]).astype(jnp.int32)
    rank = where["member"].astype(jnp.int32)[None]

    features, head, tail = on_core(
        "norm", norm_kernel, [((nodes, width), BF16), rim_rows, rim_rows], hidden, gain, boundary
    )
    left, right = swap_rims(head, tail)
    queries, own_kv, mix = on_core(
        "project",
        project_kernel,
        [((nodes, width), BF16), ((nodes, 2 * width), BF16), ((table_rows, points), BF16)],
        features, w_qkv, dec_source, dec_weight,
    )
    edge_rows = ((edges, nodes, width), BF16)
    node_out, head, tail, probs, attended, keys, values = on_core(
        "attend",
        attend_kernel,
        [
            ((nodes, width), BF16), rim_rows, rim_rows, ((nodes, columns), F32),
            ((nodes, width), BF16), edge_rows, edge_rows,
        ],
        hidden, left, right, queries, own_kv, w_qkv, w_out, edge_bias, edge_source, boundary,
        scalars=(node_count,),
        scratch=[pltpu.VMEM((table_rows, 2 * width), BF16)],
    )
    out_left, out_right = swap_rims(head, tail)
    message, change, sent = on_core(
        "decode",
        decode_kernel,
        [((width, points), BF16), ((variables, points), F32), ((variables, points), BF16)],
        node_out, out_left, out_right, mix, decoder_projection_weight,
        scratch=[pltpu.VMEM((table_rows, width), BF16)],
    )
    every = lax.all_gather(sent[None], "member", axis=0, tiled=True)
    grad, grad_message, head, tail, loss = score_call(
        rank, change, every, state, target, area[None], var_weight[:, None], mix,
        decoder_projection_weight,
        outs=[
            ((variables, points), BF16), ((width, points), BF16), rim_rows, rim_rows, ((8, LANES), F32),
        ],
        points=total_points,
    )
    back_left, back_right = swap_rims(head, tail)
    grad_own, grad_dec = on_core(
        "own_rows",
        own_rows_kernel,
        [((nodes, width), F32), ((width, variables), F32)],
        mix, grad_message, message, grad,
    )
    grad_node, grad_mixed, grad_out = on_core(
        "node_grad",
        node_grad_kernel,
        [((nodes, width), F32), ((nodes, width), BF16), ((width, width), F32)],
        grad_own, back_left, back_right, boundary, attended, w_out,
        scalars=(node_count,),
        scratch=[pltpu.VMEM((2 * rim, width), BF16)],
    )
    grad_query, grad_kv, head, tail = on_core(
        "attend_back",
        attend_back_kernel,
        [((nodes, width), BF16), ((table_rows, 2 * width), BF16), rim_rows, rim_rows],
        grad_mixed, queries, probs, keys, values, edge_source.T, w_qkv,
        scratch=[
            pltpu.VMEM((edges * nodes, 2 * width), BF16), pltpu.VMEM((table_rows, edges * nodes), BF16),
        ],
    )
    rim_left, rim_right = swap_rims(head, tail)

    packed = 4 * width + LANES
    rows = width // (regions * members)
    held = width // 2
    full = (held // rows, 2, rows, packed)
    half = (held // rows, rows, packed)
    send, keep = on_core(
        "weight_grad",
        weight_grad_kernel,
        [(half, BF16), (half, F32)],
        features, left, right, grad_query, grad_kv, grad_out, grad_dec, loss,
        scalars=(bits,),
        scratch=[pltpu.VMEM(full, F32)],
    )
    (own_feature,) = on_core(
        "own_feature", own_feature_kernel, [((nodes, width), F32)], grad_query, grad_kv, w_qkv
    )
    (grad_latent,) = on_core(
        "latent_grad",
        latent_grad_kernel,
        [((nodes, width), BF16)],
        hidden, gain, own_feature, rim_left, rim_right, boundary, grad_node,
        scratch=[pltpu.VMEM((2 * rim, width), BF16)],
    )

    kept_bits = []
    for axis, count in (("region", regions), ("member", members)):
        kept_bits += [(axis, 1 << b) for b in reversed(range(shift_of(count)))]
    for step, (axis, bit) in enumerate(order):
        count = lax.axis_size(axis)
        arrived = lax.ppermute(send, axis, [(i, i ^ bit) for i in range(count)])
        kept_bits.remove((axis, bit))
        if step + 1 == len(order):
            (total,) = on_core(
                "last", functools.partial(last_kernel, variables=variables),
                [((rows, packed), BF16)], keep.reshape(rows, packed), arrived.reshape(rows, packed),
            )
            break
        place = kept_bits.index(order[step + 1])
        before = 1 << place
        after = 1 << (len(kept_bits) - 1 - place)
        view = (before, 2, after * rows, packed)
        half = (before, after * rows, packed)
        send, keep = on_core(
            f"combine{step}",
            functools.partial(combine_kernel, which=step + 1, variables=variables),
            [(half, BF16), (half, F32)],
            keep.reshape(view), arrived.reshape(view),
            scalars=(bits,),
        )
    sums = lax.all_gather(total, "member", axis=0, tiled=True)
    held = sums.shape[0]
    share_qkv, share_out, share_dec, loss = on_core(
        "unpack",
        unpack_kernel,
        [((held, 3 * width), F32), ((held, width), F32), ((held, variables), F32), ((8, LANES), F32)],
        sums,
    )
    return (loss[0, 0], share_qkv, share_out, share_dec, grad_latent[None])


def solution(mesh):
    placed = (
        P("member", "region", None),
        P(),
        P(),
        P(),
        P("region", None),
        P("region", None),
        P("region", None),
        P("region"),
        P(),
        P(None, "region"),
        P(None, "region"),
        P(None, "region"),
        P(None, "region"),
        P("region"),
        P(),
    )
    return jax.shard_map(
        body,
        mesh=mesh,
        in_specs=placed,
        out_specs=(
            P(),
            P("region", None),
            P("region", None),
            P("region", None),
            P("member", "region", None),
        ),
        check_vma=False,
    )
```

time: 367 us -> 125 us (0.34)
  other arithmetic: 83.6 us -> 0 us
  waiting for transfers between devices: 101 us -> 29.2 us
  local copies, waits for them, and re-layouts: 81.8 us -> 19.1 us
  blocking collectives: 49 us -> 14.9 us
  Pallas kernels: 0 us -> 33.5 us
  between operations: 16.2 us -> 1.57 us
  matrix products: 13.8 us -> 0 us
  starting transfers between devices: 20.5 us -> 25.2 us
    psum x1 -> x0, waiting for transfers between devices: 92.3 us -> none  [body(): lax.psum((grad_qkv, grad_out, decoder_weight_gradient, partial_loss_value...]
    scatter-add x4 -> x0, other arithmetic: 43.6 us -> none  [the longest x1 19.5 us: body(): jax.ops.segment_sum(spread_rows, dec_source.reshape(-1), num_segments=tab...]
    psum x1 -> x0, blocking collectives: 39.7 us -> none  [body(): lax.psum((grad_qkv, grad_out, decoder_weight_gradient, partial_loss_value...]
    pallas_call x0 -> x17, Pallas kernels: none -> 33.5 us  [on_core(): pl.pallas_call(kernel, name=name, out_shape=[jax.ShapeDtypeStruct(s, d) f...]
    reshape x2 -> x0, local copies, waits for them, and re-layouts: 26.1 us -> none  [the longest x1 13.1 us: attend_backward(): grad_values.reshape(node_cap * edge_count, feature_width)]
    gather x4 -> x0, local copies, waits for them, and re-layouts: 25.3 us -> none  [the longest x1 13.3 us: body(): picked_rows = grid_table[dec_source]]
    ppermute x8 -> x13, waiting for transfers between devices: 8.5 us -> 29.2 us  [the longest x5 27.3 us: body(): arrived = lax.ppermute(send, axis, [(i, i ^ bit) for i in range(count)])]
    dot_general x12 -> x0, matrix products: 13.8 us -> none  [the longest x3 4.59 us: rows_dot(): lax.dot_general(left, right, (((0,), (0,)), ((), ())), preferred_element_...]
  transfers between devices with their start and end apart: 9 -> 13, of which waited for: 6 -> 8; matrix products, arithmetic and copies ran while one was open for 5% -> 2% of each run, Pallas kernels for 0% -> 4%
where the time goes in v1:
time: 125 us; the launch traced here: 123 us
  Pallas kernels  33.5 us (27%)
  waiting for transfers between devices  29.2 us (23%)
  starting transfers between devices  25.2 us (20%)
  local copies, waits for them, and re-layouts  19.1 us (15%)
  blocking collectives  14.9 us (12%)
  between operations  1.57 us (1%)
    pallas_call x17, Pallas kernels, on_core(): pl.pallas_call(kernel, name=name, out_shape=[jax.ShapeDtypeStruct(s, d) f...  33.5 us
    ppermute x5, waiting for transfers between devices, body(): arrived = lax.ppermute(send, axis, [(i, i ^ bit) for i in range(count)])  27.3 us
    unnamed x68, local copies, waits for them, and re-layouts  17.8 us
    ppermute x4, starting transfers between devices, swap_rims(): lax.ppermute(head, 'region', [((i + 1) % count, i) for i in range(count)])  16.8 us
    all_gather x1, blocking collectives, body(): every = lax.all_gather(sent[None], 'member', axis=0, tiled=True)  9.1 us
    all_gather x1, blocking collectives, body(): sums = lax.all_gather(total, 'member', axis=0, tiled=True)  5.81 us
    ppermute x5, starting transfers between devices, body(): arrived = lax.ppermute(send, axis, [(i, i ^ bit) for i in range(count)])  4.97 us
    ppermute x4, starting transfers between devices, swap_rims(): lax.ppermute(tail, 'region', [(i, (i + 1) % count) for i in range(count)])  3.4 us
  transfers between devices with their start and end apart: 13, of which 8 were waited for; matrix products, arithmetic and copies ran while one was open for 2% of the time, Pallas kernels for 4%

profile of v1, /device:TPU:0, one launch (start us, length us, event | category | flops | bytes accessed | tf_op | source)
XLA Modules:
  0.0 123.4 jit_solution(11941565042776791886)
XLA Ops:
  0.7 0.9 copy-done.2
  3.0 1.1 norm.1
  4.1 3.0 %collective-permute-start = (bf16[128,512]{1,0:T(8,128)(2,1)}, bf16[128,512]{1,0:T(8,128)(2,1)}, u32[]{:S(2)}, u32[]{:S(2)}) collective-permute-start(bf16[128,512]{1,0:T(8,128)(2,1)} %get-tuple-element.50), channel_id=1, source_target_pairs={{0,4},{4,8},{8,12},{12,16},{16,20},{20,24},{24,28},{28,0},{1,5},{5... | collective-permute-start | bytes 393224 | tf_op jit(solution)/shard_map/ppermute | solution.py:390
  7.1 3.0 %collective-permute-start.1 = (bf16[128,512]{1,0:T(8,128)(2,1)}, bf16[128,512]{1,0:T(8,128)(2,1)}, u32[]{:S(2)}, u32[]{:S(2)}) collective-permute-start(bf16[128,512]{1,0:T(8,128)(2,1)} %get-tuple-element.51), channel_id=1, source_target_pairs={{4,0},{8,4},{12,8},{16,12},{20,16},{24,20},{28,24},{0,28},{5,1},{9... | collective-permute-start | bytes 393224 | tf_op jit(solution)/shard_map/ppermute | solution.py:391
  10.8 0.8 copy.24.src_ref
  11.6 1.4 %copy-done = bf16[512,1536]{1,0:T(8,128)(2,1)S(1)} copy-done((bf16[512,1536]{1,0:T(8,128)(2,1)S(1)}, bf16[512,1536]{1,0:T(8,128)(2,1)}, u32[]{:S(2)}) %copy-start) | copy-done | bytes 1572888
  13.0 0.7 copy-done.25
  13.7 0.7 copy-done.26
  14.4 2.1 %project.1 = (bf16[256,512]{1,0:T(8,128)(2,1)S(1)}, bf16[256,1024]{1,0:T(8,128)(2,1)S(1)}, bf16[512,1024]{1,0:T(8,128)(2,1)S(1)}) custom-call(bf16[256,512]{1,0:T(8,128)(2,1)S(1)} %get-tuple-element.49.features_ref, bf16[512,1536]{1,0:T(8,128)(2,1)S(1)} %copy-done, s32[3,1024]{1,0:T(4,128)S(1)} %copy-done.25, f32[3,1024]{1,0:T(4,128)S(1)} %copy-done.26), custom_call_target="tpu_custom_call" | custom-call | tf_op jit(solution)/shard_map/project/pallas_call | solution.py:33
  16.6 1.0 copy-done.6
  17.6 7.7 %attend.1 = (bf16[256,512]{1,0:T(8,128)(2,1)S(1)}, bf16[128,512]{1,0:T(8,128)(2,1)}, bf16[128,512]{1,0:T(8,128)(2,1)}, f32[256,128]{1,0:T(8,128)S(1)}, bf16[256,...) custom-call(s32[1]{0:T(128)S(6)} %copy.28.count_ref, ...), custom_call_target="tpu_custom_call" | custom-call | tf_op jit(solution)/shard_map/attend/pallas_call | solution.py:33
  25.3 0.7 copy-done.14
  26.0 0.7 copy-done.16
  27.4 4.7 %collective-permute-start.3 = (bf16[128,512]{1,0:T(8,128)(2,1)}, bf16[128,512]{1,0:T(8,128)(2,1)}, u32[]{:S(2)}, u32[]{:S(2)}) collective-permute-start(bf16[128,512]{1,0:T(8,128)(2,1)} %get-tuple-element.57), channel_id=1, source_target_pairs={{4,0},{8,4},{12,8},{16,12},{20,16},{24,20},{28,24},{0,28},{5,1},{9... | collective-permute-start | bytes 393224 | tf_op jit(solution)/shard_map/ppermute | solution.py:391
  32.1 0.7 copy.26.var
  32.8 1.0 copy.25.w_ref.w
  33.9 1.6 %collective-permute-done.2.left_ref = bf16[128,512]{1,0:T(8,128)(2,1)} collective-permute-done((bf16[128,512]{1,0:T(8,128)(2,1)}, bf16[128,512]{1,0:T(8,128)(2,1)}, u32[]{:S(2)}, u32[]{:S(2)}) %collective-permute-start.2) | collective-permute-done | bytes 131104 | tf_op jit(solution)/shard_map/ppermute | solution.py:390
  35.5 0.9 copy-done.17
  36.4 1.9 %decode.1 = (bf16[512,1024]{1,0:T(8,128)(2,1)S(1)}, f32[98,1024]{1,0:T(8,128)S(1)}, bf16[98,1024]{1,0:T(8,128)(2,1)S(1)}) custom-call(bf16[256,512]{1,0:T(8,128)(2,1)S(1)} %copy-done.17, bf16[128,512]{1,0:T(8,128)(2,1)} %collective-permute-done.2.left_ref, bf16[128,512]{1,0:T(8,128)(2,1)} %collective-permute-done.3.right_ref, ...), custom_call_target="tpu_custom_call" | custom-call | tf_op jit(solution)/shard_map/decode/pallas_call | solution.py:33
  38.3 9.1 %all-gather.1.every = bf16[4,98,1024]{2,1,0:T(8,128)(2,1)S(1)} all-gather(bf16[1,98,1024]{2,1,0:T(8,128)(2,1)S(1)} %bitcast.34), channel_id=2, replica_groups=mesh['region'=8,'member'=4] {'member'}, dimensions={0}, use_global_device_ids=true | all-gather | bytes 1003520 | tf_op jit(solution)/shard_map/all_gather | solution.py:464
  47.4 2.2 %score.1 = (bf16[98,1024]{1,0:T(8,128)(2,1)S(1)}, bf16[512,1024]{1,0:T(8,128)(2,1)S(1)}, bf16[128,512]{1,0:T(8,128)(2,1)}, bf16[128,512]{1,0:T(8,128)(2,1)}, f32[8,128]{1,0:T(8,128)S(1)}) custom-call(s32[1]{0:T(128)} %bitcast.7.rank_ref, f32[98,1024]{1,0:T(8,128)S(1)} %get-tuple-element.58.change, bf16[4,98,1024]{2,1,0:T(8,128)(2,1)S(1)} %all-gather.1.every, ...), custom_call_target="tpu_custom_call" | custom-call | tf_op jit(solution)/shard_map/score/pallas_call | solution.py:33
  49.6 1.0 copy-done.10
  50.6 0.7 copy-done.18
  51.4 4.6 %collective-permute-start.5 = (bf16[128,512]{1,0:T(8,128)(2,1)}, bf16[128,512]{1,0:T(8,128)(2,1)}, u32[]{:S(2)}, u32[]{:S(2)}) collective-permute-start(bf16[128,512]{1,0:T(8,128)(2,1)} %get-tuple-element.65), channel_id=1, source_target_pairs={{4,0},{8,4},{12,8},{16,12},{20,16},{24,20},{28,24},{0,28},{5,1},{9... | collective-permute-start | bytes 393224 | tf_op jit(solution)/shard_map/ppermute | solution.py:391
  56.1 1.2 copy-done.9
  57.3 1.2 copy-done.11
  58.6 0.9 copy-done.19
  59.5 0.7 own_rows.1
  60.7 1.5 %node_grad.1 = (f32[256,512]{1,0:T(8,128)S(1)}, bf16[256,512]{1,0:T(8,128)(2,1)S(1)}, f32[512,512]{1,0:T(8,128)S(1)}) custom-call(s32[1]{0:T(128)S(6)} %copy.28.count_ref, f32[256,512]{1,0:T(8,128)S(1)} %get-tuple-element.63.own_ref, bf16[128,512]{1,0:T(8,128)(2,1)} %collective-permute-done.4.from_left_ref, ...), custom_call_target="tpu_custom_call" | custom-call | tf_op jit(solution)/shard_map/node_grad/pallas_call | solution.py:33
  62.2 6.5 %attend_back.1 = (bf16[256,512]{1,0:T(8,128)(2,1)S(1)}, bf16[512,1024]{1,0:T(8,128)(2,1)S(1)}, bf16[128,512]{1,0:T(8,128)(2,1)S(1)}, bf16[128,512]{1,0:T(8,128)(2,1)S(1)}) custom-call(bf16[256,512]{1,0:T(8,128)(2,1)S(1)} %get-tuple-element.67.mixed_ref, bf16[256,512]{1,0:T(8,128)(2,1)S(1)} %get-tuple-element.53.q_ref, f32[256,128]{1,0:T(8,128)S(1)} %copy-done.23, ...), custom_call_target="tpu_custom_call" | custom-call | tf_op jit(solution)/shard_map/attend_back/pallas_call | solution.py:33
  68.7 3.8 %weight_grad.1 = (bf16[16,16,2176]{2,1,0:T(8,128)(2,1)S(1)}, f32[16,16,2176]{2,1,0:T(8,128)}) custom-call(s32[5]{0:T(128)S(1)} %stack.23.bits_ref, bf16[256,512]{1,0:T(8,128)(2,1)S(1)} %get-tuple-element.49.features_ref, bf16[128,512]{1,0:T(8,128)(2,1)} %collective-permute-done.left_ref, bf16[128,512]{1,0:T(8,128)(2,1)} %collective-permute-done.1.right_ref, ...), custom_call_target="tpu_custom_call" | custom-call | tf_op jit(solution)/shard_map/weight_grad/pallas_call | solution.py:33
  72.5 2.8 %collective-permute-done.6 = bf16[16,16,2176]{2,1,0:T(8,128)(2,1)S(1)} collective-permute-done((bf16[16,16,2176]{2,1,0:T(8,128)(2,1)S(1)}, bf16[16,16,2176]{2,1,0:T(8,128)(2,1)S(1)}, u32[]{:S(2)}, u32[]{:S(2)}) %collective-permute-start.6) | collective-permute-done | bytes 1114144 | tf_op jit(solution)/shard_map/ppermute | solution.py:528
  75.3 1.6 %copy-done.4 = f32[16,16,2176]{2,1,0:T(8,128)S(1)} copy-done((f32[16,16,2176]{2,1,0:T(8,128)S(1)}, f32[16,16,2176]{2,1,0:T(8,128)}, u32[]{:S(2)}) %copy-start.4) | copy-done | bytes 2228248
  76.9 0.9 combine0.1
  77.9 1.3 %collective-permute-start.7 = (bf16[8,16,2176]{2,1,0:T(8,128)(2,1)S(1)}, bf16[8,16,2176]{2,1,0:T(8,128)(2,1)S(1)}, u32[]{:S(2)}, u32[]{:S(2)}) collective-permute-start(bf16[8,16,2176]{2,1,0:T(8,128)(2,1)S(1)} %get-tuple-element.79), channel_id=1, source_target_pairs={{0,2},{1,3},{2,0},{3,1},{4,6},{5,7},{6,4},{7,5},{8,10},{9,11},{10,... | collective-permute-start | bytes 1671176 | tf_op jit(solution)/shard_map/ppermute | solution.py:528
  79.2 13.4 %collective-permute-done.7 = bf16[8,16,2176]{2,1,0:T(8,128)(2,1)S(1)} collective-permute-done((bf16[8,16,2176]{2,1,0:T(8,128)(2,1)S(1)}, bf16[8,16,2176]{2,1,0:T(8,128)(2,1)S(1)}, u32[]{:S(2)}, u32[]{:S(2)}) %collective-permute-start.7) | collective-permute-done | bytes 557088 | tf_op jit(solution)/shard_map/ppermute | solution.py:528
  92.6 0.8 combine1.1
  93.5 7.8 %collective-permute-done.8 = bf16[4,16,2176]{2,1,0:T(8,128)(2,1)S(1)} collective-permute-done((bf16[4,16,2176]{2,1,0:T(8,128)(2,1)S(1)}, bf16[4,16,2176]{2,1,0:T(8,128)(2,1)S(1)}, u32[]{:S(2)}, u32[]{:S(2)}) %collective-permute-start.8) | collective-permute-done | bytes 278560 | tf_op jit(solution)/shard_map/ppermute | solution.py:528
  101.3 0.8 combine2.1
  102.1 2.5 %collective-permute-start.9 = (bf16[1,32,2176]{2,1,0:T(8,128)(2,1)S(1)}, bf16[1,32,2176]{2,1,0:T(8,128)(2,1)S(1)}, u32[]{:S(2)}, u32[]{:S(2)}) collective-permute-start(bf16[1,32,2176]{2,1,0:T(8,128)(2,1)S(1)} %get-tuple-element.83), channel_id=1, source_target_pairs={{0,16},{4,20},{8,24},{12,28},{16,0},{20,4},{24,8},{28,12},{1,17},{... | collective-permute-start | bytes 417800 | tf_op jit(solution)/shard_map/ppermute | solution.py:528
  104.9 4.4 %collective-permute-start.12 = (bf16[128,512]{1,0:T(8,128)(2,1)S(1)}, bf16[128,512]{1,0:T(8,128)(2,1)S(1)}, u32[]{:S(2)}, u32[]{:S(2)}) collective-permute-start(bf16[128,512]{1,0:T(8,128)(2,1)S(1)} %get-tuple-element.91), channel_id=1, source_target_pairs={{4,0},{8,4},{12,8},{16,12},{20,16},{24,20},{28,24},{0,28},{5,1},{9... | collective-permute-start | bytes 393224 | tf_op jit(solution)/shard_map/ppermute | solution.py:391
  109.3 1.7 %collective-permute-done.9 = bf16[1,32,2176]{2,1,0:T(8,128)(2,1)S(1)} collective-permute-done((bf16[1,32,2176]{2,1,0:T(8,128)(2,1)S(1)}, bf16[1,32,2176]{2,1,0:T(8,128)(2,1)S(1)}, u32[]{:S(2)}, u32[]{:S(2)}) %collective-permute-start.9) | collective-permute-done | bytes 139296 | tf_op jit(solution)/shard_map/ppermute | solution.py:528
  111.1 0.7 combine3.1
  111.8 1.1 collective-permute-start.10
  113.5 1.2 latent_grad.1
  114.6 1.5 %collective-permute-done.10 = bf16[1,16,2176]{2,1,0:T(8,128)(2,1)S(1)} collective-permute-done((bf16[1,16,2176]{2,1,0:T(8,128)(2,1)S(1)}, bf16[1,16,2176]{2,1,0:T(8,128)(2,1)S(1)}, u32[]{:S(2)}, u32[]{:S(2)}) %collective-permute-start.10) | collective-permute-done | bytes 69664 | tf_op jit(solution)/shard_map/ppermute | solution.py:528
  116.3 5.8 %all_gather.7.sums_ref = bf16[64,2176]{1,0:T(8,128)(2,1)S(1)} all-gather(bf16[16,2176]{1,0:T(8,128)(2,1)S(1)} %last.1), channel_id=1, replica_groups=mesh['region'=8,'member'=4] {'member'}, dimensions={0}, use_global_device_ids=true | all-gather | bytes 348160 | tf_op jit(solution)/shard_map/all_gather | solution.py:548
  122.1 0.8 unpack.1
  (68 shorter events, 4.3 us)
Async XLA Ops:
  0.6 15.9 %copy-start.28 = (s32[1,256]{1,0:T(1,128)S(1)}, s32[1,256]{1,0:T(1,128)}, u32[]{:S(2)}) copy-start(s32[1,256]{1,0:T(1,128)} %border_ref.7) | copy-start | bytes 3076
  0.6 1.0 copy-start.2
  1.6 0.7 copy-start.27
  2.3 0.7 copy-start.29
  3.0 13.6 %copy-start.3 = (bf16[1,256,512]{2,1,0:T(8,128)(2,1)S(1)}, bf16[1,256,512]{2,1,0:T(8,128)(2,1)}, u32[]{:S(2)}) copy-start(bf16[1,256,512]{2,1,0:T(8,128)(2,1)} %param.15) | copy-start | bytes 786436
  4.1 12.4 %collective-permute-start = (bf16[128,512]{1,0:T(8,128)(2,1)}, bf16[128,512]{1,0:T(8,128)(2,1)}, u32[]{:S(2)}, u32[]{:S(2)}) collective-permute-start(bf16[128,512]{1,0:T(8,128)(2,1)} %get-tuple-element.50), channel_id=1, source_target_pairs={{0,4},{4,8},{8,12},{12,16},{16,20},{20,24},{24,28},{28,0},{1,5},{5... | collective-permute-start | bytes 393224 | tf_op jit(solution)/shard_map/ppermute | solution.py:390
  7.1 9.5 %collective-permute-start.1 = (bf16[128,512]{1,0:T(8,128)(2,1)}, bf16[128,512]{1,0:T(8,128)(2,1)}, u32[]{:S(2)}, u32[]{:S(2)}) collective-permute-start(bf16[128,512]{1,0:T(8,128)(2,1)} %get-tuple-element.51), channel_id=1, source_target_pairs={{4,0},{8,4},{12,8},{16,12},{20,16},{24,20},{28,24},{0,28},{5,1},{9... | collective-permute-start | bytes 393224 | tf_op jit(solution)/shard_map/ppermute | solution.py:391
  11.6 1.4 %copy-start = (bf16[512,1536]{1,0:T(8,128)(2,1)S(1)}, bf16[512,1536]{1,0:T(8,128)(2,1)}, u32[]{:S(2)}) copy-start(bf16[512,1536]{1,0:T(8,128)(2,1)} %w_ref.8) | copy-start | bytes 4718596
  13.0 0.7 copy-start.25
  13.7 0.7 copy-start.26
  14.4 2.1 %copy-start.1 = (bf16[512,1536]{1,0:T(8,128)(2,1)S(1)}, bf16[512,1536]{1,0:T(8,128)(2,1)}, u32[]{:S(2)}) copy-start(bf16[512,1536]{1,0:T(8,128)(2,1)} %w_ref.8) | copy-start | bytes 4718596
  14.4 2.1 %copy-start.21 = (f32[256,128]{1,0:T(8,128)S(1)}, f32[256,128]{1,0:T(8,128)}, u32[]{:S(2)}) copy-start(f32[256,128]{1,0:T(8,128)} %bias_ref.1) | copy-start | bytes 393220
  16.6 1.0 copy-start.6
  17.6 14.5 %copy-start.32 = (f32[98]{0:T(128)S(1)}, f32[98]{0:T(128)}, u32[]{:S(2)}) copy-start(f32[98]{0:T(128)} %param.29) | copy-start | bytes 1180
  25.3 0.7 copy-start.14
  26.0 0.7 copy-start.16
  26.7 0.6 copy-start.22
  27.4 20.1 %copy-start.31 = (f32[1024]{0:T(1024)S(1)}, f32[1024]{0:T(1024)}, u32[]{:S(2)}) copy-start(f32[1024]{0:T(1024)} %param.28) | copy-start | bytes 12292
  27.4 8.1 %collective-permute-start.2 = (bf16[128,512]{1,0:T(8,128)(2,1)}, bf16[128,512]{1,0:T(8,128)(2,1)}, u32[]{:S(2)}, u32[]{:S(2)}) collective-permute-start(bf16[128,512]{1,0:T(8,128)(2,1)} %get-tuple-element.56), channel_id=1, source_target_pairs={{0,4},{4,8},{8,12},{12,16},{16,20},{20,24},{24,28},{28,0},{1,5},{5... | collective-permute-start | bytes 393224 | tf_op jit(solution)/shard_map/ppermute | solution.py:390
  27.4 8.1 %collective-permute-start.3 = (bf16[128,512]{1,0:T(8,128)(2,1)}, bf16[128,512]{1,0:T(8,128)(2,1)}, u32[]{:S(2)}, u32[]{:S(2)}) collective-permute-start(bf16[128,512]{1,0:T(8,128)(2,1)} %get-tuple-element.57), channel_id=1, source_target_pairs={{4,0},{8,4},{12,8},{16,12},{20,16},{24,20},{28,24},{0,28},{5,1},{9... | collective-permute-start | bytes 393224 | tf_op jit(solution)/shard_map/ppermute | solution.py:391
  33.8 13.6 %copy-start.12 = (f32[98,1024]{1,0:T(8,128)S(1)}, f32[98,1024]{1,0:T(8,128)}, u32[]{:S(2)}) copy-start(f32[98,1024]{1,0:T(8,128)} %state.1) | copy-start | bytes 1204228
  33.9 13.6 %copy-start.13 = (f32[98,1024]{1,0:T(8,128)S(1)}, f32[98,1024]{1,0:T(8,128)}, u32[]{:S(2)}) copy-start(f32[98,1024]{1,0:T(8,128)} %target.1) | copy-start | bytes 1204228
  35.5 1.0 copy-start.17
  36.4 11.0 %copy-start.20 = (f32[98,1]{1,0:T(8,128)S(1)}, f32[98,1]{1,0:T(8,128)}, u32[]{:S(2)}) copy-start(f32[98,1]{1,0:T(8,128)} %copy.26.var) | copy-start | bytes 1180
  38.3 11.3 %copy-start.8 = (bf16[512,1024]{1,0:T(8,128)(2,1)}, bf16[512,1024]{1,0:T(8,128)(2,1)S(1)}, u32[]{:S(2)}) copy-start(bf16[512,1024]{1,0:T(8,128)(2,1)S(1)} %get-tuple-element.61.message_ref) | copy-start | bytes 3145732
  49.6 1.0 copy-start.10
  50.6 0.7 copy-start.18
  51.3 9.1 %collective-permute-start.4 = (bf16[128,512]{1,0:T(8,128)(2,1)}, bf16[128,512]{1,0:T(8,128)(2,1)}, u32[]{:S(2)}, u32[]{:S(2)}) collective-permute-start(bf16[128,512]{1,0:T(8,128)(2,1)} %get-tuple-element.64), channel_id=1, source_target_pairs={{0,4},{4,8},{8,12},{12,16},{16,20},{20,24},{24,28},{28,0},{1,5},{5... | collective-permute-start | bytes 393224 | tf_op jit(solution)/shard_map/ppermute | solution.py:390
  51.4 9.2 %collective-permute-start.5 = (bf16[128,512]{1,0:T(8,128)(2,1)}, bf16[128,512]{1,0:T(8,128)(2,1)}, u32[]{:S(2)}, u32[]{:S(2)}) collective-permute-start(bf16[128,512]{1,0:T(8,128)(2,1)} %get-tuple-element.65), channel_id=1, source_target_pairs={{4,0},{8,4},{12,8},{16,12},{20,16},{24,20},{28,24},{0,28},{5,1},{9... | collective-permute-start | bytes 393224 | tf_op jit(solution)/shard_map/ppermute | solution.py:391
  56.1 1.2 copy-start.9
  57.3 1.2 copy-start.11
  58.6 0.9 copy-start.19
  59.5 1.2 copy-start.7
  59.5 1.2 copy-start.15
  59.5 2.7 %copy-start.5 = (bf16[8,256,512]{2,1,0:T(8,128)(2,1)S(1)}, bf16[8,256,512]{2,1,0:T(8,128)(2,1)}, u32[]{:S(2)}) copy-start(bf16[8,256,512]{2,1,0:T(8,128)(2,1)} %get-tuple-element.69.keys_ref) | copy-start | bytes 6291460
  60.3 2.0 %copy-start.23 = (f32[256,128]{1,0:T(8,128)S(1)}, f32[256,128]{1,0:T(8,128)}, u32[]{:S(2)}) copy-start(f32[256,128]{1,0:T(8,128)} %copy-done.22) | copy-start | bytes 393220
  60.3 2.0 %copy-start.24 = (s32[256,8]{0,1:T(8,128)S(1)}, s32[256,8]{0,1:T(8,128)}, u32[]{:S(2)}) copy-start(s32[256,8]{0,1:T(8,128)} %param.20) | copy-start | bytes 24580
  72.5 2.8 %collective-permute-start.6 = (bf16[16,16,2176]{2,1,0:T(8,128)(2,1)S(1)}, bf16[16,16,2176]{2,1,0:T(8,128)(2,1)S(1)}, u32[]{:S(2)}, u32[]{:S(2)}) collective-permute-start(bf16[16,16,2176]{2,1,0:T(8,128)(2,1)S(1)} %get-tuple-element.77), channel_id=1, source_target_pairs={{0,1},{1,0},{2,3},{3,2},{4,5},{5,4},{6,7},{7,6},{8,9},{9,8},{10,11... | collective-permute-start | bytes 3342344 | tf_op jit(solution)/shard_map/ppermute | solution.py:528
  75.3 1.6 %copy-start.4 = (f32[16,16,2176]{2,1,0:T(8,128)S(1)}, f32[16,16,2176]{2,1,0:T(8,128)}, u32[]{:S(2)}) copy-start(f32[16,16,2176]{2,1,0:T(8,128)} %get-tuple-element.76) | copy-start | bytes 6684676
  77.9 14.7 %collective-permute-start.7 = (bf16[8,16,2176]{2,1,0:T(8,128)(2,1)S(1)}, bf16[8,16,2176]{2,1,0:T(8,128)(2,1)S(1)}, u32[]{:S(2)}, u32[]{:S(2)}) collective-permute-start(bf16[8,16,2176]{2,1,0:T(8,128)(2,1)S(1)} %get-tuple-element.79), channel_id=1, source_target_pairs={{0,2},{1,3},{2,0},{3,1},{4,6},{5,7},{6,4},{7,5},{8,10},{9,11},{10,... | collective-permute-start | bytes 1671176 | tf_op jit(solution)/shard_map/ppermute | solution.py:528
  93.4 7.9 %collective-permute-start.8 = (bf16[4,16,2176]{2,1,0:T(8,128)(2,1)S(1)}, bf16[4,16,2176]{2,1,0:T(8,128)(2,1)S(1)}, u32[]{:S(2)}, u32[]{:S(2)}) collective-permute-start(bf16[4,16,2176]{2,1,0:T(8,128)(2,1)S(1)} %get-tuple-element.81), channel_id=1, source_target_pairs={{0,4},{4,0},{8,12},{12,8},{16,20},{20,16},{24,28},{28,24},{1,5},{5... | collective-permute-start | bytes 835592 | tf_op jit(solution)/shard_map/ppermute | solution.py:528
  102.1 9.0 %collective-permute-start.9 = (bf16[1,32,2176]{2,1,0:T(8,128)(2,1)S(1)}, bf16[1,32,2176]{2,1,0:T(8,128)(2,1)S(1)}, u32[]{:S(2)}, u32[]{:S(2)}) collective-permute-start(bf16[1,32,2176]{2,1,0:T(8,128)(2,1)S(1)} %get-tuple-element.83), channel_id=1, source_target_pairs={{0,16},{4,20},{8,24},{12,28},{16,0},{20,4},{24,8},{28,12},{1,17},{... | collective-permute-start | bytes 417800 | tf_op jit(solution)/shard_map/ppermute | solution.py:528
  104.6 8.8 %collective-permute-start.11 = (bf16[128,512]{1,0:T(8,128)(2,1)S(1)}, bf16[128,512]{1,0:T(8,128)(2,1)S(1)}, u32[]{:S(2)}, u32[]{:S(2)}) collective-permute-start(bf16[128,512]{1,0:T(8,128)(2,1)S(1)} %get-tuple-element.90), channel_id=1, source_target_pairs={{0,4},{4,8},{8,12},{12,16},{16,20},{20,24},{24,28},{28,0},{1,5},{5... | collective-permute-start | bytes 393224 | tf_op jit(solution)/shard_map/ppermute | solution.py:390
  104.9 8.6 %collective-permute-start.12 = (bf16[128,512]{1,0:T(8,128)(2,1)S(1)}, bf16[128,512]{1,0:T(8,128)(2,1)S(1)}, u32[]{:S(2)}, u32[]{:S(2)}) collective-permute-start(bf16[128,512]{1,0:T(8,128)(2,1)S(1)} %get-tuple-element.91), channel_id=1, source_target_pairs={{4,0},{8,4},{12,8},{16,12},{20,16},{24,20},{28,24},{0,28},{5,1},{9... | collective-permute-start | bytes 393224 | tf_op jit(solution)/shard_map/ppermute | solution.py:391
  111.8 1.7 %copy-start.30 = (f32[512]{0:T(512)S(1)}, f32[512]{0:T(512)}, u32[]{:S(2)}) copy-start(f32[512]{0:T(512)} %param.16) | copy-start | bytes 6148
  111.8 4.4 %collective-permute-start.10 = (bf16[1,16,2176]{2,1,0:T(8,128)(2,1)S(1)}, bf16[1,16,2176]{2,1,0:T(8,128)(2,1)S(1)}, u32[]{:S(2)}, u32[]{:S(2)}) collective-permute-start(bf16[1,16,2176]{2,1,0:T(8,128)(2,1)S(1)} %get-tuple-element.85), channel_id=1, source_target_pairs={{0,8},{4,12},{8,0},{12,4},{16,24},{20,28},{24,16},{28,20},{1,9},{5... | collective-permute-start | bytes 208904 | tf_op jit(solution)/shard_map/ppermute | solution.py:528

commit v2 on v1

v2 whole, which is shorter than its diff:
```python
import functools
import math

import jax
import jax.numpy as jnp
from jax import lax
from jax.experimental import pallas as pl
from jax.experimental.pallas import tpu as pltpu
from jax.sharding import PartitionSpec as P


ALPHA = 0.95
NORM_EPS = 1e-05
SMOOTH_SQ = 0.25
SMOOTH_ROOT = 0.5
F32 = jnp.float32
BF16 = jnp.bfloat16
LANES = 128


def nn(left, right):
    return lax.dot_general(left, right, (((1,), (0,)), ((), ())), preferred_element_type=F32)


def nt(left, right):
    return lax.dot_general(left, right, (((1,), (1,)), ((), ())), preferred_element_type=F32)


def tn(left, right):
    return lax.dot_general(left, right, (((0,), (0,)), ((), ())), preferred_element_type=F32)


def on_core(kernel, outs, *args, fetched=0, scratch=(), mib=8):
    return pl.pallas_call(
        kernel,
        out_shape=[jax.ShapeDtypeStruct(s, d) for s, d in outs],
        in_specs=[pl.BlockSpec(memory_space=pltpu.HBM)] * fetched
        + [pl.BlockSpec(memory_space=pltpu.VMEM)] * (len(args) - fetched),
        out_specs=[pl.BlockSpec(memory_space=pltpu.VMEM)] * len(outs),
        scratch_shapes=list(scratch) + [pltpu.SemaphoreType.DMA((fetched,))] * (fetched > 0),
        compiler_params=pltpu.CompilerParams(vmem_limit_bytes=mib * 1024 * 1024),
    )(*[pltpu.with_memory_space_constraint(a, pltpu.HBM) for a in args[:fetched]], *args[fetched:])


def iota(shape, dim):
    return lax.broadcasted_iota(jnp.int32, shape, dim)


def ones_where(mask):
    return jnp.where(mask, 1.0, 0.0).astype(BF16)


def shift_of(size):
    assert size & (size - 1) == 0
    return size.bit_length() - 1


def head_map(rows, cols, row_size, col_size):
    return ones_where(
        (iota((rows, cols), 0) >> shift_of(row_size)) == (iota((rows, cols), 1) >> shift_of(col_size))
    )


def group_reduce(values, size, op):
    lanes = values.shape[1]
    lane = iota(values.shape, 1)
    step = 1
    while step < size:
        partner = jnp.where(
            (lane & step) == 0,
            pltpu.roll(values, lanes - step, 1),
            pltpu.roll(values, step, 1),
        )
        values = op(values, partner)
        step *= 2
    return values


def norm_parts(hidden):
    values = hidden.astype(F32)
    center = values - jnp.mean(values, axis=-1, keepdims=True)
    inverse = lax.rsqrt(jnp.mean(center * center, axis=-1, keepdims=True) + NORM_EPS)
    return center * inverse, inverse


def bit_of(axis, bit):
    return (lax.axis_index(axis) >> shift_of(bit)) & 1


def border_map(border_ref, nodes):
    return ones_where(iota((nodes, border_ref.shape[1]), 0) == border_ref[...])


def fetch(pairs, sems):
    copies = [pltpu.make_async_copy(a, b, sems.at[i]) for i, (a, b) in enumerate(pairs)]
    for copy in copies:
        copy.start()
    return copies


def norm_kernel(
    hidden_hbm, gain_hbm, border_hbm, features_ref, head_ref, tail_ref, hidden_ref, gain_ref, border_ref, sems
):
    pairs = ((hidden_hbm, hidden_ref), (gain_hbm, gain_ref), (border_hbm, border_ref))
    for copy in fetch(pairs, sems):
        copy.wait()
    scaled, _ = norm_parts(hidden_ref[...])
    features = (scaled * gain_ref[...]).astype(BF16)
    features_ref[...] = features
    rows = tn(border_map(border_ref, features.shape[0]), features).astype(BF16)
    rim = head_ref.shape[0]
    head_ref[...] = rows[:rim]
    tail_ref[...] = rows[rim:]


def project_kernel(
    w_hbm, src_hbm, weight_hbm, features_ref, q_ref, kv_ref, mix_ref, w_ref, src_ref, weight_ref, sems
):
    copies = fetch(((src_hbm, src_ref), (weight_hbm, weight_ref), (w_hbm, w_ref)), sems)
    width = features_ref.shape[1]
    rows = iota(mix_ref.shape, 0)
    copies[0].wait()
    copies[1].wait()
    total = jnp.zeros(mix_ref.shape, F32)
    for j in range(src_ref.shape[0]):
        total += jnp.where(rows == src_ref[j : j + 1, :], weight_ref[j : j + 1, :], 0.0)
    mix_ref[...] = total.astype(BF16)
    copies[2].wait()
    qkv = nn(features_ref[...], w_ref[...]).astype(BF16)
    q_ref[...] = qkv[:, :width]
    kv_ref[...] = qkv[:, width:]


def attend_kernel(
    w_out_hbm, bias_hbm, dec_hbm, count_ref, hidden_ref, left_ref, right_ref, q_ref, kv_ref, w_ref,
    src_ref, border_ref, out_ref, projected_ref, head_ref, tail_ref, probs_ref, attended_ref, keys_ref, values_ref, table_ref,
    w_out_ref, bias_ref, dec_ref, sems,
):
    copies = fetch(((bias_hbm, bias_ref), (w_out_hbm, w_out_ref), (dec_hbm, dec_ref)), sems)
    nodes, width = hidden_ref.shape
    rim = left_ref.shape[0]
    edges = src_ref.shape[0]
    columns = bias_ref.shape[1]
    sources = src_ref[...].astype(F32).T
    head_size = width // (columns // edges)
    w_kv = w_ref[:, width:]
    table_ref[:nodes] = kv_ref[...]
    table_ref[nodes : nodes + rim] = nn(left_ref[...], w_kv).astype(BF16)
    table_ref[nodes + rim :] = nn(right_ref[...], w_kv).astype(BF16)
    table = table_ref[...]
    queries = q_ref[...].astype(F32)
    squeeze = head_map(width, columns, head_size, edges)
    expand = head_map(columns, width, edges, head_size)
    lane = iota((nodes, columns), 1) & (edges - 1)
    slot = iota((nodes, table.shape[0]), 1).astype(F32)
    scores = jnp.zeros((nodes, columns), F32)
    for e in range(edges):
        rows = nn(ones_where(slot == sources[:, e : e + 1]), table)
        keys_ref[e] = rows[:, :width].astype(BF16)
        values_ref[e] = rows[:, width:].astype(BF16)
        part = nn((queries * rows[:, :width]).astype(BF16), squeeze)
        scores = jnp.where(lane == e, part, scores)
    copies[0].wait()
    scores = scores / math.sqrt(head_size) + bias_ref[...]
    shifted = jnp.exp(scores - group_reduce(scores, edges, jnp.maximum))
    probs = shifted / group_reduce(shifted, edges, jnp.add)
    probs_ref[...] = probs
    total = jnp.zeros((nodes, width), F32)
    for e in range(edges):
        share = nn(jnp.where(lane == e, probs, 0.0).astype(BF16), expand)
        total += share * values_ref[e].astype(F32)
    attended = total.astype(BF16)
    attended_ref[...] = attended
    copies[1].wait()
    update = hidden_ref[...].astype(F32) + nn(attended, w_out_ref[...])
    live = iota((nodes, width), 0) < count_ref[...]
    node_out = jnp.where(live, update, 0.0).astype(BF16)
    out_ref[...] = node_out
    copies[2].wait()
    projected = nt(dec_ref[...], node_out).astype(BF16)
    projected_ref[...] = projected
    columns = nn(projected, border_map(border_ref, nodes)).astype(BF16)
    head_ref[...] = columns[:, :rim]
    tail_ref[...] = columns[:, rim:]


def decode_kernel(own_ref, left_ref, right_ref, mix_ref, change_ref, sent_ref):
    table = jnp.concatenate([own_ref[...], left_ref[...], right_ref[...]], axis=1)
    change = nn(table, mix_ref[...])
    change_ref[...] = change
    sent_ref[...] = change.astype(BF16)


def smooth_root(values):
    return values * values + SMOOTH_SQ


def score_kernel(
    change_ref, every_ref, state_ref, target_ref, area_ref, var_ref, mix_ref,
    grad_ref, head_ref, tail_ref, loss_ref, *, points,
):
    members = every_ref.shape[0]
    fair = 1.0 - (1.0 - ALPHA) / members
    pair = fair / (2.0 * members * (members - 1))
    own = change_ref[...]
    variables = own.shape[0]
    spread = jnp.zeros_like(own)
    slope = jnp.zeros_like(own)
    me = lax.axis_index("member")
    for n in range(members):
        other = jnp.where(me == n, own, every_ref[n].astype(F32))
        gap = own - other
        square = smooth_root(gap)
        inverse = lax.rsqrt(square)
        spread += square * inverse - SMOOTH_ROOT
        slope += gap * inverse
    gap = state_ref[...] + own - target_ref[...]
    square = smooth_root(gap)
    inverse = lax.rsqrt(square)
    square_map = (variables, variables)
    diagonal = iota(square_map, 0) == iota(square_map, 1)
    var = jnp.sum(jnp.where(diagonal, var_ref[...], 0.0), axis=1, keepdims=True)
    weight = area_ref[...] * var / variables
    term = (square * inverse - SMOOTH_ROOT) / members - pair * spread
    loss_ref[...] = jnp.full(loss_ref.shape, jnp.sum(term * weight) / points, F32)
    grad = ((gap * inverse / members - 2.0 * pair * slope) * weight).astype(BF16)
    grad_ref[...] = grad
    rim = head_ref.shape[1]
    nodes = mix_ref.shape[0] - 2 * rim
    columns = nt(grad, mix_ref[nodes:, :]).astype(BF16)
    head_ref[...] = columns[:, :rim]
    tail_ref[...] = columns[:, rim:]


def own_rows_kernel(mix_ref, grad_ref, src_ref, own_ref, hot_ref):
    nodes = own_ref.shape[1]
    own_ref[...] = nt(grad_ref[...], mix_ref[:nodes, :])
    slot = iota((hot_ref.shape[0], nodes), 0)
    for e in range(src_ref.shape[0]):
        hot_ref[:, e * nodes : (e + 1) * nodes] = ones_where(slot == src_ref[e : e + 1, :])


def split_halves(mine, source_ref, send_ref, keep_ref):
    for i in range(send_ref.shape[0]):
        send_ref[i] = source_ref[i, 1 - mine].astype(BF16)
        keep_ref[i] = source_ref[i, mine]


def put(full_ref, start, values):
    shape = full_ref.shape[:3]
    full_ref[:, :, :, start : start + values.shape[1]] = values.reshape(*shape, values.shape[1])


def value_back_kernel(
    count_ref, own_ref, from_left_ref, from_right_ref, border_ref, node_out_ref, w_dec_ref,
    attended_ref, w_out_ref, probs_ref, hot_ref, features_ref, left_ref, right_ref, loss_ref,
    grad_ref, mixed_ref, grad_value_ref, send_ref, keep_ref, edge_ref, full_ref,
):
    nodes, width = grad_ref.shape
    rim = left_ref.shape[0]
    columns = probs_ref.shape[1]
    edges = hot_ref.shape[1] // nodes
    head_size = width // (columns // edges)
    returned = jnp.concatenate([from_left_ref[...], from_right_ref[...]], axis=1)
    columns_grad = (own_ref[...] + nt(returned, border_map(border_ref, nodes))).astype(BF16)
    total = tn(columns_grad, w_dec_ref[...])
    total = jnp.where(iota((nodes, width), 0) < count_ref[...], total, 0.0)
    grad_ref[...] = total
    rounded = total.astype(BF16)
    mixed = nt(rounded, w_out_ref[...]).astype(BF16)
    mixed_ref[...] = mixed
    mixed = mixed.astype(F32)
    expand = head_map(columns, width, edges, head_size)
    lane = iota((nodes, columns), 1) & (edges - 1)
    probs = probs_ref[...]
    for e in range(edges):
        share = nn(jnp.where(lane == e, probs, 0.0).astype(BF16), expand)
        edge_ref[e * nodes : (e + 1) * nodes, :] = (share * mixed).astype(BF16)
    grad_value = nn(hot_ref[...], edge_ref[...]).astype(BF16)
    grad_value_ref[...] = grad_value
    features = features_ref[...]
    total = tn(features, grad_value[:nodes])
    total += tn(left_ref[...], grad_value[nodes : nodes + rim])
    total += tn(right_ref[...], grad_value[nodes + rim :])
    put(full_ref, 0, total)
    put(full_ref, width, tn(attended_ref[...], rounded))
    variables = columns_grad.shape[0]
    dec = nn(columns_grad, node_out_ref[...])
    pad = jnp.concatenate([dec, jnp.zeros((LANES - variables, width), F32)], axis=0).T
    loss = jnp.broadcast_to(loss_ref[0:1, 0:1], (width, LANES))
    high = loss.astype(BF16).astype(F32)
    lane = iota((width, LANES), 1)
    pad = jnp.where(lane == variables, high, pad)
    pad = jnp.where(lane == variables + 1, loss - high, pad)
    put(full_ref, 2 * width, pad)
    split_halves(bit_of("member", 1), full_ref, send_ref, keep_ref)


def score_back_kernel(mixed_ref, probs_ref, values_ref, grad_ref):
    nodes, width = mixed_ref.shape
    edges = values_ref.shape[0]
    columns = probs_ref.shape[1]
    squeeze = head_map(width, columns, width // (columns // edges), edges)
    lane = iota((nodes, columns), 1) & (edges - 1)
    mixed = mixed_ref[...].astype(F32)
    probs = probs_ref[...]
    grad_probs = jnp.zeros((nodes, columns), F32)
    for e in range(edges):
        part = nn((mixed * values_ref[e].astype(F32)).astype(BF16), squeeze)
        grad_probs = jnp.where(lane == e, part, grad_probs)
    grad_ref[...] = probs * (grad_probs - group_reduce(probs * grad_probs, edges, jnp.add))


def query_back_kernel(
    grad_scores_ref, q_ref, keys_ref, hot_ref, grad_value_ref, w_ref,
    grad_query_ref, grad_key_ref, head_ref, tail_ref, edge_ref,
):
    nodes, width = q_ref.shape
    edges = keys_ref.shape[0]
    columns = grad_scores_ref.shape[1]
    head_size = width // (columns // edges)
    inv_root = 1.0 / math.sqrt(head_size)
    expand = head_map(columns, width, edges, head_size)
    lane = iota((nodes, columns), 1) & (edges - 1)
    grad_scores = grad_scores_ref[...]
    query = q_ref[...].astype(F32) * inv_root
    total = jnp.zeros((nodes, width), F32)
    for e in range(edges):
        share = nn(jnp.where(lane == e, grad_scores, 0.0).astype(BF16), expand)
        total += share * keys_ref[e].astype(F32)
        edge_ref[e * nodes : (e + 1) * nodes, :] = (share * query).astype(BF16)
    grad_query_ref[...] = (total * inv_root).astype(BF16)
    grad_key = nn(hot_ref[...], edge_ref[...]).astype(BF16)
    grad_key_ref[...] = grad_key
    rim = head_ref.shape[0]
    rows = nt(grad_key[nodes:], w_ref[:, width : 2 * width])
    rows += nt(grad_value_ref[nodes:, :], w_ref[:, 2 * width :])
    rows = rows.astype(BF16)
    head_ref[...] = rows[:rim]
    tail_ref[...] = rows[rim:]


def query_weight_kernel(
    features_ref, left_ref, right_ref, grad_query_ref, grad_key_ref, send_ref, keep_ref, full_ref
):
    nodes, width = features_ref.shape
    rim = left_ref.shape[0]
    features = features_ref[...]
    put(full_ref, 0, tn(features, grad_query_ref[...]))
    total = tn(features, grad_key_ref[:nodes, :])
    total += tn(left_ref[...], grad_key_ref[nodes : nodes + rim, :])
    total += tn(right_ref[...], grad_key_ref[nodes + rim :, :])
    put(full_ref, width, total)
    split_halves(bit_of("member", 1), full_ref, send_ref, keep_ref)


def joined(keep, arrived, variables):
    total = keep.astype(F32) + arrived.astype(F32)
    if variables is None:
        return total
    last = total[..., -LANES:]
    lane = iota(last.shape, last.ndim - 1)
    loss = last[..., variables : variables + 1] + last[..., variables + 1 : variables + 2]
    high = loss.astype(BF16).astype(F32)
    last = jnp.where(lane == variables, high, last)
    last = jnp.where(lane == variables + 1, loss - high, last)
    return jnp.concatenate([total[..., :-LANES], last], axis=-1)


def combine_kernel(keep_in_ref, arrived_ref, send_ref, keep_ref, *, axis, bit, variables):
    mine = bit_of(axis, bit)
    for i in range(send_ref.shape[0]):
        away = 1 - mine
        send_ref[i] = joined(keep_in_ref[i, away], arrived_ref[i, away], variables).astype(BF16)
        keep_ref[i] = joined(keep_in_ref[i, mine], arrived_ref[i, mine], variables)


def merge_kernel(
    query_keep_ref, query_in_ref, value_keep_ref, value_in_ref, send_ref, keep_ref, *, axis, bit, variables
):
    mine = bit_of(axis, bit)
    start = query_keep_ref.shape[-1]
    for at, out_ref in ((1 - mine, send_ref), (mine, keep_ref)):
        for i in range(send_ref.shape[0]):
            query = joined(query_keep_ref[i, at], query_in_ref[i, at], None)
            value = joined(value_keep_ref[i, at], value_in_ref[i, at], variables)
            out_ref[i, :, :start] = query.astype(out_ref.dtype)
            out_ref[i, :, start:] = value.astype(out_ref.dtype)


def total_kernel(keep_ref, arrived_ref, sum_ref, *, variables):
    for i in range(sum_ref.shape[0]):
        sum_ref[i] = joined(keep_ref[i], arrived_ref[i], variables).astype(BF16)


def swapped(array, axis, bit):
    count = lax.axis_size(axis)
    return lax.ppermute(array, axis, [(i, i ^ bit) for i in range(count)])


class Halving:
    def __init__(self, regions, members, rows):
        self.left = [("region", 1 << b) for b in reversed(range(shift_of(regions)))]
        self.left += [("member", 1 << b) for b in reversed(range(shift_of(members)))]
        self.rows = rows

    def half(self, step, packed):
        place = self.left.index(step)
        half = (1 << place, (1 << (len(self.left) - 1 - place)) * self.rows, packed)
        return half, (half[0], 2) + half[1:]

    def run(self, send, keep, steps, variables):
        packed = send.shape[-1]
        for i, (axis, bit) in enumerate(steps):
            arrived = swapped(send, axis, bit)
            self.left.remove((axis, bit))
            if i + 1 == len(steps):
                return keep, arrived
            half, both = self.half(steps[i + 1], packed)
            send, keep = on_core(
                functools.partial(
                    combine_kernel, axis=steps[i + 1][0], bit=steps[i + 1][1], variables=variables
                ),
                [(half, BF16), (half, F32)],
                keep.reshape(both), arrived.reshape(both),
            )


def unpack_kernel(*refs, aways):
    sum_refs = refs[: len(aways)]
    qkv_ref, out_ref, dec_ref, loss_ref = refs[len(aways) :]
    width = out_ref.shape[-1]
    variables = dec_ref.shape[-1]
    place = lax.axis_index("member")
    for ref, away in zip(sum_refs, aways):
        at = place ^ away
        qkv_ref[at] = ref[:, : 3 * width].astype(F32)
        out_ref[at] = ref[:, 3 * width : 4 * width].astype(F32)
        dec_ref[at] = ref[:, 4 * width : 4 * width + variables].astype(F32)
    last = sum_refs[0][0:1, 4 * width :].astype(F32)
    loss_ref[...] = last[:, variables : variables + 1] + last[:, variables + 1 : variables + 2]


def own_feature_kernel(grad_query_ref, grad_key_ref, grad_value_ref, w_ref, grad_ref):
    nodes, width = grad_query_ref.shape
    total = nt(grad_query_ref[...], w_ref[:, :width])
    total += nt(grad_key_ref[:nodes, :], w_ref[:, width : 2 * width])
    grad_ref[...] = total + nt(grad_value_ref[:nodes, :], w_ref[:, 2 * width :])


def latent_grad_kernel(
    hidden_ref, gain_ref, own_ref, from_left_ref, from_right_ref, border_ref, node_ref, grad_ref, rows_ref
):
    nodes = hidden_ref.shape[0]
    rim = from_left_ref.shape[0]
    rows_ref[:rim] = from_left_ref[...]
    rows_ref[rim:] = from_right_ref[...]
    mask = ones_where(iota((nodes, 2 * rim), 0) == border_ref[...])
    grad_rows = own_ref[...] + nn(mask, rows_ref[...])
    scaled, inverse = norm_parts(hidden_ref[...])
    scaled_grad = grad_rows * gain_ref[...]
    back = inverse * (
        scaled_grad
        - jnp.mean(scaled_grad, axis=-1, keepdims=True)
        - scaled * jnp.mean(scaled_grad * scaled, axis=-1, keepdims=True)
    )
    grad_ref[...] = (node_ref[...] + back).astype(BF16)


def swap_rims(head, tail):
    count = lax.axis_size("region")
    from_left = lax.ppermute(tail, "region", [(i, (i + 1) % count) for i in range(count)])
    from_right = lax.ppermute(head, "region", [((i + 1) % count, i) for i in range(count)])
    return from_left, from_right


def layer(
    latent,
    node_gain,
    w_qkv,
    w_out,
    edge_bias,
    edge_source,
    boundary,
    node_count,
    decoder_projection_weight,
    dec_source,
    dec_weight,
    state,
    target,
    area,
    var_weight,
):
    hidden = latent[0]
    nodes, width = hidden.shape
    rim = boundary.shape[1] // 2
    table_rows = nodes + 2 * rim
    sources = edge_source.T
    edges = sources.shape[0]
    w_decoder = decoder_projection_weight.T
    count = node_count[None]
    columns = edge_bias.shape[1]
    variables, points = state.shape
    regions, members = lax.axis_size("region"), lax.axis_size("member")
    total_points = points * regions
    gain = node_gain[None]
    rim_rows = ((rim, width), BF16)
    rim_columns = ((variables, rim), BF16)
    features, head, tail = on_core(
        norm_kernel,
        [((nodes, width), BF16), rim_rows, rim_rows],
        hidden, gain, boundary,
        fetched=3,
        scratch=[
            pltpu.VMEM((nodes, width), BF16), pltpu.VMEM((1, width), F32), pltpu.VMEM((1, 2 * rim), jnp.int32),
        ],
        mib=4,
    )
    left, right = swap_rims(head, tail)
    queries, own_kv, mix, w_qkv = on_core(
        project_kernel,
        [
            ((nodes, width), BF16), ((nodes, 2 * width), BF16), ((table_rows, points), BF16),
            ((width, 3 * width), BF16),
        ],
        w_qkv, dec_source, dec_weight, features,
        fetched=3,
        scratch=[pltpu.VMEM(dec_source.shape, jnp.int32), pltpu.VMEM(dec_weight.shape, F32)],
    )
    edge_rows = ((edges, nodes, width), BF16)
    node_out, projected, head, tail, probs, attended, keys, values = on_core(
        attend_kernel,
        [
            ((nodes, width), BF16), ((variables, nodes), BF16), rim_columns, rim_columns,
            ((nodes, columns), F32), ((nodes, width), BF16), edge_rows, edge_rows,
        ],
        w_out, edge_bias, w_decoder, count, hidden, left, right, queries, own_kv, w_qkv, sources, boundary,
        fetched=3,
        scratch=[
            pltpu.VMEM((table_rows, 2 * width), BF16), pltpu.VMEM((width, width), BF16),
            pltpu.VMEM((nodes, columns), F32), pltpu.VMEM((variables, width), BF16),
        ],
        mib=16,
    )
    out_left, out_right = swap_rims(head, tail)
    change, sent = on_core(
        decode_kernel,
        [((variables, points), F32), ((variables, points), BF16)],
        projected, out_left, out_right, mix,
    )
    every = lax.all_gather(sent[None], "member", axis=0, tiled=True)
    grad, head, tail, loss = on_core(
        functools.partial(score_kernel, points=total_points),
        [((variables, points), BF16), rim_columns, rim_columns, ((1, LANES), F32)],
        change, every, state, target, area[None], var_weight[None], mix,
    )
    back_left, back_right = swap_rims(head, tail)
    grad_own, hot = on_core(
        own_rows_kernel,
        [((variables, nodes), F32), ((table_rows, edges * nodes), BF16)],
        mix, grad, sources,
    )
    rows = width // (regions * members)
    pieces = regions * members // 2

    def halves(packed):
        return [((pieces, rows, packed), BF16), ((pieces, rows, packed), F32)]

    def whole(packed):
        return pltpu.VMEM((pieces, 2, rows, packed), F32)

    grad_node, grad_mixed, grad_value, value_send, value_keep = on_core(
        value_back_kernel,
        [((nodes, width), F32), ((nodes, width), BF16), ((table_rows, width), BF16)]
        + halves(2 * width + LANES),
        count, grad_own, back_left, back_right, boundary, node_out, w_decoder,
        attended, w_out, probs, hot, features, left, right, loss,
        scratch=[pltpu.VMEM((edges * nodes, width), BF16), whole(2 * width + LANES)],
        mib=16,
    )
    (grad_scores,) = on_core(
        score_back_kernel, [((nodes, columns), F32)], grad_mixed, probs, values
    )
    grad_query, grad_key, head, tail = on_core(
        query_back_kernel,
        [((nodes, width), BF16), ((table_rows, width), BF16), rim_rows, rim_rows],
        grad_scores, queries, keys, hot, grad_value, w_qkv,
        scratch=[pltpu.VMEM((edges * nodes, width), BF16)],
        mib=12,
    )
    rim_left, rim_right = swap_rims(head, tail)
    query_send, query_keep = on_core(
        query_weight_kernel,
        halves(2 * width),
        features, left, right, grad_query, grad_key,
        scratch=[whole(2 * width)],
    )
    (own_feature,) = on_core(
        own_feature_kernel, [((nodes, width), F32)], grad_query, grad_key, grad_value, w_qkv
    )
    (grad_latent,) = on_core(
        latent_grad_kernel,
        [((nodes, width), BF16)],
        hidden, gain, own_feature, rim_left, rim_right, boundary, grad_node,
        scratch=[pltpu.VMEM((2 * rim, width), BF16)],
    )

    core = [("member", 1)]
    across = [("member", 1 << b) for b in range(1, shift_of(members))]
    around = [("region", 1 << b) for b in range(shift_of(regions))]
    value_sum, query_sum = Halving(regions, members, rows), Halving(regions, members, rows)
    value_keep, value_in = value_sum.run(
        value_send, value_keep, core + across + around[:2], variables
    )
    query_keep, query_in = query_sum.run(
        query_send, query_keep, core + across + around[1::-1], None
    )
    packed = 4 * width + LANES
    half, _ = value_sum.half(around[2], packed)
    _, both_values = value_sum.half(around[2], 2 * width + LANES)
    _, both_queries = value_sum.half(around[2], 2 * width)
    send, keep = on_core(
        functools.partial(merge_kernel, axis=around[2][0], bit=around[2][1], variables=variables),
        [(half, BF16), (half, F32)],
        query_keep.reshape(both_queries), query_in.reshape(both_queries),
        value_keep.reshape(both_values), value_in.reshape(both_values),
    )
    keep, arrived = value_sum.run(send, keep, around[2:], variables)
    piece = (1, rows, packed)
    (total,) = on_core(
        functools.partial(total_kernel, variables=variables), [(piece, BF16)],
        keep.reshape(piece), arrived.reshape(piece),
    )
    sums, aways = [total.reshape(rows, packed)], [0]
    for axis, bit in across[::-1] + core:
        sums = sums + [swapped(piece, axis, bit) for piece in sums]
        aways = aways + [away ^ bit for away in aways]
    share_qkv, share_out, share_dec, loss = on_core(
        functools.partial(unpack_kernel, aways=aways),
        [
            ((members, rows, 3 * width), F32), ((members, rows, width), F32),
            ((members, rows, variables), F32), ((1, 1), F32),
        ],
        *sums,
    )
    held = members * rows
    return (
        loss.reshape(()),
        share_qkv.reshape(held, 3 * width),
        share_out.reshape(held, width),
        share_dec.reshape(held, variables),
        grad_latent[None],
    )


def solution(mesh):
    placed = (
        P("member", "region", None),
        P(),
        P(),
        P(),
        P("region", None),
        P("region", None),
        P("region", None),
        P("region"),
        P(),
        P(None, "region"),
        P(None, "region"),
        P(None, "region"),
        P(None, "region"),
        P("region"),
        P(),
    )
    return jax.shard_map(
        layer,
        mesh=mesh,
        in_specs=placed,
        out_specs=(
            P(),
            P("region", None),
            P("region", None),
            P("region", None),
            P("member", "region", None),
        ),
        check_vma=False,
    )
```

time: 125 us -> 93.2 us (0.75); the launches traced: 123 us -> 92.9 us
  local copies, waits for them, and re-layouts: 19.1 us -> 0.06 us
  Pallas kernels: 33.5 us -> 23.4 us
  blocking collectives: 14.9 us -> 8.96 us
  starting transfers between devices: 25.2 us -> 28.7 us
    unnamed x68 -> x20, local copies, waits for them, and re-layouts: 17.8 us -> 0.06 us
    pallas_call x17 -> x21, Pallas kernels: 33.5 us -> 23.4 us  [on_core(): pl.pallas_call(kernel, out_shape=[jax.ShapeDtypeStruct(s, d) for s, d in...]
    all_gather x2 -> x1, blocking collectives: 14.9 us -> 8.96 us  [layer(): every = lax.all_gather(sent[None], 'member', axis=0, tiled=True)]
    ppermute x4, waiting for transfers between devices: 1.65 us -> 4.83 us  [swap_rims(): lax.ppermute(tail, 'region', [(i, (i + 1) % count) for i in range(count)])]
    ppermute x5 -> x12, waiting for transfers between devices: 27.3 us -> 24.4 us  [swapped(): return lax.ppermute(array, axis, [(i, i ^ bit) for i in range(count)])]
    ppermute x5 -> x12, starting transfers between devices: 4.97 us -> 7.14 us  [swapped(): return lax.ppermute(array, axis, [(i, i ^ bit) for i in range(count)])]
    ppermute x4, starting transfers between devices: 3.4 us -> 5.4 us  [swap_rims(): lax.ppermute(tail, 'region', [(i, (i + 1) % count) for i in range(count)])]
  transfers between devices with their start and end apart: 13 -> 20, of which waited for: 8 -> 12; matrix products, arithmetic and copies ran while one was open for 2% -> 0% of each run, Pallas kernels for 4% -> 11%
where the time goes in v2:
time: 93.2 us; the launch traced here: 92.9 us
  waiting for transfers between devices  30.3 us (33%)
  starting transfers between devices  28.7 us (31%)
  Pallas kernels  23.4 us (25%)
  blocking collectives  8.96 us (10%)
  between operations  1.52 us (2%)
    ppermute x12, waiting for transfers between devices, swapped(): return lax.ppermute(array, axis, [(i, i ^ bit) for i in range(count)])  24.4 us
    pallas_call x21, Pallas kernels, on_core(): pl.pallas_call(kernel, out_shape=[jax.ShapeDtypeStruct(s, d) for s, d in...  23.4 us
    ppermute x4, starting transfers between devices, swap_rims(): lax.ppermute(head, 'region', [((i + 1) % count, i) for i in range(count)])  16.2 us
    all_gather x1, blocking collectives, layer(): every = lax.all_gather(sent[None], 'member', axis=0, tiled=True)  8.96 us
    ppermute x12, starting transfers between devices, swapped(): return lax.ppermute(array, axis, [(i, i ^ bit) for i in range(count)])  7.14 us
    ppermute x4, starting transfers between devices, swap_rims(): lax.ppermute(tail, 'region', [(i, (i + 1) % count) for i in range(count)])  5.4 us
    ppermute x4, waiting for transfers between devices, swap_rims(): lax.ppermute(tail, 'region', [(i, (i + 1) % count) for i in range(count)])  4.83 us
  transfers between devices with their start and end apart: 20, of which 12 were waited for; matrix products, arithmetic and copies ran while one was open for 0% of the time, Pallas kernels for 11%

profile of v2, /device:TPU:0, one launch (start us, length us, event | category | flops | bytes accessed | tf_op | source)
XLA Modules:
  0.0 92.9 jit_solution(4249990660245833829)
XLA Ops:
  0.7 1.5 %shard_map.182 = (bf16[256,512]{1,0:T(8,128)(2,1)S(1)}, bf16[128,512]{1,0:T(8,128)(2,1)S(1)}, bf16[128,512]{1,0:T(8,128)(2,1)S(1)}) custom-call(bf16[256,512]{1,0:T(8,128)(2,1)} %bitcast.32, f32[1,512]{1,0:T(1,128)} %bitcast.59, s32[1,256]{1,0:T(1,128)} %border_ref.5), custom_call_target="tpu_custom_call" | custom-call | tf_op jit(solution)/shard_map/pallas_call | solution.py:34
  2.1 3.0 %collective-permute-start = (bf16[128,512]{1,0:T(8,128)(2,1)S(1)}, bf16[128,512]{1,0:T(8,128)(2,1)S(1)}, u32[]{:S(2)}, u32[]{:S(2)}) collective-permute-start(bf16[128,512]{1,0:T(8,128)(2,1)S(1)} %get-tuple-element.58), channel_id=1, source_target_pairs={{0,4},{4,8},{8,12},{12,16},{16,20},{20,24},{24,28},{28,0},{1,5},{5... | collective-permute-start | bytes 393224 | tf_op jit(solution)/shard_map/ppermute | solution.py:472
  5.2 3.1 %collective-permute-start.1 = (bf16[128,512]{1,0:T(8,128)(2,1)S(1)}, bf16[128,512]{1,0:T(8,128)(2,1)S(1)}, u32[]{:S(2)}, u32[]{:S(2)}) collective-permute-start(bf16[128,512]{1,0:T(8,128)(2,1)S(1)} %get-tuple-element.59), channel_id=1, source_target_pairs={{4,0},{8,4},{12,8},{16,12},{20,16},{24,20},{28,24},{0,28},{5,1},{9... | collective-permute-start | bytes 393224 | tf_op jit(solution)/shard_map/ppermute | solution.py:473
  9.0 2.1 %shard_map.183 = (bf16[256,512]{1,0:T(8,128)(2,1)S(1)}, bf16[256,1024]{1,0:T(8,128)(2,1)S(1)}, bf16[512,1024]{1,0:T(8,128)(2,1)S(1)}, bf16[512,1536]{1,0:T(8,128)(2,1)S(1)}) custom-call(bf16[512,1536]{1,0:T(8,128)(2,1)} %w_hbm.1, s32[3,1024]{1,0:T(4,128)} %src_hbm.1, f32[3,1024]{1,0:T(4,128)} %weight_hbm.1, bf16[256,512]{1,0:T(8,128)(2,1)S(1)} %get-tuple-element.57.features_ref), custom_call_target="tpu_custom_call" | custom-call | tf_op jit(solution)/shard_map/pallas_call | solution.py:34
  11.1 0.7 collective-permute-done.left_ref
  11.8 1.1 %collective-permute-done.1.right_ref = bf16[128,512]{1,0:T(8,128)(2,1)S(1)} collective-permute-done((bf16[128,512]{1,0:T(8,128)(2,1)S(1)}, bf16[128,512]{1,0:T(8,128)(2,1)S(1)}, u32[]{:S(2)}, u32[]{:S(2)}) %collective-permute-start.1) | collective-permute-done | bytes 131104 | tf_op jit(solution)/shard_map/ppermute | solution.py:473
  13.0 5.4 %shard_map.184 = (bf16[256,512]{1,0:T(8,128)(2,1)S(1)}, bf16[98,256]{1,0:T(8,128)(2,1)S(1)}, bf16[98,128]{1,0:T(8,128)(2,1)S(1)}, bf16[98,128]{1,0:T(8,128)(2,1)...) custom-call(bf16[512,512]{1,0:T(8,128)(2,1)} %w_out_ref.1, ...), custom_call_target="tpu_custom_call" | custom-call | tf_op jit(solution)/shard_map/pallas_call | solution.py:34
  18.4 0.3 collective-permute-start.2
  18.7 4.4 %collective-permute-start.3 = (bf16[98,128]{1,0:T(8,128)(2,1)S(1)}, bf16[98,128]{1,0:T(8,128)(2,1)S(1)}, u32[]{:S(2)}, u32[]{:S(2)}) collective-permute-start(bf16[98,128]{1,0:T(8,128)(2,1)S(1)} %get-tuple-element.66), channel_id=1, source_target_pairs={{4,0},{8,4},{12,8},{16,12},{20,16},{24,20},{28,24},{0,28},{5,1},{9... | collective-permute-start | bytes 75272 | tf_op jit(solution)/shard_map/ppermute | solution.py:473
  23.2 1.8 %collective-permute-done.2.left_ref = bf16[98,128]{1,0:T(8,128)(2,1)S(1)} collective-permute-done((bf16[98,128]{1,0:T(8,128)(2,1)S(1)}, bf16[98,128]{1,0:T(8,128)(2,1)S(1)}, u32[]{:S(2)}, u32[]{:S(2)}) %collective-permute-start.2) | collective-permute-done | bytes 25120 | tf_op jit(solution)/shard_map/ppermute | solution.py:472
  25.0 0.3 shard_map.185
  25.3 9.0 %all-gather.1.every_ref = bf16[4,98,1024]{2,1,0:T(8,128)(2,1)S(1)} all-gather(bf16[1,98,1024]{2,1,0:T(8,128)(2,1)S(1)} %bitcast.50), channel_id=2, replica_groups=mesh['region'=8,'member'=4] {'member'}, dimensions={0}, use_global_device_ids=true | all-gather | bytes 1003520 | tf_op jit(solution)/shard_map/all_gather | solution.py:551
  34.3 1.1 %shard_map.186 = (bf16[98,1024]{1,0:T(8,128)(2,1)S(1)}, bf16[98,128]{1,0:T(8,128)(2,1)S(1)}, bf16[98,128]{1,0:T(8,128)(2,1)S(1)}, f32[1,128]{1,0:T(1,128)S(1)}) custom-call(f32[98,1024]{1,0:T(8,128)S(1)} %get-tuple-element.67.change_ref, bf16[4,98,1024]{2,1,0:T(8,128)(2,1)S(1)} %all-gather.1.every_ref, f32[98,1024]{1,0:T(8,128)S(1)} %copy-done.2, ...), custom_call_target="tpu_custom_call" | custom-call | tf_op jit(solution)/shard_map/pallas_call | solution.py:34
  35.4 0.9 %collective-permute-start.4 = (bf16[98,128]{1,0:T(8,128)(2,1)S(1)}, bf16[98,128]{1,0:T(8,128)(2,1)S(1)}, u32[]{:S(2)}, u32[]{:S(2)}) collective-permute-start(bf16[98,128]{1,0:T(8,128)(2,1)S(1)} %get-tuple-element.71), channel_id=1, source_target_pairs={{0,4},{4,8},{8,12},{12,16},{16,20},{20,24},{24,28},{28,0},{1,5},{5... | collective-permute-start | bytes 75272 | tf_op jit(solution)/shard_map/ppermute | solution.py:472
  36.3 4.1 %collective-permute-start.5 = (bf16[98,128]{1,0:T(8,128)(2,1)S(1)}, bf16[98,128]{1,0:T(8,128)(2,1)S(1)}, u32[]{:S(2)}, u32[]{:S(2)}) collective-permute-start(bf16[98,128]{1,0:T(8,128)(2,1)S(1)} %get-tuple-element.72), channel_id=1, source_target_pairs={{4,0},{8,4},{12,8},{16,12},{20,16},{24,20},{28,24},{0,28},{5,1},{9... | collective-permute-start | bytes 75272 | tf_op jit(solution)/shard_map/ppermute | solution.py:473
  40.4 1.1 %shard_map.187 = (f32[98,256]{1,0:T(8,128)S(1)}, bf16[512,2048]{1,0:T(8,128)(2,1)S(1)}) custom-call(bf16[512,1024]{1,0:T(8,128)(2,1)S(1)} %get-tuple-element.60.mix_ref, bf16[98,1024]{1,0:T(8,128)(2,1)S(1)} %get-tuple-element.69.grad_ref, s32[8,256]{1,0:T(8,128)S(1)} %bitcast.58), custom_call_target="tpu_custom_call" | custom-call | tf_op jit(solution)/shard_map/pallas_call | solution.py:34
  41.5 0.5 collective-permute-done.4.from_left_ref
  42.0 3.5 %shard_map.188 = (f32[256,512]{1,0:T(8,128)S(1)}, bf16[256,512]{1,0:T(8,128)(2,1)S(1)}, bf16[512,512]{1,0:T(8,128)(2,1)S(1)}, bf16[16,16,1152]{2,1,0:T(8,128)(2,1)S(1)}, f32[16,16,1152]{2,1,0:T(8,128)S(1)}) custom-call(s32[1,1]{1,0:T(1,128)} %bitcast.31.count_ref, f32[98,256]{1,0:T(8,128)S(1)} %get-tuple-element.70.own_ref, ...), custom_call_target="tpu_custom_call" | custom-call | tf_op jit(solution)/shard_map/pallas_call | solution.py:34
  45.6 1.0 %shard_map.189.grad_scores_ref = f32[256,128]{1,0:T(8,128)S(1)} custom-call(bf16[256,512]{1,0:T(8,128)(2,1)S(1)} %get-tuple-element.78.mixed_ref, f32[256,128]{1,0:T(8,128)S(1)} %get-tuple-element.75.probs_ref, bf16[8,256,512]{2,1,0:T(8,128)(2,1)S(1)} %get-tuple-element.79.values_ref), custom_call_target="tpu_custom_call" | custom-call | tf_op jit(solution)/shard_map/pallas_call | solution.py:34
  46.6 2.5 %shard_map.190 = (bf16[256,512]{1,0:T(8,128)(2,1)S(1)}, bf16[512,512]{1,0:T(8,128)(2,1)S(1)}, bf16[128,512]{1,0:T(8,128)(2,1)S(1)}, bf16[128,512]{1,0:T(8,128)(2,1)S(1)}) custom-call(f32[256,128]{1,0:T(8,128)S(1)} %shard_map.189.grad_scores_ref, bf16[256,512]{1,0:T(8,128)(2,1)S(1)} %get-tuple-element.61.q_ref, ...), custom_call_target="tpu_custom_call" | custom-call | tf_op jit(solution)/shard_map/pallas_call | solution.py:34
  49.1 1.0 %shard_map.191 = (bf16[16,16,1024]{2,1,0:T(8,128)(2,1)S(1)}, f32[16,16,1024]{2,1,0:T(8,128)S(1)}) custom-call(bf16[256,512]{1,0:T(8,128)(2,1)S(1)} %get-tuple-element.57.features_ref, bf16[128,512]{1,0:T(8,128)(2,1)S(1)} %collective-permute-done.left_ref, bf16[128,512]{1,0:T(8,128)(2,1)S(1)} %collective-permute-done.1.right_ref, ...), custom_call_target="tpu_custom_call" | custom-call | tf_op jit(solution)/shard_map/pallas_call | solution.py:34
  50.2 0.5 collective-permute-start.6
  50.7 0.3 shard_map.195
  51.0 0.6 collective-permute-start.11
  51.6 0.7 collective-permute-done.6
  52.3 0.1 shard_map.192
  52.3 0.9 collective-permute-start.7
  53.2 7.7 %collective-permute-done.11 = bf16[8,16,1152]{2,1,0:T(8,128)(2,1)S(1)} collective-permute-done((bf16[8,16,1152]{2,1,0:T(8,128)(2,1)S(1)}, bf16[8,16,1152]{2,1,0:T(8,128)(2,1)S(1)}, u32[]{:S(2)}, u32[]{:S(2)}) %collective-permute-start.11) | collective-permute-done | bytes 294944 | tf_op jit(solution)/shard_map/ppermute | solution.py:398
  60.9 0.2 shard_map.196
  61.3 4.4 %collective-permute-done.7 = bf16[8,16,1024]{2,1,0:T(8,128)(2,1)S(1)} collective-permute-done((bf16[8,16,1024]{2,1,0:T(8,128)(2,1)S(1)}, bf16[8,16,1024]{2,1,0:T(8,128)(2,1)S(1)}, u32[]{:S(2)}, u32[]{:S(2)}) %collective-permute-start.7) | collective-permute-done | bytes 262176 | tf_op jit(solution)/shard_map/ppermute | solution.py:398
  65.7 0.1 collective-permute-start.8
  65.8 0.6 collective-permute-done.12
  66.4 0.2 shard_map.197
  66.6 1.5 %collective-permute-start.13 = (bf16[2,16,1152]{2,1,0:T(8,128)(2,1)S(1)}, bf16[2,16,1152]{2,1,0:T(8,128)(2,1)S(1)}, u32[]{:S(2)}, u32[]{:S(2)}) collective-permute-start(bf16[2,16,1152]{2,1,0:T(8,128)(2,1)S(1)} %get-tuple-element.99), channel_id=1, source_target_pairs={{0,8},{4,12},{8,0},{12,4},{16,24},{20,28},{24,16},{28,20},{1,9},{5... | collective-permute-start | bytes 221192 | tf_op jit(solution)/shard_map/ppermute | solution.py:398
  68.0 3.1 %collective-permute-done.8 = bf16[2,32,1024]{2,1,0:T(8,128)(2,1)S(1)} collective-permute-done((bf16[2,32,1024]{2,1,0:T(8,128)(2,1)S(1)}, bf16[2,32,1024]{2,1,0:T(8,128)(2,1)S(1)}, u32[]{:S(2)}, u32[]{:S(2)}) %collective-permute-start.8) | collective-permute-done | bytes 131104 | tf_op jit(solution)/shard_map/ppermute | solution.py:398
  71.2 4.3 %collective-permute-done.9 = bf16[2,16,1024]{2,1,0:T(8,128)(2,1)S(1)} collective-permute-done((bf16[2,16,1024]{2,1,0:T(8,128)(2,1)S(1)}, bf16[2,16,1024]{2,1,0:T(8,128)(2,1)S(1)}, u32[]{:S(2)}, u32[]{:S(2)}) %collective-permute-start.9) | collective-permute-done | bytes 65568 | tf_op jit(solution)/shard_map/ppermute | solution.py:398
  75.5 0.2 shard_map.198
  75.7 2.4 %collective-permute-start.14 = (bf16[1,16,2176]{2,1,0:T(8,128)(2,1)S(1)}, bf16[1,16,2176]{2,1,0:T(8,128)(2,1)S(1)}, u32[]{:S(2)}, u32[]{:S(2)}) collective-permute-start(bf16[1,16,2176]{2,1,0:T(8,128)(2,1)S(1)} %get-tuple-element.101), channel_id=1, source_target_pairs={{0,16},{4,20},{8,24},{12,28},{16,0},{20,4},{24,8},{28,12},{1,17},{... | collective-permute-start | bytes 208904 | tf_op jit(solution)/shard_map/ppermute | solution.py:398
  78.1 3.6 %collective-permute-done.14.arrived_ref = bf16[1,16,2176]{2,1,0:T(8,128)(2,1)S(1)} collective-permute-done((bf16[1,16,2176]{2,1,0:T(8,128)(2,1)S(1)}, bf16[1,16,2176]{2,1,0:T(8,128)(2,1)S(1)}, u32[]{:S(2)}, u32[]{:S(2)}) %collective-permute-start.14) | collective-permute-done | bytes 69664 | tf_op jit(solution)/shard_map/ppermute | solution.py:398
  81.7 0.2 shard_map.199
  81.9 0.4 collective-permute-start.15
  82.3 1.1 %collective-permute-start.18 = (bf16[128,512]{1,0:T(8,128)(2,1)S(1)}, bf16[128,512]{1,0:T(8,128)(2,1)S(1)}, u32[]{:S(2)}, u32[]{:S(2)}) collective-permute-start(bf16[128,512]{1,0:T(8,128)(2,1)S(1)} %get-tuple-element.106), channel_id=1, source_target_pairs={{0,4},{4,8},{8,12},{12,16},{16,20},{20,24},{24,28},{28,0},{1,5},{5... | collective-permute-start | bytes 393224 | tf_op jit(solution)/shard_map/ppermute | solution.py:472
  83.4 4.6 %collective-permute-start.19 = (bf16[128,512]{1,0:T(8,128)(2,1)S(1)}, bf16[128,512]{1,0:T(8,128)(2,1)S(1)}, u32[]{:S(2)}, u32[]{:S(2)}) collective-permute-start(bf16[128,512]{1,0:T(8,128)(2,1)S(1)} %get-tuple-element.107), channel_id=1, source_target_pairs={{4,0},{8,4},{12,8},{16,12},{20,16},{24,20},{28,24},{0,28},{5,1},{9... | collective-permute-start | bytes 393224 | tf_op jit(solution)/shard_map/ppermute | solution.py:473
  87.9 0.5 collective-permute-start.17
  88.4 0.6 shard_map.201.own_ref
  89.0 1.8 %collective-permute-done.18.from_left_ref = bf16[128,512]{1,0:T(8,128)(2,1)S(1)} collective-permute-done((bf16[128,512]{1,0:T(8,128)(2,1)S(1)}, bf16[128,512]{1,0:T(8,128)(2,1)S(1)}, u32[]{:S(2)}, u32[]{:S(2)}) %collective-permute-start.18) | collective-permute-done | bytes 131104 | tf_op jit(solution)/shard_map/ppermute | solution.py:472
  90.9 1.2 %shard_map.202 = bf16[256,512]{1,0:T(8,128)(2,1)} custom-call(bf16[256,512]{1,0:T(8,128)(2,1)S(1)} %bitcast.34, f32[1,512]{1,0:T(1,128)S(1)} %bitcast.60, f32[256,512]{1,0:T(8,128)S(1)} %shard_map.201.own_ref, bf16[128,512]{1,0:T(8,128)(2,1)S(1)} %collective-permute-done.18.from_left_ref, bf16[128,512]{1,0:T(8,128)(2,1)S(1)} %collective-permute-done.19.from_right_ref, ...), custom_call_target="tpu_custom_call" | custom-call | tf_op jit(solution)/shard_map/pallas_call | solution.py:34
  92.0 0.9 shard_map.200
  (34 shorter events, 0.4 us)
Async XLA Ops:
  0.6 12.3 %copy-start.6 = (s32[1,256]{1,0:T(1,128)S(1)}, s32[1,256]{1,0:T(1,128)}, u32[]{:S(2)}) copy-start(s32[1,256]{1,0:T(1,128)} %border_ref.5) | copy-start | bytes 3076
  0.6 12.3 %copy-start = (bf16[1,256,512]{2,1,0:T(8,128)(2,1)S(1)}, bf16[1,256,512]{2,1,0:T(8,128)(2,1)}, u32[]{:S(2)}) copy-start(bf16[1,256,512]{2,1,0:T(8,128)(2,1)} %param.15) | copy-start | bytes 786436
  0.7 12.3 %copy-start.5 = (s32[256,8]{0,1:T(8,128)S(1)}, s32[256,8]{0,1:T(8,128)}, u32[]{:S(2)}) copy-start(s32[256,8]{0,1:T(8,128)} %param.20) | copy-start | bytes 24580
  2.1 9.7 %collective-permute-start = (bf16[128,512]{1,0:T(8,128)(2,1)S(1)}, bf16[128,512]{1,0:T(8,128)(2,1)S(1)}, u32[]{:S(2)}, u32[]{:S(2)}) collective-permute-start(bf16[128,512]{1,0:T(8,128)(2,1)S(1)} %get-tuple-element.58), channel_id=1, source_target_pairs={{0,4},{4,8},{8,12},{12,16},{16,20},{20,24},{24,28},{28,0},{1,5},{5... | collective-permute-start | bytes 393224 | tf_op jit(solution)/shard_map/ppermute | solution.py:472
  5.2 7.8 %collective-permute-start.1 = (bf16[128,512]{1,0:T(8,128)(2,1)S(1)}, bf16[128,512]{1,0:T(8,128)(2,1)S(1)}, u32[]{:S(2)}, u32[]{:S(2)}) collective-permute-start(bf16[128,512]{1,0:T(8,128)(2,1)S(1)} %get-tuple-element.59), channel_id=1, source_target_pairs={{4,0},{8,4},{12,8},{16,12},{20,16},{24,20},{28,24},{0,28},{5,1},{9... | collective-permute-start | bytes 393224 | tf_op jit(solution)/shard_map/ppermute | solution.py:473
  13.0 21.3 %copy-start.2 = (f32[98,1024]{1,0:T(8,128)S(1)}, f32[98,1024]{1,0:T(8,128)}, u32[]{:S(2)}) copy-start(f32[98,1024]{1,0:T(8,128)} %state_ref.1) | copy-start | bytes 1204228
  13.0 21.3 %copy-start.3 = (f32[98,1024]{1,0:T(8,128)S(1)}, f32[98,1024]{1,0:T(8,128)}, u32[]{:S(2)}) copy-start(f32[98,1024]{1,0:T(8,128)} %target_ref.1) | copy-start | bytes 1204228
  13.0 21.3 %copy-start.8 = (f32[1024]{0:T(1024)S(1)}, f32[1024]{0:T(1024)}, u32[]{:S(2)}) copy-start(f32[1024]{0:T(1024)} %param.28) | copy-start | bytes 12292
  13.0 21.3 %copy-start.9 = (f32[98]{0:T(128)S(1)}, f32[98]{0:T(128)}, u32[]{:S(2)}) copy-start(f32[98]{0:T(128)} %param.29) | copy-start | bytes 1180
  18.4 6.6 %collective-permute-start.2 = (bf16[98,128]{1,0:T(8,128)(2,1)S(1)}, bf16[98,128]{1,0:T(8,128)(2,1)S(1)}, u32[]{:S(2)}, u32[]{:S(2)}) collective-permute-start(bf16[98,128]{1,0:T(8,128)(2,1)S(1)} %get-tuple-element.65), channel_id=1, source_target_pairs={{0,4},{4,8},{8,12},{12,16},{16,20},{20,24},{24,28},{28,0},{1,5},{5... | collective-permute-start | bytes 75272 | tf_op jit(solution)/shard_map/ppermute | solution.py:472
  18.7 6.3 %collective-permute-start.3 = (bf16[98,128]{1,0:T(8,128)(2,1)S(1)}, bf16[98,128]{1,0:T(8,128)(2,1)S(1)}, u32[]{:S(2)}, u32[]{:S(2)}) collective-permute-start(bf16[98,128]{1,0:T(8,128)(2,1)S(1)} %get-tuple-element.66), channel_id=1, source_target_pairs={{4,0},{8,4},{12,8},{16,12},{20,16},{24,20},{28,24},{0,28},{5,1},{9... | collective-permute-start | bytes 75272 | tf_op jit(solution)/shard_map/ppermute | solution.py:473
  34.3 7.7 %copy-start.1 = (bf16[512,512]{1,0:T(8,128)(2,1)S(1)}, bf16[512,512]{1,0:T(8,128)(2,1)}, u32[]{:S(2)}) copy-start(bf16[512,512]{1,0:T(8,128)(2,1)} %w_out_ref.1) | copy-start | bytes 1572868
  34.3 7.7 %copy-start.4 = (bf16[512,98]{0,1:T(8,128)(2,1)S(1)}, bf16[512,98]{0,1:T(8,128)(2,1)}, u32[]{:S(2)}) copy-start(bf16[512,98]{0,1:T(8,128)(2,1)} %param.23) | copy-start | bytes 301060
  35.4 6.6 %collective-permute-start.4 = (bf16[98,128]{1,0:T(8,128)(2,1)S(1)}, bf16[98,128]{1,0:T(8,128)(2,1)S(1)}, u32[]{:S(2)}, u32[]{:S(2)}) collective-permute-start(bf16[98,128]{1,0:T(8,128)(2,1)S(1)} %get-tuple-element.71), channel_id=1, source_target_pairs={{0,4},{4,8},{8,12},{12,16},{16,20},{20,24},{24,28},{28,0},{1,5},{5... | collective-permute-start | bytes 75272 | tf_op jit(solution)/shard_map/ppermute | solution.py:472
  36.3 5.7 %collective-permute-start.5 = (bf16[98,128]{1,0:T(8,128)(2,1)S(1)}, bf16[98,128]{1,0:T(8,128)(2,1)S(1)}, u32[]{:S(2)}, u32[]{:S(2)}) collective-permute-start(bf16[98,128]{1,0:T(8,128)(2,1)S(1)} %get-tuple-element.72), channel_id=1, source_target_pairs={{4,0},{8,4},{12,8},{16,12},{20,16},{24,20},{28,24},{0,28},{5,1},{9... | collective-permute-start | bytes 75272 | tf_op jit(solution)/shard_map/ppermute | solution.py:473
  45.5 5.2 %collective-permute-start.10 = (bf16[16,16,1152]{2,1,0:T(8,128)(2,1)S(1)}, bf16[16,16,1152]{2,1,0:T(8,128)(2,1)S(1)}, u32[]{:S(2)}, u32[]{:S(2)}) collective-permute-start(bf16[16,16,1152]{2,1,0:T(8,128)(2,1)S(1)} %get-tuple-element.93), channel_id=1, source_target_pairs={{0,1},{1,0},{2,3},{3,2},{4,5},{5,4},{6,7},{7,6},{8,9},{9,8},{10,11... | collective-permute-start | bytes 1769480 | tf_op jit(solution)/shard_map/ppermute | solution.py:398
  50.2 2.1 %collective-permute-start.6 = (bf16[16,16,1024]{2,1,0:T(8,128)(2,1)S(1)}, bf16[16,16,1024]{2,1,0:T(8,128)(2,1)S(1)}, u32[]{:S(2)}, u32[]{:S(2)}) collective-permute-start(bf16[16,16,1024]{2,1,0:T(8,128)(2,1)S(1)} %get-tuple-element.85), channel_id=1, source_target_pairs={{0,1},{1,0},{2,3},{3,2},{4,5},{5,4},{6,7},{7,6},{8,9},{9,8},{10,11... | collective-permute-start | bytes 1572872 | tf_op jit(solution)/shard_map/ppermute | solution.py:398
  51.0 9.9 %collective-permute-start.11 = (bf16[8,16,1152]{2,1,0:T(8,128)(2,1)S(1)}, bf16[8,16,1152]{2,1,0:T(8,128)(2,1)S(1)}, u32[]{:S(2)}, u32[]{:S(2)}) collective-permute-start(bf16[8,16,1152]{2,1,0:T(8,128)(2,1)S(1)} %get-tuple-element.95), channel_id=1, source_target_pairs={{0,2},{1,3},{2,0},{3,1},{4,6},{5,7},{6,4},{7,5},{8,10},{9,11},{10,... | collective-permute-start | bytes 884744 | tf_op jit(solution)/shard_map/ppermute | solution.py:398
  52.3 13.3 %collective-permute-start.7 = (bf16[8,16,1024]{2,1,0:T(8,128)(2,1)S(1)}, bf16[8,16,1024]{2,1,0:T(8,128)(2,1)S(1)}, u32[]{:S(2)}, u32[]{:S(2)}) collective-permute-start(bf16[8,16,1024]{2,1,0:T(8,128)(2,1)S(1)} %get-tuple-element.87), channel_id=1, source_target_pairs={{0,2},{1,3},{2,0},{3,1},{4,6},{5,7},{6,4},{7,5},{8,10},{9,11},{10,... | collective-permute-start | bytes 786440 | tf_op jit(solution)/shard_map/ppermute | solution.py:398
  61.2 5.2 %collective-permute-start.12 = (bf16[4,16,1152]{2,1,0:T(8,128)(2,1)S(1)}, bf16[4,16,1152]{2,1,0:T(8,128)(2,1)S(1)}, u32[]{:S(2)}, u32[]{:S(2)}) collective-permute-start(bf16[4,16,1152]{2,1,0:T(8,128)(2,1)S(1)} %get-tuple-element.97), channel_id=1, source_target_pairs={{0,4},{4,0},{8,12},{12,8},{16,20},{20,16},{24,28},{28,24},{1,5},{5... | collective-permute-start | bytes 442376 | tf_op jit(solution)/shard_map/ppermute | solution.py:398
  65.7 5.4 %collective-permute-start.8 = (bf16[2,32,1024]{2,1,0:T(8,128)(2,1)S(1)}, bf16[2,32,1024]{2,1,0:T(8,128)(2,1)S(1)}, u32[]{:S(2)}, u32[]{:S(2)}) collective-permute-start(bf16[2,32,1024]{2,1,0:T(8,128)(2,1)S(1)} %get-tuple-element.89), channel_id=1, source_target_pairs={{0,8},{4,12},{8,0},{12,4},{16,24},{20,28},{24,16},{28,20},{1,9},{5... | collective-permute-start | bytes 393224 | tf_op jit(solution)/shard_map/ppermute | solution.py:398
  66.6 8.9 %collective-permute-start.13 = (bf16[2,16,1152]{2,1,0:T(8,128)(2,1)S(1)}, bf16[2,16,1152]{2,1,0:T(8,128)(2,1)S(1)}, u32[]{:S(2)}, u32[]{:S(2)}) collective-permute-start(bf16[2,16,1152]{2,1,0:T(8,128)(2,1)S(1)} %get-tuple-element.99), channel_id=1, source_target_pairs={{0,8},{4,12},{8,0},{12,4},{16,24},{20,28},{24,16},{28,20},{1,9},{5... | collective-permute-start | bytes 221192 | tf_op jit(solution)/shard_map/ppermute | solution.py:398
  71.1 19.7 %copy-start.7 = (f32[512]{0:T(512)S(1)}, f32[512]{0:T(512)}, u32[]{:S(2)}) copy-start(f32[512]{0:T(512)} %param.16) | copy-start | bytes 6148
  71.2 4.3 %collective-permute-start.9 = (bf16[2,16,1024]{2,1,0:T(8,128)(2,1)S(1)}, bf16[2,16,1024]{2,1,0:T(8,128)(2,1)S(1)}, u32[]{:S(2)}, u32[]{:S(2)}) collective-permute-start(bf16[2,16,1024]{2,1,0:T(8,128)(2,1)S(1)} %get-tuple-element.91), channel_id=1, source_target_pairs={{0,4},{4,0},{8,12},{12,8},{16,20},{20,16},{24,28},{28,24},{1,5},{5... | collective-permute-start | bytes 196616 | tf_op jit(solution)/shard_map/ppermute | solution.py:398
  75.7 6.1 %collective-permute-start.14 = (bf16[1,16,2176]{2,1,0:T(8,128)(2,1)S(1)}, bf16[1,16,2176]{2,1,0:T(8,128)(2,1)S(1)}, u32[]{:S(2)}, u32[]{:S(2)}) collective-permute-start(bf16[1,16,2176]{2,1,0:T(8,128)(2,1)S(1)} %get-tuple-element.101), channel_id=1, source_target_pairs={{0,16},{4,20},{8,24},{12,28},{16,0},{20,4},{24,8},{28,12},{1,17},{... | collective-permute-start | bytes 208904 | tf_op jit(solution)/shard_map/ppermute | solution.py:398
  81.9 6.0 %collective-permute-start.15 = (bf16[16,2176]{1,0:T(8,128)(2,1)S(1)}, bf16[16,2176]{1,0:T(8,128)(2,1)S(1)}, u32[]{:S(2)}, u32[]{:S(2)}) collective-permute-start(bf16[16,2176]{1,0:T(8,128)(2,1)S(1)} %bitcast.45), channel_id=1, source_target_pairs={{0,2},{1,3},{2,0},{3,1},{4,6},{5,7},{6,4},{7,5},{8,10},{9,11},{10,... | collective-permute-start | bytes 208904 | tf_op jit(solution)/shard_map/ppermute | solution.py:398
  82.3 8.6 %collective-permute-start.18 = (bf16[128,512]{1,0:T(8,128)(2,1)S(1)}, bf16[128,512]{1,0:T(8,128)(2,1)S(1)}, u32[]{:S(2)}, u32[]{:S(2)}) collective-permute-start(bf16[128,512]{1,0:T(8,128)(2,1)S(1)} %get-tuple-element.106), channel_id=1, source_target_pairs={{0,4},{4,8},{8,12},{12,16},{16,20},{20,24},{24,28},{28,0},{1,5},{5... | collective-permute-start | bytes 393224 | tf_op jit(solution)/shard_map/ppermute | solution.py:472
  83.4 7.5 %collective-permute-start.19 = (bf16[128,512]{1,0:T(8,128)(2,1)S(1)}, bf16[128,512]{1,0:T(8,128)(2,1)S(1)}, u32[]{:S(2)}, u32[]{:S(2)}) collective-permute-start(bf16[128,512]{1,0:T(8,128)(2,1)S(1)} %get-tuple-element.107), channel_id=1, source_target_pairs={{4,0},{8,4},{12,8},{16,12},{20,16},{24,20},{28,24},{0,28},{5,1},{9... | collective-permute-start | bytes 393224 | tf_op jit(solution)/shard_map/ppermute | solution.py:473
  87.9 4.1 %collective-permute-start.16 = (bf16[16,2176]{1,0:T(8,128)(2,1)S(1)}, bf16[16,2176]{1,0:T(8,128)(2,1)S(1)}, u32[]{:S(2)}, u32[]{:S(2)}) collective-permute-start(bf16[16,2176]{1,0:T(8,128)(2,1)S(1)} %bitcast.46), channel_id=1, source_target_pairs={{0,1},{1,0},{2,3},{3,2},{4,5},{5,4},{6,7},{7,6},{8,9},{9,8},{10,11... | collective-permute-start | bytes 208904 | tf_op jit(solution)/shard_map/ppermute | solution.py:398
  87.9 4.1 %collective-permute-start.17 = (bf16[16,2176]{1,0:T(8,128)(2,1)S(1)}, bf16[16,2176]{1,0:T(8,128)(2,1)S(1)}, u32[]{:S(2)}, u32[]{:S(2)}) collective-permute-start(bf16[16,2176]{1,0:T(8,128)(2,1)S(1)} %collective-permute-done.15.refs_1_), channel_id=1, source_target_pairs={{0,1},{1,0},{2,3},{3,2},{4,5},{5,4},{6,7},{7,6},{8,9},{9,8},{10,11... | collective-permute-start | bytes 208904 | tf_op jit(solution)/shard_map/ppermute | solution.py:398

commit v3 on v2

--- a/solution.py
+++ b/solution.py
@@ -184,32 +184,34 @@
     tail_ref[...] = columns[:, rim:]
 
 
-def decode_kernel(own_ref, left_ref, right_ref, mix_ref, change_ref, sent_ref):
-    table = jnp.concatenate([own_ref[...], left_ref[...], right_ref[...]], axis=1)
-    change = nn(table, mix_ref[...])
-    change_ref[...] = change
-    sent_ref[...] = change.astype(BF16)
+def join_kernel(left_ref, right_ref, rims_ref):
+    rim = left_ref.shape[1]
+    rims_ref[:, :rim] = left_ref[...]
+    rims_ref[:, rim:] = right_ref[...]
 
 
 def smooth_root(values):
     return values * values + SMOOTH_SQ
 
 
-def score_kernel(
-    change_ref, every_ref, state_ref, target_ref, area_ref, var_ref, mix_ref,
-    grad_ref, head_ref, tail_ref, loss_ref, *, points,
-):
-    members = every_ref.shape[0]
+def score_kernel(state_ref, target_ref, area_ref, var_ref, mix_ref, *refs, points):
+    grad_ref, head_ref, tail_ref, loss_ref = refs[-4:]
+    table_refs = refs[:-4]
+    members = len(table_refs) // 2
     fair = 1.0 - (1.0 - ALPHA) / members
     pair = fair / (2.0 * members * (members - 1))
-    own = change_ref[...]
+    mix = mix_ref[...]
+    nodes = table_refs[0].shape[1]
+
+    def change(n):
+        return nn(table_refs[n][...], mix[:nodes]) + nn(table_refs[members + n][...], mix[nodes:])
+
+    own = change(0)
     variables = own.shape[0]
     spread = jnp.zeros_like(own)
     slope = jnp.zeros_like(own)
-    me = lax.axis_index("member")
     for n in range(members):
-        other = jnp.where(me == n, own, every_ref[n].astype(F32))
-        gap = own - other
+        gap = own - (change(n) if n else own)
         square = smooth_root(gap)
         inverse = lax.rsqrt(square)
         spread += square * inverse - SMOOTH_ROOT
@@ -240,6 +242,10 @@
         hot_ref[:, e * nodes : (e + 1) * nodes] = ones_where(slot == src_ref[e : e + 1, :])
 
 
+def padded(variables):
+    return -(-variables // 8) * 8
+
+
 def split_halves(mine, source_ref, send_ref, keep_ref):
     for i in range(send_ref.shape[0]):
         send_ref[i] = source_ref[i, 1 - mine].astype(BF16)
@@ -262,9 +268,10 @@
     edges = hot_ref.shape[1] // nodes
     head_size = width // (columns // edges)
     returned = jnp.concatenate([from_left_ref[...], from_right_ref[...]], axis=1)
-    columns_grad = (own_ref[...] + nt(returned, border_map(border_ref, nodes))).astype(BF16)
+    columns_grad = own_ref[...] + nt(returned, border_map(border_ref, nodes))
+    live = iota(columns_grad.shape, 1) < count_ref[...]
+    columns_grad = jnp.where(live, columns_grad, 0.0).astype(BF16)
     total = tn(columns_grad, w_dec_ref[...])
-    total = jnp.where(iota((nodes, width), 0) < count_ref[...], total, 0.0)
     grad_ref[...] = total
     rounded = total.astype(BF16)
     mixed = nt(rounded, w_out_ref[...]).astype(BF16)
@@ -283,24 +290,28 @@
     total += tn(left_ref[...], grad_value[nodes : nodes + rim])
     total += tn(right_ref[...], grad_value[nodes + rim :])
     put(full_ref, 0, total)
-    put(full_ref, width, tn(attended_ref[...], rounded))
     variables = columns_grad.shape[0]
-    dec = nn(columns_grad, node_out_ref[...])
-    pad = jnp.concatenate([dec, jnp.zeros((LANES - variables, width), F32)], axis=0).T
-    loss = jnp.broadcast_to(loss_ref[0:1, 0:1], (width, LANES))
+    step = padded(variables)
+    columns_grad = jnp.concatenate(
+        [columns_grad.astype(F32), jnp.zeros((step - variables, nodes), F32)], axis=0
+    ).astype(BF16)
+    loss = jnp.broadcast_to(loss_ref[0:1, 0:1], (2 * LANES - 2 * step, width))
     high = loss.astype(BF16).astype(F32)
-    lane = iota((width, LANES), 1)
-    pad = jnp.where(lane == variables, high, pad)
-    pad = jnp.where(lane == variables + 1, loss - high, pad)
-    put(full_ref, 2 * width, pad)
+    row = iota(loss.shape, 0)
+    loss = jnp.where(row == 0, high, jnp.where(row == 1, loss - high, 0.0))
+    few = [nn(columns_grad, attended_ref[...]), nn(columns_grad, node_out_ref[...]), loss]
+    put(full_ref, width, jnp.concatenate(few, axis=0).T)
     split_halves(bit_of("member", 1), full_ref, send_ref, keep_ref)
 
 
-def score_back_kernel(mixed_ref, probs_ref, values_ref, grad_ref):
+def score_back_kernel(mixed_ref, probs_ref, values_ref, q_ref, keys_ref, grad_query_ref, edge_ref):
     nodes, width = mixed_ref.shape
     edges = values_ref.shape[0]
     columns = probs_ref.shape[1]
-    squeeze = head_map(width, columns, width // (columns // edges), edges)
+    head_size = width // (columns // edges)
+    inv_root = 1.0 / math.sqrt(head_size)
+    squeeze = head_map(width, columns, head_size, edges)
+    expand = head_map(columns, width, edges, head_size)
     lane = iota((nodes, columns), 1) & (edges - 1)
     mixed = mixed_ref[...].astype(F32)
     probs = probs_ref[...]
@@ -308,21 +319,7 @@
     for e in range(edges):
         part = nn((mixed * values_ref[e].astype(F32)).astype(BF16), squeeze)
         grad_probs = jnp.where(lane == e, part, grad_probs)
-    grad_ref[...] = probs * (grad_probs - group_reduce(probs * grad_probs, edges, jnp.add))
-
-
-def query_back_kernel(
-    grad_scores_ref, q_ref, keys_ref, hot_ref, grad_value_ref, w_ref,
-    grad_query_ref, grad_key_ref, head_ref, tail_ref, edge_ref,
-):
-    nodes, width = q_ref.shape
-    edges = keys_ref.shape[0]
-    columns = grad_scores_ref.shape[1]
-    head_size = width // (columns // edges)
-    inv_root = 1.0 / math.sqrt(head_size)
-    expand = head_map(columns, width, edges, head_size)
-    lane = iota((nodes, columns), 1) & (edges - 1)
-    grad_scores = grad_scores_ref[...]
+    grad_scores = probs * (grad_probs - group_reduce(probs * grad_probs, edges, jnp.add))
     query = q_ref[...].astype(F32) * inv_root
     total = jnp.zeros((nodes, width), F32)
     for e in range(edges):
@@ -330,9 +327,14 @@
         total += share * keys_ref[e].astype(F32)
         edge_ref[e * nodes : (e + 1) * nodes, :] = (share * query).astype(BF16)
     grad_query_ref[...] = (total * inv_root).astype(BF16)
+
+
+def query_back_kernel(edge_ref, hot_ref, grad_value_ref, w_ref, grad_key_ref, head_ref, tail_ref):
+    width = edge_ref.shape[1]
+    rim = head_ref.shape[0]
+    nodes = hot_ref.shape[0] - 2 * rim
     grad_key = nn(hot_ref[...], edge_ref[...]).astype(BF16)
     grad_key_ref[...] = grad_key
-    rim = head_ref.shape[0]
     rows = nt(grad_key[nodes:], w_ref[:, width : 2 * width])
     rows += nt(grad_value_ref[nodes:, :], w_ref[:, 2 * width :])
     rows = rows.astype(BF16)
@@ -355,15 +357,16 @@
 
 
 def joined(keep, arrived, variables):
-    total = keep.astype(F32) + arrived.astype(F32)
+    total = keep + arrived.astype(F32)
     if variables is None:
         return total
     last = total[..., -LANES:]
     lane = iota(last.shape, last.ndim - 1)
-    loss = last[..., variables : variables + 1] + last[..., variables + 1 : variables + 2]
+    at = 2 * padded(variables) - LANES
+    loss = last[..., at : at + 1] + last[..., at + 1 : at + 2]
     high = loss.astype(BF16).astype(F32)
-    last = jnp.where(lane == variables, high, last)
-    last = jnp.where(lane == variables + 1, loss - high, last)
+    last = jnp.where(lane == at, high, last)
+    last = jnp.where(lane == at + 1, loss - high, last)
     return jnp.concatenate([total[..., :-LANES], last], axis=-1)
 
 
@@ -396,6 +399,11 @@
 def swapped(array, axis, bit):
     count = lax.axis_size(axis)
     return lax.ppermute(array, axis, [(i, i ^ bit) for i in range(count)])
+
+
+def from_members(array, members):
+    others = {away: swapped(array, "member", away) for away in reversed(range(1, members))}
+    return [array] + [others[away] for away in range(1, members)]
 
 
 class Halving:
@@ -426,19 +434,22 @@
             )
 
 
-def unpack_kernel(*refs, aways):
-    sum_refs = refs[: len(aways)]
-    qkv_ref, out_ref, dec_ref, loss_ref = refs[len(aways) :]
+def unpack_kernel(w_dec_ref, *refs):
+    sum_refs = refs[:-4]
+    qkv_ref, out_ref, dec_ref, loss_ref = refs[-4:]
     width = out_ref.shape[-1]
     variables = dec_ref.shape[-1]
+    step = padded(variables)
+    start = 3 * width
     place = lax.axis_index("member")
-    for ref, away in zip(sum_refs, aways):
+    for away, ref in enumerate(sum_refs):
         at = place ^ away
-        qkv_ref[at] = ref[:, : 3 * width].astype(F32)
-        out_ref[at] = ref[:, 3 * width : 4 * width].astype(F32)
-        dec_ref[at] = ref[:, 4 * width : 4 * width + variables].astype(F32)
-    last = sum_refs[0][0:1, 4 * width :].astype(F32)
-    loss_ref[...] = last[:, variables : variables + 1] + last[:, variables + 1 : variables + 2]
+        qkv_ref[at] = ref[:, :start].astype(F32)
+        out_ref[at] = nn(ref[:, start : start + variables], w_dec_ref[...])
+        dec_ref[at] = ref[:, start + step : start + step + variables].astype(F32)
+    start += 2 * step
+    last = sum_refs[0][0:1, start : start + 2].astype(F32)
+    loss_ref[...] = last[:, 0:1] + last[:, 1:2]
 
 
 def own_feature_kernel(grad_query_ref, grad_key_ref, grad_value_ref, w_ref, grad_ref):
@@ -543,16 +554,15 @@
         mib=16,
     )
     out_left, out_right = swap_rims(head, tail)
-    change, sent = on_core(
-        decode_kernel,
-        [((variables, points), F32), ((variables, points), BF16)],
-        projected, out_left, out_right, mix,
-    )
-    every = lax.all_gather(sent[None], "member", axis=0, tiled=True)
+    core = [("member", 1)]
+    across = [("member", 1 << b) for b in range(1, shift_of(members))]
+    own_tables = from_members(projected, members)
+    (rims,) = on_core(join_kernel, [((variables, 2 * rim), BF16)], out_left, out_right)
+    rim_tables = from_members(rims, members)
     grad, head, tail, loss = on_core(
         functools.partial(score_kernel, points=total_points),
         [((variables, points), BF16), rim_columns, rim_columns, ((1, LANES), F32)],
-        change, every, state, target, area[None], var_weight[None], mix,
+        state, target, area[None], var_weight[None], mix, *own_tables, *rim_tables,
     )
     back_left, back_right = swap_rims(head, tail)
     grad_own, hot = on_core(
@@ -572,21 +582,21 @@
     grad_node, grad_mixed, grad_value, value_send, value_keep = on_core(
         value_back_kernel,
         [((nodes, width), F32), ((nodes, width), BF16), ((table_rows, width), BF16)]
-        + halves(2 * width + LANES),
+        + halves(width + 2 * LANES),
         count, grad_own, back_left, back_right, boundary, node_out, w_decoder,
         attended, w_out, probs, hot, features, left, right, loss,
-        scratch=[pltpu.VMEM((edges * nodes, width), BF16), whole(2 * width + LANES)],
+        scratch=[pltpu.VMEM((edges * nodes, width), BF16), whole(width + 2 * LANES)],
         mib=16,
     )
-    (grad_scores,) = on_core(
-        score_back_kernel, [((nodes, columns), F32)], grad_mixed, probs, values
-    )
-    grad_query, grad_key, head, tail = on_core(
+    grad_query, key_edges = on_core(
+        score_back_kernel,
+        [((nodes, width), BF16), ((edges * nodes, width), BF16)],
+        grad_mixed, probs, values, queries, keys,
+    )
+    grad_key, head, tail = on_core(
         query_back_kernel,
-        [((nodes, width), BF16), ((table_rows, width), BF16), rim_rows, rim_rows],
-        grad_scores, queries, keys, hot, grad_value, w_qkv,
-        scratch=[pltpu.VMEM((edges * nodes, width), BF16)],
-        mib=12,
+        [((table_rows, width), BF16), rim_rows, rim_rows],
+        key_edges, hot, grad_value, w_qkv,
     )
     rim_left, rim_right = swap_rims(head, tail)
     query_send, query_keep = on_core(
@@ -595,9 +605,7 @@
         features, left, right, grad_query, grad_key,
         scratch=[whole(2 * width)],
     )
-    (own_feature,) = on_core(
-        own_feature_kernel, [((nodes, width), F32)], grad_query, grad_key, grad_value, w_qkv
-    )
+    (own_feature,) = on_core(own_feature_kernel, [((nodes, width), F32)], grad_query, grad_key, grad_value, w_qkv)
     (grad_latent,) = on_core(
         latent_grad_kernel,
         [((nodes, width), BF16)],
@@ -605,43 +613,35 @@
         scratch=[pltpu.VMEM((2 * rim, width), BF16)],
     )
 
-    core = [("member", 1)]
-    across = [("member", 1 << b) for b in range(1, shift_of(members))]
     around = [("region", 1 << b) for b in range(shift_of(regions))]
+    around[:2] = around[1::-1]
     value_sum, query_sum = Halving(regions, members, rows), Halving(regions, members, rows)
-    value_keep, value_in = value_sum.run(
-        value_send, value_keep, core + across + around[:2], variables
-    )
-    query_keep, query_in = query_sum.run(
-        query_send, query_keep, core + across + around[1::-1], None
-    )
-    packed = 4 * width + LANES
-    half, _ = value_sum.half(around[2], packed)
-    _, both_values = value_sum.half(around[2], 2 * width + LANES)
-    _, both_queries = value_sum.half(around[2], 2 * width)
+    value_keep, value_in = value_sum.run(value_send, value_keep, core + across + around[:1], variables)
+    query_keep, query_in = query_sum.run(query_send, query_keep, core + across + around[:1], None)
+    packed = 3 * width + 2 * LANES
+    half, _ = value_sum.half(around[1], packed)
+    _, both_values = value_sum.half(around[1], width + 2 * LANES)
+    _, both_queries = value_sum.half(around[1], 2 * width)
     send, keep = on_core(
-        functools.partial(merge_kernel, axis=around[2][0], bit=around[2][1], variables=variables),
+        functools.partial(merge_kernel, axis=around[1][0], bit=around[1][1], variables=variables),
         [(half, BF16), (half, F32)],
         query_keep.reshape(both_queries), query_in.reshape(both_queries),
         value_keep.reshape(both_values), value_in.reshape(both_values),
     )
-    keep, arrived = value_sum.run(send, keep, around[2:], variables)
+    keep, arrived = value_sum.run(send, keep, around[1:], variables)
     piece = (1, rows, packed)
     (total,) = on_core(
         functools.partial(total_kernel, variables=variables), [(piece, BF16)],
         keep.reshape(piece), arrived.reshape(piece),
     )
-    sums, aways = [total.reshape(rows, packed)], [0]
-    for axis, bit in across[::-1] + core:
-        sums = sums + [swapped(piece, axis, bit) for piece in sums]
-        aways = aways + [away ^ bit for away in aways]
+    sums = from_members(total.reshape(rows, packed), members)
     share_qkv, share_out, share_dec, loss = on_core(
-        functools.partial(unpack_kernel, aways=aways),
+        unpack_kernel,
         [
             ((members, rows, 3 * width), F32), ((members, rows, width), F32),
             ((members, rows, variables), F32), ((1, 1), F32),
         ],
-        *sums,
+        w_decoder, *sums,
     )
     held = members * rows
     return (

time: 93.2 us -> 85.3 us (0.915)
  blocking collectives: 8.96 us -> 0 us
  starting transfers between devices: 28.7 us -> 34.3 us
  waiting for transfers between devices: 30.3 us -> 26.1 us
    all_gather x1 -> x0, blocking collectives: 8.96 us -> none  [layer(): every = lax.all_gather(sent[None], 'member', axis=0, tiled=True)]
    ppermute x12 -> x17, starting transfers between devices: 7.14 us -> 13.6 us  [swapped(): return lax.ppermute(array, axis, [(i, i ^ bit) for i in range(count)])]
    ppermute x4, waiting for transfers between devices: 4.83 us -> 1.47 us  [swap_rims(): lax.ppermute(tail, 'region', [(i, (i + 1) % count) for i in range(count)])]
    ppermute x4, starting transfers between devices: 16.2 us -> 14.4 us  [swap_rims(): lax.ppermute(head, 'region', [((i + 1) % count, i) for i in range(count)])]
    ppermute x12 -> x17, waiting for transfers between devices: 24.4 us -> 23.5 us  [swapped(): return lax.ppermute(array, axis, [(i, i ^ bit) for i in range(count)])]
    pallas_call x21 -> x20, Pallas kernels: 23.4 us -> 23.1 us  [on_core(): pl.pallas_call(kernel, out_shape=[jax.ShapeDtypeStruct(s, d) for s, d in...]
  transfers between devices with their start and end apart: 20 -> 25, of which waited for: 12 -> 15; matrix products, arithmetic and copies ran while one was open for 0% -> 0% of each run, Pallas kernels for 11% -> 7%
where the time goes in v3:
time: 85.3 us; the launch traced here: 85.1 us
  starting transfers between devices  34.3 us (40%)
  waiting for transfers between devices  26.1 us (31%)
  Pallas kernels  23.1 us (27%)
  between operations  1.57 us (2%)
    ppermute x17, waiting for transfers between devices, swapped(): return lax.ppermute(array, axis, [(i, i ^ bit) for i in range(count)])  23.5 us
    pallas_call x20, Pallas kernels, on_core(): pl.pallas_call(kernel, out_shape=[jax.ShapeDtypeStruct(s, d) for s, d in...  23.1 us
    ppermute x4, starting transfers between devices, swap_rims(): lax.ppermute(head, 'region', [((i + 1) % count, i) for i in range(count)])  14.4 us
    ppermute x17, starting transfers between devices, swapped(): return lax.ppermute(array, axis, [(i, i ^ bit) for i in range(count)])  13.6 us
    ppermute x4, starting transfers between devices, swap_rims(): lax.ppermute(tail, 'region', [(i, (i + 1) % count) for i in range(count)])  6.31 us
  transfers between devices with their start and end apart: 25, of which 15 were waited for; matrix products, arithmetic and copies ran while one was open for 0% of the time, Pallas kernels for 7%

profile of v3, /device:TPU:0, one launch (start us, length us, event | category | flops | bytes accessed | tf_op | source)
XLA Modules:
  0.0 85.1 jit_solution(6020183537487902753)
XLA Ops:
  0.7 1.5 %shard_map.182 = (bf16[256,512]{1,0:T(8,128)(2,1)S(1)}, bf16[128,512]{1,0:T(8,128)(2,1)S(1)}, bf16[128,512]{1,0:T(8,128)(2,1)S(1)}) custom-call(bf16[256,512]{1,0:T(8,128)(2,1)} %bitcast.29, f32[1,512]{1,0:T(1,128)} %bitcast.55, s32[1,256]{1,0:T(1,128)} %border_ref.5), custom_call_target="tpu_custom_call" | custom-call | tf_op jit(solution)/shard_map/pallas_call | solution.py:34
  2.1 3.0 %collective-permute-start = (bf16[128,512]{1,0:T(8,128)(2,1)S(1)}, bf16[128,512]{1,0:T(8,128)(2,1)S(1)}, u32[]{:S(2)}, u32[]{:S(2)}) collective-permute-start(bf16[128,512]{1,0:T(8,128)(2,1)S(1)} %get-tuple-element.55), channel_id=1, source_target_pairs={{0,4},{4,8},{8,12},{12,16},{16,20},{20,24},{24,28},{28,0},{1,5},{5... | collective-permute-start | bytes 393224 | tf_op jit(solution)/shard_map/ppermute | solution.py:483
  5.2 3.1 %collective-permute-start.1 = (bf16[128,512]{1,0:T(8,128)(2,1)S(1)}, bf16[128,512]{1,0:T(8,128)(2,1)S(1)}, u32[]{:S(2)}, u32[]{:S(2)}) collective-permute-start(bf16[128,512]{1,0:T(8,128)(2,1)S(1)} %get-tuple-element.56), channel_id=1, source_target_pairs={{4,0},{8,4},{12,8},{16,12},{20,16},{24,20},{28,24},{0,28},{5,1},{9... | collective-permute-start | bytes 393224 | tf_op jit(solution)/shard_map/ppermute | solution.py:484
  9.0 2.1 %shard_map.183 = (bf16[256,512]{1,0:T(8,128)(2,1)S(1)}, bf16[256,1024]{1,0:T(8,128)(2,1)S(1)}, bf16[512,1024]{1,0:T(8,128)(2,1)S(1)}, bf16[512,1536]{1,0:T(8,128)(2,1)S(1)}) custom-call(bf16[512,1536]{1,0:T(8,128)(2,1)} %w_hbm.1, s32[3,1024]{1,0:T(4,128)} %src_hbm.1, f32[3,1024]{1,0:T(4,128)} %weight_hbm.1, bf16[256,512]{1,0:T(8,128)(2,1)S(1)} %get-tuple-element.54.features_ref), custom_call_target="tpu_custom_call" | custom-call | tf_op jit(solution)/shard_map/pallas_call | solution.py:34
  11.2 0.7 collective-permute-done.left_ref
  11.8 1.1 %collective-permute-done.1.right_ref = bf16[128,512]{1,0:T(8,128)(2,1)S(1)} collective-permute-done((bf16[128,512]{1,0:T(8,128)(2,1)S(1)}, bf16[128,512]{1,0:T(8,128)(2,1)S(1)}, u32[]{:S(2)}, u32[]{:S(2)}) %collective-permute-start.1) | collective-permute-done | bytes 131104 | tf_op jit(solution)/shard_map/ppermute | solution.py:484
  13.0 5.4 %shard_map.184 = (bf16[256,512]{1,0:T(8,128)(2,1)S(1)}, bf16[98,256]{1,0:T(8,128)(2,1)S(1)}, bf16[98,128]{1,0:T(8,128)(2,1)S(1)}, bf16[98,128]{1,0:T(8,128)(2,1)...) custom-call(bf16[512,512]{1,0:T(8,128)(2,1)} %w_out_ref.1, ...), custom_call_target="tpu_custom_call" | custom-call | tf_op jit(solution)/shard_map/pallas_call | solution.py:34
  18.4 0.3 collective-permute-start.5
  18.8 4.4 %collective-permute-start.6 = (bf16[98,128]{1,0:T(8,128)(2,1)S(1)}, bf16[98,128]{1,0:T(8,128)(2,1)S(1)}, u32[]{:S(2)}, u32[]{:S(2)}) collective-permute-start(bf16[98,128]{1,0:T(8,128)(2,1)S(1)} %get-tuple-element.63), channel_id=1, source_target_pairs={{4,0},{8,4},{12,8},{16,12},{20,16},{24,20},{28,24},{0,28},{5,1},{9... | collective-permute-start | bytes 75272 | tf_op jit(solution)/shard_map/ppermute | solution.py:484
  23.2 1.5 %collective-permute-start.3 = (bf16[98,256]{1,0:T(8,128)(2,1)S(1)}, bf16[98,256]{1,0:T(8,128)(2,1)S(1)}, u32[]{:S(2)}, u32[]{:S(2)}) collective-permute-start(bf16[98,256]{1,0:T(8,128)(2,1)S(1)} %get-tuple-element.61.refs_0_), channel_id=1, source_target_pairs={{0,2},{1,3},{2,0},{3,1},{4,6},{5,7},{6,4},{7,5},{8,10},{9,11},{10,... | collective-permute-start | bytes 150536 | tf_op jit(solution)/shard_map/ppermute | solution.py:401
  24.7 0.3 collective-permute-done.5.left_ref
  25.1 0.6 collective-permute-start.9
  25.7 1.5 %collective-permute-start.8 = (bf16[98,256]{1,0:T(8,128)(2,1)S(1)}, bf16[98,256]{1,0:T(8,128)(2,1)S(1)}, u32[]{:S(2)}, u32[]{:S(2)}) collective-permute-start(bf16[98,256]{1,0:T(8,128)(2,1)S(1)} %shard_map.185.refs_4_), channel_id=1, source_target_pairs={{0,2},{1,3},{2,0},{3,1},{4,6},{5,7},{6,4},{7,5},{8,10},{9,11},{10,... | collective-permute-start | bytes 150536 | tf_op jit(solution)/shard_map/ppermute | solution.py:401
  27.2 0.8 collective-permute-done.3.refs_2_
  27.9 0.8 collective-permute-done.9.refs_7_
  28.7 1.6 %collective-permute-done.8.refs_6_ = bf16[98,256]{1,0:T(8,128)(2,1)S(1)} collective-permute-done((bf16[98,256]{1,0:T(8,128)(2,1)S(1)}, bf16[98,256]{1,0:T(8,128)(2,1)S(1)}, u32[]{:S(2)}, u32[]{:S(2)}) %collective-permute-start.8) | collective-permute-done | bytes 50208 | tf_op jit(solution)/shard_map/ppermute | solution.py:401
  30.4 1.5 %shard_map.186 = (bf16[98,1024]{1,0:T(8,128)(2,1)S(1)}, bf16[98,128]{1,0:T(8,128)(2,1)S(1)}, bf16[98,128]{1,0:T(8,128)(2,1)S(1)}, f32[1,128]{1,0:T(1,128)S(1)}) custom-call(f32[98,1024]{1,0:T(8,128)S(1)} %copy-done.3, f32[98,1024]{1,0:T(8,128)S(1)} %copy-done.4, f32[1,1024]{1,0:T(1,128)S(1)} %bitcast.57, f32[1,98]{1,0:T(1,128)S(1)} %bitcast.58, ...), custom_call_target="tpu_custom_call" | custom-call | tf_op jit(solution)/shard_map/pallas_call | solution.py:34
  31.9 1.5 %collective-permute-start.10 = (bf16[98,128]{1,0:T(8,128)(2,1)S(1)}, bf16[98,128]{1,0:T(8,128)(2,1)S(1)}, u32[]{:S(2)}, u32[]{:S(2)}) collective-permute-start(bf16[98,128]{1,0:T(8,128)(2,1)S(1)} %get-tuple-element.66), channel_id=1, source_target_pairs={{0,4},{4,8},{8,12},{12,16},{16,20},{20,24},{24,28},{28,0},{1,5},{5... | collective-permute-start | bytes 75272 | tf_op jit(solution)/shard_map/ppermute | solution.py:483
  33.3 3.5 %collective-permute-start.11 = (bf16[98,128]{1,0:T(8,128)(2,1)S(1)}, bf16[98,128]{1,0:T(8,128)(2,1)S(1)}, u32[]{:S(2)}, u32[]{:S(2)}) collective-permute-start(bf16[98,128]{1,0:T(8,128)(2,1)S(1)} %get-tuple-element.67), channel_id=1, source_target_pairs={{4,0},{8,4},{12,8},{16,12},{20,16},{24,20},{28,24},{0,28},{5,1},{9... | collective-permute-start | bytes 75272 | tf_op jit(solution)/shard_map/ppermute | solution.py:484
  36.9 1.1 %shard_map.187 = (f32[98,256]{1,0:T(8,128)S(1)}, bf16[512,2048]{1,0:T(8,128)(2,1)S(1)}) custom-call(bf16[512,1024]{1,0:T(8,128)(2,1)S(1)} %get-tuple-element.57.mix_ref, bf16[98,1024]{1,0:T(8,128)(2,1)S(1)} %get-tuple-element.64.grad_ref, s32[8,256]{1,0:T(8,128)S(1)} %bitcast.54), custom_call_target="tpu_custom_call" | custom-call | tf_op jit(solution)/shard_map/pallas_call | solution.py:34
  38.0 0.5 collective-permute-done.10.from_left_ref
  38.5 3.2 %shard_map.188 = (f32[256,512]{1,0:T(8,128)S(1)}, bf16[256,512]{1,0:T(8,128)(2,1)S(1)}, bf16[512,512]{1,0:T(8,128)(2,1)S(1)}, bf16[16,16,768]{2,1,0:T(8,128)(2,1)S(1)}, f32[16,16,768]{2,1,0:T(8,128)S(1)}) custom-call(s32[1,1]{1,0:T(1,128)} %bitcast.28.count_ref, f32[98,256]{1,0:T(8,128)S(1)} %get-tuple-element.65.own_ref, ...), custom_call_target="tpu_custom_call" | custom-call | tf_op jit(solution)/shard_map/pallas_call | solution.py:34
  41.7 1.9 %shard_map.189 = (bf16[256,512]{1,0:T(8,128)(2,1)S(1)}, bf16[2048,512]{1,0:T(8,128)(2,1)S(1)}) custom-call(bf16[256,512]{1,0:T(8,128)(2,1)S(1)} %get-tuple-element.73.mixed_ref, f32[256,128]{1,0:T(8,128)S(1)} %get-tuple-element.70.probs_ref, bf16[8,256,512]{2,1,0:T(8,128)(2,1)S(1)} %get-tuple-element.74.values_ref, ...), custom_call_target="tpu_custom_call" | custom-call | tf_op jit(solution)/shard_map/pallas_call | solution.py:34
  43.7 1.5 %shard_map.190 = (bf16[512,512]{1,0:T(8,128)(2,1)S(1)}, bf16[128,512]{1,0:T(8,128)(2,1)S(1)}, bf16[128,512]{1,0:T(8,128)(2,1)S(1)}) custom-call(bf16[2048,512]{1,0:T(8,128)(2,1)S(1)} %get-tuple-element.77.edge_ref, bf16[512,2048]{1,0:T(8,128)(2,1)S(1)} %get-tuple-element.71.hot_ref, bf16[512,512]{1,0:T(8,128)(2,1)S(1)} %get-tuple-element.78.grad_value_ref, ...), custom_call_target="tpu_custom_call" | custom-call | tf_op jit(solution)/shard_map/pallas_call | solution.py:34
  45.2 1.0 %shard_map.191 = (bf16[16,16,1024]{2,1,0:T(8,128)(2,1)S(1)}, f32[16,16,1024]{2,1,0:T(8,128)S(1)}) custom-call(bf16[256,512]{1,0:T(8,128)(2,1)S(1)} %get-tuple-element.54.features_ref, bf16[128,512]{1,0:T(8,128)(2,1)S(1)} %collective-permute-done.left_ref, bf16[128,512]{1,0:T(8,128)(2,1)S(1)} %collective-permute-done.1.right_ref, ...), custom_call_target="tpu_custom_call" | custom-call | tf_op jit(solution)/shard_map/pallas_call | solution.py:34
  46.3 0.5 collective-permute-start.15
  46.8 1.4 %collective-permute-done.12 = bf16[16,16,1024]{2,1,0:T(8,128)(2,1)S(1)} collective-permute-done((bf16[16,16,1024]{2,1,0:T(8,128)(2,1)S(1)}, bf16[16,16,1024]{2,1,0:T(8,128)(2,1)S(1)}, u32[]{:S(2)}, u32[]{:S(2)}) %collective-permute-start.12) | collective-permute-done | bytes 524320 | tf_op jit(solution)/shard_map/ppermute | solution.py:401
  48.3 1.2 %collective-permute-start.13 = (bf16[8,16,1024]{2,1,0:T(8,128)(2,1)S(1)}, bf16[8,16,1024]{2,1,0:T(8,128)(2,1)S(1)}, u32[]{:S(2)}, u32[]{:S(2)}) collective-permute-start(bf16[8,16,1024]{2,1,0:T(8,128)(2,1)S(1)} %get-tuple-element.83), channel_id=1, source_target_pairs={{0,2},{1,3},{2,0},{3,1},{4,6},{5,7},{6,4},{7,5},{8,10},{9,11},{10,... | collective-permute-start | bytes 786440 | tf_op jit(solution)/shard_map/ppermute | solution.py:401
  49.6 0.2 shard_map.194
  49.8 0.9 %collective-permute-start.16 = (bf16[8,16,768]{2,1,0:T(8,128)(2,1)S(1)}, bf16[8,16,768]{2,1,0:T(8,128)(2,1)S(1)}, u32[]{:S(2)}, u32[]{:S(2)}) collective-permute-start(bf16[8,16,768]{2,1,0:T(8,128)(2,1)S(1)} %get-tuple-element.89), channel_id=1, source_target_pairs={{0,2},{1,3},{2,0},{3,1},{4,6},{5,7},{6,4},{7,5},{8,10},{9,11},{10,... | collective-permute-start | bytes 589832 | tf_op jit(solution)/shard_map/ppermute | solution.py:401
  50.8 6.8 %collective-permute-done.13 = bf16[8,16,1024]{2,1,0:T(8,128)(2,1)S(1)} collective-permute-done((bf16[8,16,1024]{2,1,0:T(8,128)(2,1)S(1)}, bf16[8,16,1024]{2,1,0:T(8,128)(2,1)S(1)}, u32[]{:S(2)}, u32[]{:S(2)}) %collective-permute-start.13) | collective-permute-done | bytes 262176 | tf_op jit(solution)/shard_map/ppermute | solution.py:401
  57.6 0.4 collective-permute-start.14
  58.0 2.9 %collective-permute-done.16 = bf16[8,16,768]{2,1,0:T(8,128)(2,1)S(1)} collective-permute-done((bf16[8,16,768]{2,1,0:T(8,128)(2,1)S(1)}, bf16[8,16,768]{2,1,0:T(8,128)(2,1)S(1)}, u32[]{:S(2)}, u32[]{:S(2)}) %collective-permute-start.16) | collective-permute-done | bytes 196640 | tf_op jit(solution)/shard_map/ppermute | solution.py:401
  61.2 0.4 collective-permute-start.17
  61.5 4.3 %collective-permute-done.17 = bf16[2,32,768]{2,1,0:T(8,128)(2,1)S(1)} collective-permute-done((bf16[2,32,768]{2,1,0:T(8,128)(2,1)S(1)}, bf16[2,32,768]{2,1,0:T(8,128)(2,1)S(1)}, u32[]{:S(2)}, u32[]{:S(2)}) %collective-permute-start.17) | collective-permute-done | bytes 98336 | tf_op jit(solution)/shard_map/ppermute | solution.py:401
  65.8 0.2 shard_map.196
  66.1 0.6 collective-permute-start.18
  66.7 1.5 %collective-permute-start.23 = (bf16[128,512]{1,0:T(8,128)(2,1)S(1)}, bf16[128,512]{1,0:T(8,128)(2,1)S(1)}, u32[]{:S(2)}, u32[]{:S(2)}) collective-permute-start(bf16[128,512]{1,0:T(8,128)(2,1)S(1)} %get-tuple-element.100), channel_id=1, source_target_pairs={{0,4},{4,8},{8,12},{12,16},{16,20},{20,24},{24,28},{28,0},{1,5},{5... | collective-permute-start | bytes 393224 | tf_op jit(solution)/shard_map/ppermute | solution.py:483
  68.1 3.3 %collective-permute-start.24 = (bf16[128,512]{1,0:T(8,128)(2,1)S(1)}, bf16[128,512]{1,0:T(8,128)(2,1)S(1)}, u32[]{:S(2)}, u32[]{:S(2)}) collective-permute-start(bf16[128,512]{1,0:T(8,128)(2,1)S(1)} %get-tuple-element.101), channel_id=1, source_target_pairs={{4,0},{8,4},{12,8},{16,12},{20,16},{24,20},{28,24},{0,28},{5,1},{9... | collective-permute-start | bytes 393224 | tf_op jit(solution)/shard_map/ppermute | solution.py:484
  71.4 0.9 %collective-permute-done.18 = bf16[2,16,1792]{2,1,0:T(8,128)(2,1)S(1)} collective-permute-done((bf16[2,16,1792]{2,1,0:T(8,128)(2,1)S(1)}, bf16[2,16,1792]{2,1,0:T(8,128)(2,1)S(1)}, u32[]{:S(2)}, u32[]{:S(2)}) %collective-permute-start.18) | collective-permute-done | bytes 114720 | tf_op jit(solution)/shard_map/ppermute | solution.py:401
  72.5 4.0 %collective-permute-start.19 = (bf16[1,16,1792]{2,1,0:T(8,128)(2,1)S(1)}, bf16[1,16,1792]{2,1,0:T(8,128)(2,1)S(1)}, u32[]{:S(2)}, u32[]{:S(2)}) collective-permute-start(bf16[1,16,1792]{2,1,0:T(8,128)(2,1)S(1)} %get-tuple-element.95), channel_id=1, source_target_pairs={{0,16},{4,20},{8,24},{12,28},{16,0},{20,4},{24,8},{28,12},{1,17},{... | collective-permute-start | bytes 172040 | tf_op jit(solution)/shard_map/ppermute | solution.py:401
  76.5 2.2 %collective-permute-done.19.arrived_ref = bf16[1,16,1792]{2,1,0:T(8,128)(2,1)S(1)} collective-permute-done((bf16[1,16,1792]{2,1,0:T(8,128)(2,1)S(1)}, bf16[1,16,1792]{2,1,0:T(8,128)(2,1)S(1)}, u32[]{:S(2)}, u32[]{:S(2)}) %collective-permute-start.19) | collective-permute-done | bytes 57376 | tf_op jit(solution)/shard_map/ppermute | solution.py:401
  78.8 1.7 %collective-permute-start.21 = (bf16[16,1792]{1,0:T(8,128)(2,1)S(1)}, bf16[16,1792]{1,0:T(8,128)(2,1)S(1)}, u32[]{:S(2)}, u32[]{:S(2)}) collective-permute-start(bf16[16,1792]{1,0:T(8,128)(2,1)S(1)} %bitcast.45), channel_id=1, source_target_pairs={{0,2},{1,3},{2,0},{3,1},{4,6},{5,7},{6,4},{7,5},{8,10},{9,11},{10,... | collective-permute-start | bytes 172040 | tf_op jit(solution)/shard_map/ppermute | solution.py:401
  80.7 0.6 shard_map.200.own_ref
  81.3 1.1 %shard_map.201 = bf16[256,512]{1,0:T(8,128)(2,1)} custom-call(bf16[256,512]{1,0:T(8,128)(2,1)S(1)} %bitcast.31, f32[1,512]{1,0:T(1,128)S(1)} %bitcast.56, f32[256,512]{1,0:T(8,128)S(1)} %shard_map.200.own_ref, bf16[128,512]{1,0:T(8,128)(2,1)S(1)} %collective-permute-done.23.from_left_ref, bf16[128,512]{1,0:T(8,128)(2,1)S(1)} %collective-permute-done.24.from_right_ref, ...), custom_call_target="tpu_custom_call" | custom-call | tf_op jit(solution)/shard_map/pallas_call | solution.py:34
  82.4 0.4 collective-permute-done.22.refs_3_
  82.9 1.3 %collective-permute-done.21.refs_2_ = bf16[16,1792]{1,0:T(8,128)(2,1)S(1)} collective-permute-done((bf16[16,1792]{1,0:T(8,128)(2,1)S(1)}, bf16[16,1792]{1,0:T(8,128)(2,1)S(1)}, u32[]{:S(2)}, u32[]{:S(2)}) %collective-permute-start.21) | collective-permute-done | bytes 57376 | tf_op jit(solution)/shard_map/ppermute | solution.py:401
  84.2 0.9 %shard_map.199 = (f32[4,16,1536]{2,1,0:T(8,128)}, f32[4,16,512]{2,1,0:T(8,128)}, f32[4,16,98]{2,1,0:T(8,128)}, f32[1,1]{1,0:T(1,128)}) custom-call(bf16[98,512]{1,0:T(8,128)(2,1)S(1)} %bitcast.35, bf16[16,1792]{1,0:T(8,128)(2,1)S(1)} %bitcast.47, bf16[16,1792]{1,0:T(8,128)(2,1)S(1)} %collective-permute-done.20.refs_1_, ...), custom_call_target="tpu_custom_call" | custom-call | tf_op jit(solution)/shard_map/pallas_call | solution.py:34
  (42 shorter events, 1.1 us)
Async XLA Ops:
  0.6 12.3 %copy-start.6 = (s32[1,256]{1,0:T(1,128)S(1)}, s32[1,256]{1,0:T(1,128)}, u32[]{:S(2)}) copy-start(s32[1,256]{1,0:T(1,128)} %border_ref.5) | copy-start | bytes 3076
  0.6 12.3 %copy-start = (bf16[1,256,512]{2,1,0:T(8,128)(2,1)S(1)}, bf16[1,256,512]{2,1,0:T(8,128)(2,1)}, u32[]{:S(2)}) copy-start(bf16[1,256,512]{2,1,0:T(8,128)(2,1)} %param.15) | copy-start | bytes 786436
  0.7 12.3 %copy-start.5 = (s32[256,8]{0,1:T(8,128)S(1)}, s32[256,8]{0,1:T(8,128)}, u32[]{:S(2)}) copy-start(s32[256,8]{0,1:T(8,128)} %param.20) | copy-start | bytes 24580
  2.1 9.7 %collective-permute-start = (bf16[128,512]{1,0:T(8,128)(2,1)S(1)}, bf16[128,512]{1,0:T(8,128)(2,1)S(1)}, u32[]{:S(2)}, u32[]{:S(2)}) collective-permute-start(bf16[128,512]{1,0:T(8,128)(2,1)S(1)} %get-tuple-element.55), channel_id=1, source_target_pairs={{0,4},{4,8},{8,12},{12,16},{16,20},{20,24},{24,28},{28,0},{1,5},{5... | collective-permute-start | bytes 393224 | tf_op jit(solution)/shard_map/ppermute | solution.py:483
  5.2 7.8 %collective-permute-start.1 = (bf16[128,512]{1,0:T(8,128)(2,1)S(1)}, bf16[128,512]{1,0:T(8,128)(2,1)S(1)}, u32[]{:S(2)}, u32[]{:S(2)}) collective-permute-start(bf16[128,512]{1,0:T(8,128)(2,1)S(1)} %get-tuple-element.56), channel_id=1, source_target_pairs={{4,0},{8,4},{12,8},{16,12},{20,16},{24,20},{28,24},{0,28},{5,1},{9... | collective-permute-start | bytes 393224 | tf_op jit(solution)/shard_map/ppermute | solution.py:484
  11.1 19.2 %copy-start.3 = (f32[98,1024]{1,0:T(8,128)S(1)}, f32[98,1024]{1,0:T(8,128)}, u32[]{:S(2)}) copy-start(f32[98,1024]{1,0:T(8,128)} %state_ref.1) | copy-start | bytes 1204228
  11.1 19.2 %copy-start.4 = (f32[98,1024]{1,0:T(8,128)S(1)}, f32[98,1024]{1,0:T(8,128)}, u32[]{:S(2)}) copy-start(f32[98,1024]{1,0:T(8,128)} %target_ref.1) | copy-start | bytes 1204228
  11.1 19.2 %copy-start.8 = (f32[1024]{0:T(1024)S(1)}, f32[1024]{0:T(1024)}, u32[]{:S(2)}) copy-start(f32[1024]{0:T(1024)} %param.28) | copy-start | bytes 12292
  11.1 19.2 %copy-start.9 = (f32[98]{0:T(128)S(1)}, f32[98]{0:T(128)}, u32[]{:S(2)}) copy-start(f32[98]{0:T(128)} %param.29) | copy-start | bytes 1180
  18.3 20.1 %copy-start.1 = (bf16[512,512]{1,0:T(8,128)(2,1)S(1)}, bf16[512,512]{1,0:T(8,128)(2,1)}, u32[]{:S(2)}) copy-start(bf16[512,512]{1,0:T(8,128)(2,1)} %w_out_ref.1) | copy-start | bytes 1572868
  18.4 20.1 %copy-start.2 = (bf16[512,98]{0,1:T(8,128)(2,1)S(1)}, bf16[512,98]{0,1:T(8,128)(2,1)}, u32[]{:S(2)}) copy-start(bf16[512,98]{0,1:T(8,128)(2,1)} %param.23) | copy-start | bytes 301060
  18.4 8.8 %collective-permute-start.4 = (bf16[98,256]{1,0:T(8,128)(2,1)S(1)}, bf16[98,256]{1,0:T(8,128)(2,1)S(1)}, u32[]{:S(2)}, u32[]{:S(2)}) collective-permute-start(bf16[98,256]{1,0:T(8,128)(2,1)S(1)} %get-tuple-element.61.refs_0_), channel_id=1, source_target_pairs={{0,3},{1,2},{2,1},{3,0},{4,7},{5,6},{6,5},{7,4},{8,11},{9,10},{10,... | collective-permute-start | bytes 150536 | tf_op jit(solution)/shard_map/ppermute | solution.py:401
  18.4 6.6 %collective-permute-start.5 = (bf16[98,128]{1,0:T(8,128)(2,1)S(1)}, bf16[98,128]{1,0:T(8,128)(2,1)S(1)}, u32[]{:S(2)}, u32[]{:S(2)}) collective-permute-start(bf16[98,128]{1,0:T(8,128)(2,1)S(1)} %get-tuple-element.62), channel_id=1, source_target_pairs={{0,4},{4,8},{8,12},{12,16},{16,20},{20,24},{24,28},{28,0},{1,5},{5... | collective-permute-start | bytes 75272 | tf_op jit(solution)/shard_map/ppermute | solution.py:483
  18.8 6.3 %collective-permute-start.6 = (bf16[98,128]{1,0:T(8,128)(2,1)S(1)}, bf16[98,128]{1,0:T(8,128)(2,1)S(1)}, u32[]{:S(2)}, u32[]{:S(2)}) collective-permute-start(bf16[98,128]{1,0:T(8,128)(2,1)S(1)} %get-tuple-element.63), channel_id=1, source_target_pairs={{4,0},{8,4},{12,8},{16,12},{20,16},{24,20},{28,24},{0,28},{5,1},{9... | collective-permute-start | bytes 75272 | tf_op jit(solution)/shard_map/ppermute | solution.py:484
  23.2 4.7 %collective-permute-start.3 = (bf16[98,256]{1,0:T(8,128)(2,1)S(1)}, bf16[98,256]{1,0:T(8,128)(2,1)S(1)}, u32[]{:S(2)}, u32[]{:S(2)}) collective-permute-start(bf16[98,256]{1,0:T(8,128)(2,1)S(1)} %get-tuple-element.61.refs_0_), channel_id=1, source_target_pairs={{0,2},{1,3},{2,0},{3,1},{4,6},{5,7},{6,4},{7,5},{8,10},{9,11},{10,... | collective-permute-start | bytes 150536 | tf_op jit(solution)/shard_map/ppermute | solution.py:401
  24.7 3.2 %collective-permute-start.2 = (bf16[98,256]{1,0:T(8,128)(2,1)S(1)}, bf16[98,256]{1,0:T(8,128)(2,1)S(1)}, u32[]{:S(2)}, u32[]{:S(2)}) collective-permute-start(bf16[98,256]{1,0:T(8,128)(2,1)S(1)} %get-tuple-element.61.refs_0_), channel_id=1, source_target_pairs={{0,1},{1,0},{2,3},{3,2},{4,5},{5,4},{6,7},{7,6},{8,9},{9,8},{10,11... | collective-permute-start | bytes 150536 | tf_op jit(solution)/shard_map/ppermute | solution.py:401
  25.1 3.6 %collective-permute-start.9 = (bf16[98,256]{1,0:T(8,128)(2,1)S(1)}, bf16[98,256]{1,0:T(8,128)(2,1)S(1)}, u32[]{:S(2)}, u32[]{:S(2)}) collective-permute-start(bf16[98,256]{1,0:T(8,128)(2,1)S(1)} %shard_map.185.refs_4_), channel_id=1, source_target_pairs={{0,3},{1,2},{2,1},{3,0},{4,7},{5,6},{6,5},{7,4},{8,11},{9,10},{10,... | collective-permute-start | bytes 150536 | tf_op jit(solution)/shard_map/ppermute | solution.py:401
  25.7 4.7 %collective-permute-start.8 = (bf16[98,256]{1,0:T(8,128)(2,1)S(1)}, bf16[98,256]{1,0:T(8,128)(2,1)S(1)}, u32[]{:S(2)}, u32[]{:S(2)}) collective-permute-start(bf16[98,256]{1,0:T(8,128)(2,1)S(1)} %shard_map.185.refs_4_), channel_id=1, source_target_pairs={{0,2},{1,3},{2,0},{3,1},{4,6},{5,7},{6,4},{7,5},{8,10},{9,11},{10,... | collective-permute-start | bytes 150536 | tf_op jit(solution)/shard_map/ppermute | solution.py:401
  27.2 3.2 %collective-permute-start.7 = (bf16[98,256]{1,0:T(8,128)(2,1)S(1)}, bf16[98,256]{1,0:T(8,128)(2,1)S(1)}, u32[]{:S(2)}, u32[]{:S(2)}) collective-permute-start(bf16[98,256]{1,0:T(8,128)(2,1)S(1)} %shard_map.185.refs_4_), channel_id=1, source_target_pairs={{0,1},{1,0},{2,3},{3,2},{4,5},{5,4},{6,7},{7,6},{8,9},{9,8},{10,11... | collective-permute-start | bytes 150536 | tf_op jit(solution)/shard_map/ppermute | solution.py:401
  31.9 6.6 %collective-permute-start.10 = (bf16[98,128]{1,0:T(8,128)(2,1)S(1)}, bf16[98,128]{1,0:T(8,128)(2,1)S(1)}, u32[]{:S(2)}, u32[]{:S(2)}) collective-permute-start(bf16[98,128]{1,0:T(8,128)(2,1)S(1)} %get-tuple-element.66), channel_id=1, source_target_pairs={{0,4},{4,8},{8,12},{12,16},{16,20},{20,24},{24,28},{28,0},{1,5},{5... | collective-permute-start | bytes 75272 | tf_op jit(solution)/shard_map/ppermute | solution.py:483
  33.3 5.1 %collective-permute-start.11 = (bf16[98,128]{1,0:T(8,128)(2,1)S(1)}, bf16[98,128]{1,0:T(8,128)(2,1)S(1)}, u32[]{:S(2)}, u32[]{:S(2)}) collective-permute-start(bf16[98,128]{1,0:T(8,128)(2,1)S(1)} %get-tuple-element.67), channel_id=1, source_target_pairs={{4,0},{8,4},{12,8},{16,12},{20,16},{24,20},{28,24},{0,28},{5,1},{9... | collective-permute-start | bytes 75272 | tf_op jit(solution)/shard_map/ppermute | solution.py:484
  46.2 2.0 %collective-permute-start.12 = (bf16[16,16,1024]{2,1,0:T(8,128)(2,1)S(1)}, bf16[16,16,1024]{2,1,0:T(8,128)(2,1)S(1)}, u32[]{:S(2)}, u32[]{:S(2)}) collective-permute-start(bf16[16,16,1024]{2,1,0:T(8,128)(2,1)S(1)} %get-tuple-element.81), channel_id=1, source_target_pairs={{0,1},{1,0},{2,3},{3,2},{4,5},{5,4},{6,7},{7,6},{8,9},{9,8},{10,11... | collective-permute-start | bytes 1572872 | tf_op jit(solution)/shard_map/ppermute | solution.py:401
  46.3 3.3 %collective-permute-start.15 = (bf16[16,16,768]{2,1,0:T(8,128)(2,1)S(1)}, bf16[16,16,768]{2,1,0:T(8,128)(2,1)S(1)}, u32[]{:S(2)}, u32[]{:S(2)}) collective-permute-start(bf16[16,16,768]{2,1,0:T(8,128)(2,1)S(1)} %get-tuple-element.87), channel_id=1, source_target_pairs={{0,1},{1,0},{2,3},{3,2},{4,5},{5,4},{6,7},{7,6},{8,9},{9,8},{10,11... | collective-permute-start | bytes 1179656 | tf_op jit(solution)/shard_map/ppermute | solution.py:401
  48.3 9.2 %collective-permute-start.13 = (bf16[8,16,1024]{2,1,0:T(8,128)(2,1)S(1)}, bf16[8,16,1024]{2,1,0:T(8,128)(2,1)S(1)}, u32[]{:S(2)}, u32[]{:S(2)}) collective-permute-start(bf16[8,16,1024]{2,1,0:T(8,128)(2,1)S(1)} %get-tuple-element.83), channel_id=1, source_target_pairs={{0,2},{1,3},{2,0},{3,1},{4,6},{5,7},{6,4},{7,5},{8,10},{9,11},{10,... | collective-permute-start | bytes 786440 | tf_op jit(solution)/shard_map/ppermute | solution.py:401
  49.8 11.1 %collective-permute-start.16 = (bf16[8,16,768]{2,1,0:T(8,128)(2,1)S(1)}, bf16[8,16,768]{2,1,0:T(8,128)(2,1)S(1)}, u32[]{:S(2)}, u32[]{:S(2)}) collective-permute-start(bf16[8,16,768]{2,1,0:T(8,128)(2,1)S(1)} %get-tuple-element.89), channel_id=1, source_target_pairs={{0,2},{1,3},{2,0},{3,1},{4,6},{5,7},{6,4},{7,5},{8,10},{9,11},{10,... | collective-permute-start | bytes 589832 | tf_op jit(solution)/shard_map/ppermute | solution.py:401
  57.6 8.2 %collective-permute-start.14 = (bf16[2,32,1024]{2,1,0:T(8,128)(2,1)S(1)}, bf16[2,32,1024]{2,1,0:T(8,128)(2,1)S(1)}, u32[]{:S(2)}, u32[]{:S(2)}) collective-permute-start(bf16[2,32,1024]{2,1,0:T(8,128)(2,1)S(1)} %get-tuple-element.85), channel_id=1, source_target_pairs={{0,8},{4,12},{8,0},{12,4},{16,24},{20,28},{24,16},{28,20},{1,9},{5... | collective-permute-start | bytes 393224 | tf_op jit(solution)/shard_map/ppermute | solution.py:401
  61.2 4.7 %collective-permute-start.17 = (bf16[2,32,768]{2,1,0:T(8,128)(2,1)S(1)}, bf16[2,32,768]{2,1,0:T(8,128)(2,1)S(1)}, u32[]{:S(2)}, u32[]{:S(2)}) collective-permute-start(bf16[2,32,768]{2,1,0:T(8,128)(2,1)S(1)} %get-tuple-element.91), channel_id=1, source_target_pairs={{0,8},{4,12},{8,0},{12,4},{16,24},{20,28},{24,16},{28,20},{1,9},{5... | collective-permute-start | bytes 294920 | tf_op jit(solution)/shard_map/ppermute | solution.py:401
  66.0 15.3 %copy-start.7 = (f32[512]{0:T(512)S(1)}, f32[512]{0:T(512)}, u32[]{:S(2)}) copy-start(f32[512]{0:T(512)} %param.16) | copy-start | bytes 6148
  66.1 6.3 %collective-permute-start.18 = (bf16[2,16,1792]{2,1,0:T(8,128)(2,1)S(1)}, bf16[2,16,1792]{2,1,0:T(8,128)(2,1)S(1)}, u32[]{:S(2)}, u32[]{:S(2)}) collective-permute-start(bf16[2,16,1792]{2,1,0:T(8,128)(2,1)S(1)} %get-tuple-element.93), channel_id=1, source_target_pairs={{0,4},{4,0},{8,12},{12,8},{16,20},{20,16},{24,28},{28,24},{1,5},{5... | collective-permute-start | bytes 344072 | tf_op jit(solution)/shard_map/ppermute | solution.py:401
  66.7 14.6 %collective-permute-start.23 = (bf16[128,512]{1,0:T(8,128)(2,1)S(1)}, bf16[128,512]{1,0:T(8,128)(2,1)S(1)}, u32[]{:S(2)}, u32[]{:S(2)}) collective-permute-start(bf16[128,512]{1,0:T(8,128)(2,1)S(1)} %get-tuple-element.100), channel_id=1, source_target_pairs={{0,4},{4,8},{8,12},{12,16},{16,20},{20,24},{24,28},{28,0},{1,5},{5... | collective-permute-start | bytes 393224 | tf_op jit(solution)/shard_map/ppermute | solution.py:483
  68.1 13.2 %collective-permute-start.24 = (bf16[128,512]{1,0:T(8,128)(2,1)S(1)}, bf16[128,512]{1,0:T(8,128)(2,1)S(1)}, u32[]{:S(2)}, u32[]{:S(2)}) collective-permute-start(bf16[128,512]{1,0:T(8,128)(2,1)S(1)} %get-tuple-element.101), channel_id=1, source_target_pairs={{4,0},{8,4},{12,8},{16,12},{20,16},{24,20},{28,24},{0,28},{5,1},{9... | collective-permute-start | bytes 393224 | tf_op jit(solution)/shard_map/ppermute | solution.py:484
  72.5 6.2 %collective-permute-start.19 = (bf16[1,16,1792]{2,1,0:T(8,128)(2,1)S(1)}, bf16[1,16,1792]{2,1,0:T(8,128)(2,1)S(1)}, u32[]{:S(2)}, u32[]{:S(2)}) collective-permute-start(bf16[1,16,1792]{2,1,0:T(8,128)(2,1)S(1)} %get-tuple-element.95), channel_id=1, source_target_pairs={{0,16},{4,20},{8,24},{12,28},{16,0},{20,4},{24,8},{28,12},{1,17},{... | collective-permute-start | bytes 172040 | tf_op jit(solution)/shard_map/ppermute | solution.py:401
  78.8 4.1 %collective-permute-start.22 = (bf16[16,1792]{1,0:T(8,128)(2,1)S(1)}, bf16[16,1792]{1,0:T(8,128)(2,1)S(1)}, u32[]{:S(2)}, u32[]{:S(2)}) collective-permute-start(bf16[16,1792]{1,0:T(8,128)(2,1)S(1)} %bitcast.44), channel_id=1, source_target_pairs={{0,3},{1,2},{2,1},{3,0},{4,7},{5,6},{6,5},{7,4},{8,11},{9,10},{10,... | collective-permute-start | bytes 172040 | tf_op jit(solution)/shard_map/ppermute | solution.py:401
  78.8 5.3 %collective-permute-start.21 = (bf16[16,1792]{1,0:T(8,128)(2,1)S(1)}, bf16[16,1792]{1,0:T(8,128)(2,1)S(1)}, u32[]{:S(2)}, u32[]{:S(2)}) collective-permute-start(bf16[16,1792]{1,0:T(8,128)(2,1)S(1)} %bitcast.45), channel_id=1, source_target_pairs={{0,2},{1,3},{2,0},{3,1},{4,6},{5,7},{6,4},{7,5},{8,10},{9,11},{10,... | collective-permute-start | bytes 172040 | tf_op jit(solution)/shard_map/ppermute | solution.py:401
  80.5 3.7 %collective-permute-start.20 = (bf16[16,1792]{1,0:T(8,128)(2,1)S(1)}, bf16[16,1792]{1,0:T(8,128)(2,1)S(1)}, u32[]{:S(2)}, u32[]{:S(2)}) collective-permute-start(bf16[16,1792]{1,0:T(8,128)(2,1)S(1)} %bitcast.46), channel_id=1, source_target_pairs={{0,1},{1,0},{2,3},{3,2},{4,5},{5,4},{6,7},{7,6},{8,9},{9,8},{10,11... | collective-permute-start | bytes 172040 | tf_op jit(solution)/shard_map/ppermute | solution.py:401

commit v4 on v3

--- a/solution.py
+++ b/solution.py
@@ -114,9 +114,11 @@
 
 
 def project_kernel(
-    w_hbm, src_hbm, weight_hbm, features_ref, q_ref, kv_ref, mix_ref, w_ref, src_ref, weight_ref, sems
+    w_hbm, src_hbm, weight_hbm, edge_hbm, features_ref, q_ref, own_ref, mix_ref, w_ref,
+    src_ref, weight_ref, edge_ref, sems,
 ):
-    copies = fetch(((src_hbm, src_ref), (weight_hbm, weight_ref), (w_hbm, w_ref)), sems)
+    pairs = ((src_hbm, src_ref), (weight_hbm, weight_ref), (w_hbm, w_ref), (edge_hbm, edge_ref))
+    copies = fetch(pairs, sems)
     width = features_ref.shape[1]
     rows = iota(mix_ref.shape, 0)
     copies[0].wait()
@@ -128,12 +130,18 @@
     copies[2].wait()
     qkv = nn(features_ref[...], w_ref[...]).astype(BF16)
     q_ref[...] = qkv[:, :width]
-    kv_ref[...] = qkv[:, width:]
+    key_value = qkv[:, width:]
+    copies[3].wait()
+    nodes = features_ref.shape[0]
+    sources = edge_ref[...].astype(F32).T
+    slot = iota((nodes, nodes), 1).astype(F32)
+    for e in range(own_ref.shape[0]):
+        own_ref[e] = nn(ones_where(slot == sources[:, e : e + 1]), key_value).astype(BF16)
 
 
 def attend_kernel(
-    w_out_hbm, bias_hbm, dec_hbm, count_ref, hidden_ref, left_ref, right_ref, q_ref, kv_ref, w_ref,
-    src_ref, border_ref, out_ref, projected_ref, head_ref, tail_ref, probs_ref, attended_ref, keys_ref, values_ref, table_ref,
+    w_out_hbm, bias_hbm, dec_hbm, count_ref, hidden_ref, left_ref, right_ref, q_ref, own_ref, w_ref,
+    src_ref, border_ref, out_ref, projected_ref, head_ref, tail_ref, probs_ref, attended_ref, keys_ref, values_ref, shares_ref, table_ref,
     w_out_ref, bias_ref, dec_ref, sems,
 ):
     copies = fetch(((bias_hbm, bias_ref), (w_out_hbm, w_out_ref), (dec_hbm, dec_ref)), sems)
@@ -144,18 +152,17 @@
     sources = src_ref[...].astype(F32).T
     head_size = width // (columns // edges)
     w_kv = w_ref[:, width:]
-    table_ref[:nodes] = kv_ref[...]
-    table_ref[nodes : nodes + rim] = nn(left_ref[...], w_kv).astype(BF16)
-    table_ref[nodes + rim :] = nn(right_ref[...], w_kv).astype(BF16)
+    table_ref[:rim] = nn(left_ref[...], w_kv).astype(BF16)
+    table_ref[rim:] = nn(right_ref[...], w_kv).astype(BF16)
     table = table_ref[...]
     queries = q_ref[...].astype(F32)
     squeeze = head_map(width, columns, head_size, edges)
     expand = head_map(columns, width, edges, head_size)
     lane = iota((nodes, columns), 1) & (edges - 1)
-    slot = iota((nodes, table.shape[0]), 1).astype(F32)
+    slot = (iota((nodes, table.shape[0]), 1) + nodes).astype(F32)
     scores = jnp.zeros((nodes, columns), F32)
     for e in range(edges):
-        rows = nn(ones_where(slot == sources[:, e : e + 1]), table)
+        rows = nn(ones_where(slot == sources[:, e : e + 1]), table) + own_ref[e].astype(F32)
         keys_ref[e] = rows[:, :width].astype(BF16)
         values_ref[e] = rows[:, width:].astype(BF16)
         part = nn((queries * rows[:, :width]).astype(BF16), squeeze)
@@ -168,6 +175,7 @@
     total = jnp.zeros((nodes, width), F32)
     for e in range(edges):
         share = nn(jnp.where(lane == e, probs, 0.0).astype(BF16), expand)
+        shares_ref[e] = share.astype(BF16)
         total += share * values_ref[e].astype(F32)
     attended = total.astype(BF16)
     attended_ref[...] = attended
@@ -259,14 +267,12 @@
 
 def value_back_kernel(
     count_ref, own_ref, from_left_ref, from_right_ref, border_ref, node_out_ref, w_dec_ref,
-    attended_ref, w_out_ref, probs_ref, hot_ref, features_ref, left_ref, right_ref, loss_ref,
+    attended_ref, w_out_ref, shares_ref, hot_ref, features_ref, left_ref, right_ref, loss_ref,
     grad_ref, mixed_ref, grad_value_ref, send_ref, keep_ref, edge_ref, full_ref,
 ):
     nodes, width = grad_ref.shape
     rim = left_ref.shape[0]
-    columns = probs_ref.shape[1]
-    edges = hot_ref.shape[1] // nodes
-    head_size = width // (columns // edges)
+    edges = shares_ref.shape[0]
     returned = jnp.concatenate([from_left_ref[...], from_right_ref[...]], axis=1)
     columns_grad = own_ref[...] + nt(returned, border_map(border_ref, nodes))
     live = iota(columns_grad.shape, 1) < count_ref[...]
@@ -277,12 +283,8 @@
     mixed = nt(rounded, w_out_ref[...]).astype(BF16)
     mixed_ref[...] = mixed
     mixed = mixed.astype(F32)
-    expand = head_map(columns, width, edges, head_size)
-    lane = iota((nodes, columns), 1) & (edges - 1)
-    probs = probs_ref[...]
     for e in range(edges):
-        share = nn(jnp.where(lane == e, probs, 0.0).astype(BF16), expand)
-        edge_ref[e * nodes : (e + 1) * nodes, :] = (share * mixed).astype(BF16)
+        edge_ref[e * nodes : (e + 1) * nodes, :] = (shares_ref[e].astype(F32) * mixed).astype(BF16)
     grad_value = nn(hot_ref[...], edge_ref[...]).astype(BF16)
     grad_value_ref[...] = grad_value
     features = features_ref[...]
@@ -378,17 +380,36 @@
         keep_ref[i] = joined(keep_in_ref[i, mine], arrived_ref[i, mine], variables)
 
 
-def merge_kernel(
-    query_keep_ref, query_in_ref, value_keep_ref, value_in_ref, send_ref, keep_ref, *, axis, bit, variables
+def part_kernel(
+    keep_a_ref, in_a_ref, keep_b_ref, in_b_ref,
+    query_send_ref, query_keep_ref, key_send_ref, key_keep_ref, *, steps,
 ):
+    width = query_send_ref.shape[-1]
+    cases = (
+        (steps[0], keep_a_ref, in_a_ref, query_send_ref, query_keep_ref, slice(0, width)),
+        (steps[1], keep_b_ref, in_b_ref, key_send_ref, key_keep_ref, slice(width, 2 * width)),
+    )
+    for (axis, bit), keep_in_ref, in_ref, send_ref, keep_ref, columns in cases:
+        mine = bit_of(axis, bit)
+        for at, out_ref in ((1 - mine, send_ref), (mine, keep_ref)):
+            for i in range(send_ref.shape[0]):
+                total = joined(keep_in_ref[i, at, :, columns], in_ref[i, at, :, columns], None)
+                out_ref[i] = total.astype(out_ref.dtype)
+
+
+def merge_kernel(*refs, axis, bit, variables):
+    send_ref, keep_ref = refs[-2:]
+    chains = [refs[i : i + 2] for i in range(0, len(refs) - 2, 2)]
     mine = bit_of(axis, bit)
-    start = query_keep_ref.shape[-1]
     for at, out_ref in ((1 - mine, send_ref), (mine, keep_ref)):
         for i in range(send_ref.shape[0]):
-            query = joined(query_keep_ref[i, at], query_in_ref[i, at], None)
-            value = joined(value_keep_ref[i, at], value_in_ref[i, at], variables)
-            out_ref[i, :, :start] = query.astype(out_ref.dtype)
-            out_ref[i, :, start:] = value.astype(out_ref.dtype)
+            start = 0
+            for n, (keep_in_ref, in_ref) in enumerate(chains):
+                total = joined(
+                    keep_in_ref[i, at], in_ref[i, at], variables if n + 1 == len(chains) else None
+                )
+                out_ref[i, :, start : start + total.shape[-1]] = total.astype(out_ref.dtype)
+                start += total.shape[-1]
 
 
 def total_kernel(keep_ref, arrived_ref, sum_ref, *, variables):
@@ -528,27 +549,31 @@
         mib=4,
     )
     left, right = swap_rims(head, tail)
-    queries, own_kv, mix, w_qkv = on_core(
+    queries, own_edges, mix, w_qkv = on_core(
         project_kernel,
         [
-            ((nodes, width), BF16), ((nodes, 2 * width), BF16), ((table_rows, points), BF16),
+            ((nodes, width), BF16), ((edges, nodes, 2 * width), BF16), ((table_rows, points), BF16),
             ((width, 3 * width), BF16),
         ],
-        w_qkv, dec_source, dec_weight, features,
-        fetched=3,
-        scratch=[pltpu.VMEM(dec_source.shape, jnp.int32), pltpu.VMEM(dec_weight.shape, F32)],
+        w_qkv, dec_source, dec_weight, sources, features,
+        fetched=4,
+        scratch=[
+            pltpu.VMEM(dec_source.shape, jnp.int32), pltpu.VMEM(dec_weight.shape, F32),
+            pltpu.VMEM((edges, nodes), jnp.int32),
+        ],
+        mib=12,
     )
     edge_rows = ((edges, nodes, width), BF16)
-    node_out, projected, head, tail, probs, attended, keys, values = on_core(
+    node_out, projected, head, tail, probs, attended, keys, values, shares = on_core(
         attend_kernel,
         [
             ((nodes, width), BF16), ((variables, nodes), BF16), rim_columns, rim_columns,
-            ((nodes, columns), F32), ((nodes, width), BF16), edge_rows, edge_rows,
+            ((nodes, columns), F32), ((nodes, width), BF16), edge_rows, edge_rows, edge_rows,
         ],
-        w_out, edge_bias, w_decoder, count, hidden, left, right, queries, own_kv, w_qkv, sources, boundary,
+        w_out, edge_bias, w_decoder, count, hidden, left, right, queries, own_edges, w_qkv, sources, boundary,
         fetched=3,
         scratch=[
-            pltpu.VMEM((table_rows, 2 * width), BF16), pltpu.VMEM((width, width), BF16),
+            pltpu.VMEM((2 * rim, 2 * width), BF16), pltpu.VMEM((width, width), BF16),
             pltpu.VMEM((nodes, columns), F32), pltpu.VMEM((variables, width), BF16),
         ],
         mib=16,
@@ -584,7 +609,7 @@
         [((nodes, width), F32), ((nodes, width), BF16), ((table_rows, width), BF16)]
         + halves(width + 2 * LANES),
         count, grad_own, back_left, back_right, boundary, node_out, w_decoder,
-        attended, w_out, probs, hot, features, left, right, loss,
+        attended, w_out, shares, hot, features, left, right, loss,
         scratch=[pltpu.VMEM((edges * nodes, width), BF16), whole(width + 2 * LANES)],
         mib=16,
     )
@@ -615,18 +640,31 @@
 
     around = [("region", 1 << b) for b in range(shift_of(regions))]
     around[:2] = around[1::-1]
-    value_sum, query_sum = Halving(regions, members, rows), Halving(regions, members, rows)
-    value_keep, value_in = value_sum.run(value_send, value_keep, core + across + around[:1], variables)
-    query_keep, query_in = query_sum.run(query_send, query_keep, core + across + around[:1], None)
+    value_sum, query_sum, key_sum = (Halving(regions, members, rows) for _ in range(3))
+    value_parts = value_sum.run(value_send, value_keep, core + across + around[:1], variables)
+    for chain in (query_sum, key_sum):
+        chain.left.remove(core[0])
+    steps = (across[0], around[0])
+    arrived = swapped(query_send, *core[0])
+    parts, views = [], []
+    for chain, step in zip((query_sum, key_sum), steps):
+        half, _ = chain.half(step, width)
+        _, both = chain.half(step, 2 * width)
+        parts += [(half, BF16), (half, F32)]
+        views += [query_keep.reshape(both), arrived.reshape(both)]
+    parts = on_core(functools.partial(part_kernel, steps=steps), parts, *views)
+    query_parts = query_sum.run(*parts[:2], across + around[:1], None)
+    key_parts = key_sum.run(*parts[2:], around[:1] + across, None)
     packed = 3 * width + 2 * LANES
     half, _ = value_sum.half(around[1], packed)
-    _, both_values = value_sum.half(around[1], width + 2 * LANES)
-    _, both_queries = value_sum.half(around[1], 2 * width)
+    views = []
+    for chain in (query_parts, key_parts, value_parts):
+        _, both = value_sum.half(around[1], chain[0].shape[-1])
+        views += [part.reshape(both) for part in chain]
     send, keep = on_core(
         functools.partial(merge_kernel, axis=around[1][0], bit=around[1][1], variables=variables),
         [(half, BF16), (half, F32)],
-        query_keep.reshape(both_queries), query_in.reshape(both_queries),
-        value_keep.reshape(both_values), value_in.reshape(both_values),
+        *views,
     )
     keep, arrived = value_sum.run(send, keep, around[1:], variables)
     piece = (1, rows, packed)

time: 85.3 us -> 82.4 us (0.966)
  waiting for transfers between devices: 26.1 us -> 21.7 us
  starting transfers between devices: 34.3 us -> 35.6 us
    ppermute x17 -> x19, waiting for transfers between devices: 23.5 us -> 20.4 us  [swapped(): return lax.ppermute(array, axis, [(i, i ^ bit) for i in range(count)])]
    ppermute x4, starting transfers between devices: 14.4 us -> 15.8 us  [swap_rims(): lax.ppermute(head, 'region', [((i + 1) % count, i) for i in range(count)])]
    ppermute x4, starting transfers between devices: 6.31 us -> 5.02 us  [swap_rims(): lax.ppermute(tail, 'region', [(i, (i + 1) % count) for i in range(count)])]
    ppermute x17 -> x19, starting transfers between devices: 13.6 us -> 14.7 us  [swapped(): return lax.ppermute(array, axis, [(i, i ^ bit) for i in range(count)])]
    pallas_call x20 -> x21, Pallas kernels: 23.1 us -> 23.2 us  [on_core(): pl.pallas_call(kernel, out_shape=[jax.ShapeDtypeStruct(s, d) for s, d in...]
  transfers between devices with their start and end apart: 25 -> 27, of which waited for: 15 -> 15; matrix products, arithmetic and copies ran while one was open for 0% -> 0% of each run, Pallas kernels for 7% -> 9%
where the time goes in v4:
time: 82.4 us; the launch traced here: 82.1 us
  starting transfers between devices  35.6 us (43%)
  Pallas kernels  23.2 us (28%)
  waiting for transfers between devices  21.7 us (26%)
  between operations  1.58 us (2%)
    pallas_call x21, Pallas kernels, on_core(): pl.pallas_call(kernel, out_shape=[jax.ShapeDtypeStruct(s, d) for s, d in...  23.2 us
    ppermute x19, waiting for transfers between devices, swapped(): return lax.ppermute(array, axis, [(i, i ^ bit) for i in range(count)])  20.4 us
    ppermute x4, starting transfers between devices, swap_rims(): lax.ppermute(head, 'region', [((i + 1) % count, i) for i in range(count)])  15.8 us
    ppermute x19, starting transfers between devices, swapped(): return lax.ppermute(array, axis, [(i, i ^ bit) for i in range(count)])  14.7 us
    ppermute x4, starting transfers between devices, swap_rims(): lax.ppermute(tail, 'region', [(i, (i + 1) % count) for i in range(count)])  5.02 us
  transfers between devices with their start and end apart: 27, of which 15 were waited for; matrix products, arithmetic and copies ran while one was open for 0% of the time, Pallas kernels for 9%

profile of v4, /device:TPU:0, one launch (start us, length us, event | category | flops | bytes accessed | tf_op | source)
XLA Modules:
  0.0 82.1 jit_solution(16990524077803530659)
XLA Ops:
  0.7 1.5 %shard_map.182 = (bf16[256,512]{1,0:T(8,128)(2,1)S(1)}, bf16[128,512]{1,0:T(8,128)(2,1)S(1)}, bf16[128,512]{1,0:T(8,128)(2,1)S(1)}) custom-call(bf16[256,512]{1,0:T(8,128)(2,1)} %bitcast.37, f32[1,512]{1,0:T(1,128)} %bitcast.68, s32[1,256]{1,0:T(1,128)} %border_ref.5), custom_call_target="tpu_custom_call" | custom-call | tf_op jit(solution)/shard_map/pallas_call | solution.py:34
  2.1 3.0 %collective-permute-start = (bf16[128,512]{1,0:T(8,128)(2,1)S(1)}, bf16[128,512]{1,0:T(8,128)(2,1)S(1)}, u32[]{:S(2)}, u32[]{:S(2)}) collective-permute-start(bf16[128,512]{1,0:T(8,128)(2,1)S(1)} %get-tuple-element.60), channel_id=1, source_target_pairs={{0,4},{4,8},{8,12},{12,16},{16,20},{20,24},{24,28},{28,0},{1,5},{5... | collective-permute-start | bytes 393224 | tf_op jit(solution)/shard_map/ppermute | solution.py:504
  5.2 3.1 %collective-permute-start.1 = (bf16[128,512]{1,0:T(8,128)(2,1)S(1)}, bf16[128,512]{1,0:T(8,128)(2,1)S(1)}, u32[]{:S(2)}, u32[]{:S(2)}) collective-permute-start(bf16[128,512]{1,0:T(8,128)(2,1)S(1)} %get-tuple-element.61), channel_id=1, source_target_pairs={{4,0},{8,4},{12,8},{16,12},{20,16},{24,20},{28,24},{0,28},{5,1},{9... | collective-permute-start | bytes 393224 | tf_op jit(solution)/shard_map/ppermute | solution.py:505
  9.0 3.6 %shard_map.183 = (bf16[256,512]{1,0:T(8,128)(2,1)S(1)}, bf16[8,256,1024]{2,1,0:T(8,128)(2,1)S(1)}, bf16[512,1024]{1,0:T(8,128)(2,1)S(1)}, bf16[512,1536]{1,0:T(8,128)(2,1)S(1)}) custom-call(bf16[512,1536]{1,0:T(8,128)(2,1)} %w_hbm.1, s32[3,1024]{1,0:T(4,128)} %src_hbm.1, f32[3,1024]{1,0:T(4,128)} %weight_hbm.1, s32[8,256]{1,0:T(8,128)} %bitcast.63, ...), custom_call_target="tpu_custom_call" | custom-call | tf_op jit(solution)/shard_map/pallas_call | solution.py:34
  12.6 0.4 collective-permute-done.1.right_ref
  13.0 4.4 %shard_map.184 = (bf16[256,512]{1,0:T(8,128)(2,1)S(1)}, bf16[98,256]{1,0:T(8,128)(2,1)S(1)}, bf16[98,128]{1,0:T(8,128)(2,1)S(1)}, bf16[98,128]{1,0:T(8,128)(2,1)...) custom-call(bf16[512,512]{1,0:T(8,128)(2,1)} %w_out_ref.1, ...), custom_call_target="tpu_custom_call" | custom-call | tf_op jit(solution)/shard_map/pallas_call | solution.py:34
  17.4 0.4 collective-permute-start.4
  17.9 4.7 %collective-permute-start.6 = (bf16[98,128]{1,0:T(8,128)(2,1)S(1)}, bf16[98,128]{1,0:T(8,128)(2,1)S(1)}, u32[]{:S(2)}, u32[]{:S(2)}) collective-permute-start(bf16[98,128]{1,0:T(8,128)(2,1)S(1)} %get-tuple-element.68), channel_id=1, source_target_pairs={{4,0},{8,4},{12,8},{16,12},{20,16},{24,20},{28,24},{0,28},{5,1},{9... | collective-permute-start | bytes 75272 | tf_op jit(solution)/shard_map/ppermute | solution.py:505
  22.5 1.3 %collective-permute-start.3 = (bf16[98,256]{1,0:T(8,128)(2,1)S(1)}, bf16[98,256]{1,0:T(8,128)(2,1)S(1)}, u32[]{:S(2)}, u32[]{:S(2)}) collective-permute-start(bf16[98,256]{1,0:T(8,128)(2,1)S(1)} %get-tuple-element.66.refs_0_), channel_id=1, source_target_pairs={{0,2},{1,3},{2,0},{3,1},{4,6},{5,7},{6,4},{7,5},{8,10},{9,11},{10,... | collective-permute-start | bytes 150536 | tf_op jit(solution)/shard_map/ppermute | solution.py:422
  23.8 0.6 collective-permute-done.5.left_ref
  24.4 0.4 collective-permute-start.9
  24.7 1.5 %collective-permute-start.8 = (bf16[98,256]{1,0:T(8,128)(2,1)S(1)}, bf16[98,256]{1,0:T(8,128)(2,1)S(1)}, u32[]{:S(2)}, u32[]{:S(2)}) collective-permute-start(bf16[98,256]{1,0:T(8,128)(2,1)S(1)} %shard_map.185.refs_4_), channel_id=1, source_target_pairs={{0,2},{1,3},{2,0},{3,1},{4,6},{5,7},{6,4},{7,5},{8,10},{9,11},{10,... | collective-permute-start | bytes 150536 | tf_op jit(solution)/shard_map/ppermute | solution.py:422
  26.3 0.7 collective-permute-done.3.refs_2_
  27.0 1.2 %collective-permute-done.9.refs_7_ = bf16[98,256]{1,0:T(8,128)(2,1)S(1)} collective-permute-done((bf16[98,256]{1,0:T(8,128)(2,1)S(1)}, bf16[98,256]{1,0:T(8,128)(2,1)S(1)}, u32[]{:S(2)}, u32[]{:S(2)}) %collective-permute-start.9) | collective-permute-done | bytes 50208 | tf_op jit(solution)/shard_map/ppermute | solution.py:422
  28.2 1.5 %collective-permute-done.8.refs_6_ = bf16[98,256]{1,0:T(8,128)(2,1)S(1)} collective-permute-done((bf16[98,256]{1,0:T(8,128)(2,1)S(1)}, bf16[98,256]{1,0:T(8,128)(2,1)S(1)}, u32[]{:S(2)}, u32[]{:S(2)}) %collective-permute-start.8) | collective-permute-done | bytes 50208 | tf_op jit(solution)/shard_map/ppermute | solution.py:422
  29.7 1.5 %shard_map.186 = (bf16[98,1024]{1,0:T(8,128)(2,1)S(1)}, bf16[98,128]{1,0:T(8,128)(2,1)S(1)}, bf16[98,128]{1,0:T(8,128)(2,1)S(1)}, f32[1,128]{1,0:T(1,128)S(1)}) custom-call(f32[98,1024]{1,0:T(8,128)S(1)} %copy-done.3, f32[98,1024]{1,0:T(8,128)S(1)} %copy-done.4, f32[1,1024]{1,0:T(1,128)S(1)} %bitcast.70, f32[1,98]{1,0:T(1,128)S(1)} %bitcast.71, ...), custom_call_target="tpu_custom_call" | custom-call | tf_op jit(solution)/shard_map/pallas_call | solution.py:34
  31.2 1.2 %collective-permute-start.10 = (bf16[98,128]{1,0:T(8,128)(2,1)S(1)}, bf16[98,128]{1,0:T(8,128)(2,1)S(1)}, u32[]{:S(2)}, u32[]{:S(2)}) collective-permute-start(bf16[98,128]{1,0:T(8,128)(2,1)S(1)} %get-tuple-element.71), channel_id=1, source_target_pairs={{0,4},{4,8},{8,12},{12,16},{16,20},{20,24},{24,28},{28,0},{1,5},{5... | collective-permute-start | bytes 75272 | tf_op jit(solution)/shard_map/ppermute | solution.py:504
  32.4 4.0 %collective-permute-start.11 = (bf16[98,128]{1,0:T(8,128)(2,1)S(1)}, bf16[98,128]{1,0:T(8,128)(2,1)S(1)}, u32[]{:S(2)}, u32[]{:S(2)}) collective-permute-start(bf16[98,128]{1,0:T(8,128)(2,1)S(1)} %get-tuple-element.72), channel_id=1, source_target_pairs={{4,0},{8,4},{12,8},{16,12},{20,16},{24,20},{28,24},{0,28},{5,1},{9... | collective-permute-start | bytes 75272 | tf_op jit(solution)/shard_map/ppermute | solution.py:505
  36.5 1.1 %shard_map.187 = (f32[98,256]{1,0:T(8,128)S(1)}, bf16[512,2048]{1,0:T(8,128)(2,1)S(1)}) custom-call(bf16[512,1024]{1,0:T(8,128)(2,1)S(1)} %get-tuple-element.62.mix_ref, bf16[98,1024]{1,0:T(8,128)(2,1)S(1)} %get-tuple-element.69.grad_ref, s32[8,256]{1,0:T(8,128)S(1)} %bitcast.65), custom_call_target="tpu_custom_call" | custom-call | tf_op jit(solution)/shard_map/pallas_call | solution.py:34
  37.6 0.5 collective-permute-done.10.from_left_ref
  38.1 2.9 %shard_map.188 = (f32[256,512]{1,0:T(8,128)S(1)}, bf16[256,512]{1,0:T(8,128)(2,1)S(1)}, bf16[512,512]{1,0:T(8,128)(2,1)S(1)}, bf16[16,16,768]{2,1,0:T(8,128)(2,1)S(1)}, f32[16,16,768]{2,1,0:T(8,128)S(1)}) custom-call(s32[1,1]{1,0:T(1,128)} %bitcast.34.count_ref, f32[98,256]{1,0:T(8,128)S(1)} %get-tuple-element.70.own_ref, ...), custom_call_target="tpu_custom_call" | custom-call | tf_op jit(solution)/shard_map/pallas_call | solution.py:34
  41.0 1.9 %shard_map.189 = (bf16[256,512]{1,0:T(8,128)(2,1)S(1)}, bf16[2048,512]{1,0:T(8,128)(2,1)S(1)}) custom-call(bf16[256,512]{1,0:T(8,128)(2,1)S(1)} %get-tuple-element.78.mixed_ref, f32[256,128]{1,0:T(8,128)S(1)} %get-tuple-element.79.probs_ref, bf16[8,256,512]{2,1,0:T(8,128)(2,1)S(1)} %get-tuple-element.80.values_ref, ...), custom_call_target="tpu_custom_call" | custom-call | tf_op jit(solution)/shard_map/pallas_call | solution.py:34
  42.9 1.5 %shard_map.190 = (bf16[512,512]{1,0:T(8,128)(2,1)S(1)}, bf16[128,512]{1,0:T(8,128)(2,1)S(1)}, bf16[128,512]{1,0:T(8,128)(2,1)S(1)}) custom-call(bf16[2048,512]{1,0:T(8,128)(2,1)S(1)} %get-tuple-element.83.edge_ref, bf16[512,2048]{1,0:T(8,128)(2,1)S(1)} %get-tuple-element.76.hot_ref, bf16[512,512]{1,0:T(8,128)(2,1)S(1)} %get-tuple-element.84.grad_value_ref, ...), custom_call_target="tpu_custom_call" | custom-call | tf_op jit(solution)/shard_map/pallas_call | solution.py:34
  44.4 1.0 %shard_map.191 = (bf16[16,16,1024]{2,1,0:T(8,128)(2,1)S(1)}, f32[16,16,1024]{2,1,0:T(8,128)S(1)}) custom-call(bf16[256,512]{1,0:T(8,128)(2,1)S(1)} %get-tuple-element.59.features_ref, bf16[128,512]{1,0:T(8,128)(2,1)S(1)} %collective-permute-done.left_ref, bf16[128,512]{1,0:T(8,128)(2,1)S(1)} %collective-permute-done.1.right_ref, ...), custom_call_target="tpu_custom_call" | custom-call | tf_op jit(solution)/shard_map/pallas_call | solution.py:34
  45.5 0.5 collective-permute-start.17
  46.0 2.0 %collective-permute-done.17 = bf16[16,16,768]{2,1,0:T(8,128)(2,1)S(1)} collective-permute-done((bf16[16,16,768]{2,1,0:T(8,128)(2,1)S(1)}, bf16[16,16,768]{2,1,0:T(8,128)(2,1)S(1)}, u32[]{:S(2)}, u32[]{:S(2)}) %collective-permute-start.17) | collective-permute-done | bytes 393248 | tf_op jit(solution)/shard_map/ppermute | solution.py:422
  48.0 0.2 shard_map.195
  48.2 0.7 collective-permute-start.18
  49.1 1.4 %collective-permute-start.13 = (bf16[8,16,512]{2,1,0:T(8,128)(2,1)S(1)}, bf16[8,16,512]{2,1,0:T(8,128)(2,1)S(1)}, u32[]{:S(2)}, u32[]{:S(2)}) collective-permute-start(bf16[8,16,512]{2,1,0:T(8,128)(2,1)S(1)} %get-tuple-element.89), channel_id=1, source_target_pairs={{0,2},{1,3},{2,0},{3,1},{4,6},{5,7},{6,4},{7,5},{8,10},{9,11},{10,... | collective-permute-start | bytes 393224 | tf_op jit(solution)/shard_map/ppermute | solution.py:422
  50.5 5.6 %collective-permute-done.18 = bf16[8,16,768]{2,1,0:T(8,128)(2,1)S(1)} collective-permute-done((bf16[8,16,768]{2,1,0:T(8,128)(2,1)S(1)}, bf16[8,16,768]{2,1,0:T(8,128)(2,1)S(1)}, u32[]{:S(2)}, u32[]{:S(2)}) %collective-permute-start.18) | collective-permute-done | bytes 196640 | tf_op jit(solution)/shard_map/ppermute | solution.py:422
  56.3 1.7 %collective-permute-done.13 = bf16[8,16,512]{2,1,0:T(8,128)(2,1)S(1)} collective-permute-done((bf16[8,16,512]{2,1,0:T(8,128)(2,1)S(1)}, bf16[8,16,512]{2,1,0:T(8,128)(2,1)S(1)}, u32[]{:S(2)}, u32[]{:S(2)}) %collective-permute-start.13) | collective-permute-done | bytes 131104 | tf_op jit(solution)/shard_map/ppermute | solution.py:422
  58.1 0.4 collective-permute-start.14
  58.5 0.7 collective-permute-start.16
  59.2 2.4 %collective-permute-done.19 = bf16[2,32,768]{2,1,0:T(8,128)(2,1)S(1)} collective-permute-done((bf16[2,32,768]{2,1,0:T(8,128)(2,1)S(1)}, bf16[2,32,768]{2,1,0:T(8,128)(2,1)S(1)}, u32[]{:S(2)}, u32[]{:S(2)}) %collective-permute-start.19) | collective-permute-done | bytes 98336 | tf_op jit(solution)/shard_map/ppermute | solution.py:422
  61.6 0.8 collective-permute-done.14
  62.4 0.4 collective-permute-done.16
  63.0 1.4 %collective-permute-start.20 = (bf16[2,16,1792]{2,1,0:T(8,128)(2,1)S(1)}, bf16[2,16,1792]{2,1,0:T(8,128)(2,1)S(1)}, u32[]{:S(2)}, u32[]{:S(2)}) collective-permute-start(bf16[2,16,1792]{2,1,0:T(8,128)(2,1)S(1)} %get-tuple-element.103), channel_id=1, source_target_pairs={{0,4},{4,0},{8,12},{12,8},{16,20},{20,16},{24,28},{28,24},{1,5},{5... | collective-permute-start | bytes 344072 | tf_op jit(solution)/shard_map/ppermute | solution.py:422
  64.4 0.7 collective-permute-start.25
  65.1 4.0 %collective-permute-start.26 = (bf16[128,512]{1,0:T(8,128)(2,1)S(1)}, bf16[128,512]{1,0:T(8,128)(2,1)S(1)}, u32[]{:S(2)}, u32[]{:S(2)}) collective-permute-start(bf16[128,512]{1,0:T(8,128)(2,1)S(1)} %get-tuple-element.111), channel_id=1, source_target_pairs={{4,0},{8,4},{12,8},{16,12},{20,16},{24,20},{28,24},{0,28},{5,1},{9... | collective-permute-start | bytes 393224 | tf_op jit(solution)/shard_map/ppermute | solution.py:505
  69.1 0.8 collective-permute-done.20
  70.1 4.0 %collective-permute-start.21 = (bf16[1,16,1792]{2,1,0:T(8,128)(2,1)S(1)}, bf16[1,16,1792]{2,1,0:T(8,128)(2,1)S(1)}, u32[]{:S(2)}, u32[]{:S(2)}) collective-permute-start(bf16[1,16,1792]{2,1,0:T(8,128)(2,1)S(1)} %get-tuple-element.105), channel_id=1, source_target_pairs={{0,16},{4,20},{8,24},{12,28},{16,0},{20,4},{24,8},{28,12},{1,17},{... | collective-permute-start | bytes 172040 | tf_op jit(solution)/shard_map/ppermute | solution.py:422
  74.1 2.2 %collective-permute-done.21.arrived_ref = bf16[1,16,1792]{2,1,0:T(8,128)(2,1)S(1)} collective-permute-done((bf16[1,16,1792]{2,1,0:T(8,128)(2,1)S(1)}, bf16[1,16,1792]{2,1,0:T(8,128)(2,1)S(1)}, u32[]{:S(2)}, u32[]{:S(2)}) %collective-permute-start.21) | collective-permute-done | bytes 57376 | tf_op jit(solution)/shard_map/ppermute | solution.py:422
  76.4 0.7 collective-permute-start.23
  77.1 1.2 %collective-permute-start.22 = (bf16[16,1792]{1,0:T(8,128)(2,1)S(1)}, bf16[16,1792]{1,0:T(8,128)(2,1)S(1)}, u32[]{:S(2)}, u32[]{:S(2)}) collective-permute-start(bf16[16,1792]{1,0:T(8,128)(2,1)S(1)} %bitcast.53), channel_id=1, source_target_pairs={{0,1},{1,0},{2,3},{3,2},{4,5},{5,4},{6,7},{7,6},{8,9},{9,8},{10,11... | collective-permute-start | bytes 172040 | tf_op jit(solution)/shard_map/ppermute | solution.py:422
  78.3 0.6 shard_map.201.own_ref
  78.9 1.2 %shard_map.202 = bf16[256,512]{1,0:T(8,128)(2,1)} custom-call(bf16[256,512]{1,0:T(8,128)(2,1)S(1)} %bitcast.39, f32[1,512]{1,0:T(1,128)S(1)} %bitcast.69, f32[256,512]{1,0:T(8,128)S(1)} %shard_map.201.own_ref, bf16[128,512]{1,0:T(8,128)(2,1)S(1)} %collective-permute-done.25.from_left_ref, bf16[128,512]{1,0:T(8,128)(2,1)S(1)} %collective-permute-done.26.from_right_ref, ...), custom_call_target="tpu_custom_call" | custom-call | tf_op jit(solution)/shard_map/pallas_call | solution.py:34
  80.1 1.2 %collective-permute-done.23.refs_2_ = bf16[16,1792]{1,0:T(8,128)(2,1)S(1)} collective-permute-done((bf16[16,1792]{1,0:T(8,128)(2,1)S(1)}, bf16[16,1792]{1,0:T(8,128)(2,1)S(1)}, u32[]{:S(2)}, u32[]{:S(2)}) %collective-permute-start.23) | collective-permute-done | bytes 57376 | tf_op jit(solution)/shard_map/ppermute | solution.py:422
  81.2 0.9 %shard_map.200 = (f32[4,16,1536]{2,1,0:T(8,128)}, f32[4,16,512]{2,1,0:T(8,128)}, f32[4,16,98]{2,1,0:T(8,128)}, f32[1,1]{1,0:T(1,128)}) custom-call(bf16[98,512]{1,0:T(8,128)(2,1)S(1)} %bitcast.44, bf16[16,1792]{1,0:T(8,128)(2,1)S(1)} %bitcast.54, bf16[16,1792]{1,0:T(8,128)(2,1)S(1)} %collective-permute-done.22.refs_1_, ...), custom_call_target="tpu_custom_call" | custom-call | tf_op jit(solution)/shard_map/pallas_call | solution.py:34
  (47 shorter events, 1.2 us)
Async XLA Ops:
  0.6 12.3 %copy-start.6 = (s32[1,256]{1,0:T(1,128)S(1)}, s32[1,256]{1,0:T(1,128)}, u32[]{:S(2)}) copy-start(s32[1,256]{1,0:T(1,128)} %border_ref.5) | copy-start | bytes 3076
  0.6 12.3 %copy-start = (bf16[1,256,512]{2,1,0:T(8,128)(2,1)S(1)}, bf16[1,256,512]{2,1,0:T(8,128)(2,1)}, u32[]{:S(2)}) copy-start(bf16[1,256,512]{2,1,0:T(8,128)(2,1)} %param.15) | copy-start | bytes 786436
  0.7 12.3 %copy-start.5 = (s32[256,8]{0,1:T(8,128)S(1)}, s32[256,8]{0,1:T(8,128)}, u32[]{:S(2)}) copy-start(s32[256,8]{0,1:T(8,128)} %param.20) | copy-start | bytes 24580
  2.1 10.4 %collective-permute-start = (bf16[128,512]{1,0:T(8,128)(2,1)S(1)}, bf16[128,512]{1,0:T(8,128)(2,1)S(1)}, u32[]{:S(2)}, u32[]{:S(2)}) collective-permute-start(bf16[128,512]{1,0:T(8,128)(2,1)S(1)} %get-tuple-element.60), channel_id=1, source_target_pairs={{0,4},{4,8},{8,12},{12,16},{16,20},{20,24},{24,28},{28,0},{1,5},{5... | collective-permute-start | bytes 393224 | tf_op jit(solution)/shard_map/ppermute | solution.py:504
  5.2 7.8 %collective-permute-start.1 = (bf16[128,512]{1,0:T(8,128)(2,1)S(1)}, bf16[128,512]{1,0:T(8,128)(2,1)S(1)}, u32[]{:S(2)}, u32[]{:S(2)}) collective-permute-start(bf16[128,512]{1,0:T(8,128)(2,1)S(1)} %get-tuple-element.61), channel_id=1, source_target_pairs={{4,0},{8,4},{12,8},{16,12},{20,16},{24,20},{28,24},{0,28},{5,1},{9... | collective-permute-start | bytes 393224 | tf_op jit(solution)/shard_map/ppermute | solution.py:505
  13.0 16.7 %copy-start.3 = (f32[98,1024]{1,0:T(8,128)S(1)}, f32[98,1024]{1,0:T(8,128)}, u32[]{:S(2)}) copy-start(f32[98,1024]{1,0:T(8,128)} %state_ref.1) | copy-start | bytes 1204228
  13.0 16.7 %copy-start.4 = (f32[98,1024]{1,0:T(8,128)S(1)}, f32[98,1024]{1,0:T(8,128)}, u32[]{:S(2)}) copy-start(f32[98,1024]{1,0:T(8,128)} %target_ref.1) | copy-start | bytes 1204228
  13.0 16.7 %copy-start.8 = (f32[1024]{0:T(1024)S(1)}, f32[1024]{0:T(1024)}, u32[]{:S(2)}) copy-start(f32[1024]{0:T(1024)} %param.28) | copy-start | bytes 12292
  13.0 16.7 %copy-start.9 = (f32[98]{0:T(128)S(1)}, f32[98]{0:T(128)}, u32[]{:S(2)}) copy-start(f32[98]{0:T(128)} %param.29) | copy-start | bytes 1180
  17.4 20.6 %copy-start.1 = (bf16[512,512]{1,0:T(8,128)(2,1)S(1)}, bf16[512,512]{1,0:T(8,128)(2,1)}, u32[]{:S(2)}) copy-start(bf16[512,512]{1,0:T(8,128)(2,1)} %w_out_ref.1) | copy-start | bytes 1572868
  17.4 20.6 %copy-start.2 = (bf16[512,98]{0,1:T(8,128)(2,1)S(1)}, bf16[512,98]{0,1:T(8,128)(2,1)}, u32[]{:S(2)}) copy-start(bf16[512,98]{0,1:T(8,128)(2,1)} %param.23) | copy-start | bytes 301060
  17.4 8.8 %collective-permute-start.4 = (bf16[98,256]{1,0:T(8,128)(2,1)S(1)}, bf16[98,256]{1,0:T(8,128)(2,1)S(1)}, u32[]{:S(2)}, u32[]{:S(2)}) collective-permute-start(bf16[98,256]{1,0:T(8,128)(2,1)S(1)} %get-tuple-element.66.refs_0_), channel_id=1, source_target_pairs={{0,3},{1,2},{2,1},{3,0},{4,7},{5,6},{6,5},{7,4},{8,11},{9,10},{10,... | collective-permute-start | bytes 150536 | tf_op jit(solution)/shard_map/ppermute | solution.py:422
  17.8 6.5 %collective-permute-start.5 = (bf16[98,128]{1,0:T(8,128)(2,1)S(1)}, bf16[98,128]{1,0:T(8,128)(2,1)S(1)}, u32[]{:S(2)}, u32[]{:S(2)}) collective-permute-start(bf16[98,128]{1,0:T(8,128)(2,1)S(1)} %get-tuple-element.67), channel_id=1, source_target_pairs={{0,4},{4,8},{8,12},{12,16},{16,20},{20,24},{24,28},{28,0},{1,5},{5... | collective-permute-start | bytes 75272 | tf_op jit(solution)/shard_map/ppermute | solution.py:504
  17.9 6.5 %collective-permute-start.6 = (bf16[98,128]{1,0:T(8,128)(2,1)S(1)}, bf16[98,128]{1,0:T(8,128)(2,1)S(1)}, u32[]{:S(2)}, u32[]{:S(2)}) collective-permute-start(bf16[98,128]{1,0:T(8,128)(2,1)S(1)} %get-tuple-element.68), channel_id=1, source_target_pairs={{4,0},{8,4},{12,8},{16,12},{20,16},{24,20},{28,24},{0,28},{5,1},{9... | collective-permute-start | bytes 75272 | tf_op jit(solution)/shard_map/ppermute | solution.py:505
  22.5 4.5 %collective-permute-start.3 = (bf16[98,256]{1,0:T(8,128)(2,1)S(1)}, bf16[98,256]{1,0:T(8,128)(2,1)S(1)}, u32[]{:S(2)}, u32[]{:S(2)}) collective-permute-start(bf16[98,256]{1,0:T(8,128)(2,1)S(1)} %get-tuple-element.66.refs_0_), channel_id=1, source_target_pairs={{0,2},{1,3},{2,0},{3,1},{4,6},{5,7},{6,4},{7,5},{8,10},{9,11},{10,... | collective-permute-start | bytes 150536 | tf_op jit(solution)/shard_map/ppermute | solution.py:422
  23.8 3.2 %collective-permute-start.2 = (bf16[98,256]{1,0:T(8,128)(2,1)S(1)}, bf16[98,256]{1,0:T(8,128)(2,1)S(1)}, u32[]{:S(2)}, u32[]{:S(2)}) collective-permute-start(bf16[98,256]{1,0:T(8,128)(2,1)S(1)} %get-tuple-element.66.refs_0_), channel_id=1, source_target_pairs={{0,1},{1,0},{2,3},{3,2},{4,5},{5,4},{6,7},{7,6},{8,9},{9,8},{10,11... | collective-permute-start | bytes 150536 | tf_op jit(solution)/shard_map/ppermute | solution.py:422
  24.4 3.8 %collective-permute-start.9 = (bf16[98,256]{1,0:T(8,128)(2,1)S(1)}, bf16[98,256]{1,0:T(8,128)(2,1)S(1)}, u32[]{:S(2)}, u32[]{:S(2)}) collective-permute-start(bf16[98,256]{1,0:T(8,128)(2,1)S(1)} %shard_map.185.refs_4_), channel_id=1, source_target_pairs={{0,3},{1,2},{2,1},{3,0},{4,7},{5,6},{6,5},{7,4},{8,11},{9,10},{10,... | collective-permute-start | bytes 150536 | tf_op jit(solution)/shard_map/ppermute | solution.py:422
  24.7 4.9 %collective-permute-start.8 = (bf16[98,256]{1,0:T(8,128)(2,1)S(1)}, bf16[98,256]{1,0:T(8,128)(2,1)S(1)}, u32[]{:S(2)}, u32[]{:S(2)}) collective-permute-start(bf16[98,256]{1,0:T(8,128)(2,1)S(1)} %shard_map.185.refs_4_), channel_id=1, source_target_pairs={{0,2},{1,3},{2,0},{3,1},{4,6},{5,7},{6,4},{7,5},{8,10},{9,11},{10,... | collective-permute-start | bytes 150536 | tf_op jit(solution)/shard_map/ppermute | solution.py:422
  26.2 3.5 %collective-permute-start.7 = (bf16[98,256]{1,0:T(8,128)(2,1)S(1)}, bf16[98,256]{1,0:T(8,128)(2,1)S(1)}, u32[]{:S(2)}, u32[]{:S(2)}) collective-permute-start(bf16[98,256]{1,0:T(8,128)(2,1)S(1)} %shard_map.185.refs_4_), channel_id=1, source_target_pairs={{0,1},{1,0},{2,3},{3,2},{4,5},{5,4},{6,7},{7,6},{8,9},{9,8},{10,11... | collective-permute-start | bytes 150536 | tf_op jit(solution)/shard_map/ppermute | solution.py:422
  31.2 6.8 %collective-permute-start.10 = (bf16[98,128]{1,0:T(8,128)(2,1)S(1)}, bf16[98,128]{1,0:T(8,128)(2,1)S(1)}, u32[]{:S(2)}, u32[]{:S(2)}) collective-permute-start(bf16[98,128]{1,0:T(8,128)(2,1)S(1)} %get-tuple-element.71), channel_id=1, source_target_pairs={{0,4},{4,8},{8,12},{12,16},{16,20},{20,24},{24,28},{28,0},{1,5},{5... | collective-permute-start | bytes 75272 | tf_op jit(solution)/shard_map/ppermute | solution.py:504
  32.4 5.6 %collective-permute-start.11 = (bf16[98,128]{1,0:T(8,128)(2,1)S(1)}, bf16[98,128]{1,0:T(8,128)(2,1)S(1)}, u32[]{:S(2)}, u32[]{:S(2)}) collective-permute-start(bf16[98,128]{1,0:T(8,128)(2,1)S(1)} %get-tuple-element.72), channel_id=1, source_target_pairs={{4,0},{8,4},{12,8},{16,12},{20,16},{24,20},{28,24},{0,28},{5,1},{9... | collective-permute-start | bytes 75272 | tf_op jit(solution)/shard_map/ppermute | solution.py:505
  45.4 3.5 %collective-permute-start.12 = (bf16[16,16,1024]{2,1,0:T(8,128)(2,1)S(1)}, bf16[16,16,1024]{2,1,0:T(8,128)(2,1)S(1)}, u32[]{:S(2)}, u32[]{:S(2)}) collective-permute-start(bf16[16,16,1024]{2,1,0:T(8,128)(2,1)S(1)} %get-tuple-element.87), channel_id=1, source_target_pairs={{0,1},{1,0},{2,3},{3,2},{4,5},{5,4},{6,7},{7,6},{8,9},{9,8},{10,11... | collective-permute-start | bytes 1572872 | tf_op jit(solution)/shard_map/ppermute | solution.py:422
  45.5 2.5 %collective-permute-start.17 = (bf16[16,16,768]{2,1,0:T(8,128)(2,1)S(1)}, bf16[16,16,768]{2,1,0:T(8,128)(2,1)S(1)}, u32[]{:S(2)}, u32[]{:S(2)}) collective-permute-start(bf16[16,16,768]{2,1,0:T(8,128)(2,1)S(1)} %get-tuple-element.97), channel_id=1, source_target_pairs={{0,1},{1,0},{2,3},{3,2},{4,5},{5,4},{6,7},{7,6},{8,9},{9,8},{10,11... | collective-permute-start | bytes 1179656 | tf_op jit(solution)/shard_map/ppermute | solution.py:422
  48.2 7.8 %collective-permute-start.18 = (bf16[8,16,768]{2,1,0:T(8,128)(2,1)S(1)}, bf16[8,16,768]{2,1,0:T(8,128)(2,1)S(1)}, u32[]{:S(2)}, u32[]{:S(2)}) collective-permute-start(bf16[8,16,768]{2,1,0:T(8,128)(2,1)S(1)} %get-tuple-element.99), channel_id=1, source_target_pairs={{0,2},{1,3},{2,0},{3,1},{4,6},{5,7},{6,4},{7,5},{8,10},{9,11},{10,... | collective-permute-start | bytes 589832 | tf_op jit(solution)/shard_map/ppermute | solution.py:422
  49.1 9.0 %collective-permute-start.13 = (bf16[8,16,512]{2,1,0:T(8,128)(2,1)S(1)}, bf16[8,16,512]{2,1,0:T(8,128)(2,1)S(1)}, u32[]{:S(2)}, u32[]{:S(2)}) collective-permute-start(bf16[8,16,512]{2,1,0:T(8,128)(2,1)S(1)} %get-tuple-element.89), channel_id=1, source_target_pairs={{0,2},{1,3},{2,0},{3,1},{4,6},{5,7},{6,4},{7,5},{8,10},{9,11},{10,... | collective-permute-start | bytes 393224 | tf_op jit(solution)/shard_map/ppermute | solution.py:422
  50.5 8.0 %collective-permute-start.15 = (bf16[2,64,512]{2,1,0:T(8,128)(2,1)S(1)}, bf16[2,64,512]{2,1,0:T(8,128)(2,1)S(1)}, u32[]{:S(2)}, u32[]{:S(2)}) collective-permute-start(bf16[2,64,512]{2,1,0:T(8,128)(2,1)S(1)} %get-tuple-element.93), channel_id=1, source_target_pairs={{0,8},{4,12},{8,0},{12,4},{16,24},{20,28},{24,16},{28,20},{1,9},{5... | collective-permute-start | bytes 393224 | tf_op jit(solution)/shard_map/ppermute | solution.py:422
  56.2 5.4 %collective-permute-start.19 = (bf16[2,32,768]{2,1,0:T(8,128)(2,1)S(1)}, bf16[2,32,768]{2,1,0:T(8,128)(2,1)S(1)}, u32[]{:S(2)}, u32[]{:S(2)}) collective-permute-start(bf16[2,32,768]{2,1,0:T(8,128)(2,1)S(1)} %get-tuple-element.101), channel_id=1, source_target_pairs={{0,8},{4,12},{8,0},{12,4},{16,24},{20,28},{24,16},{28,20},{1,9},{5... | collective-permute-start | bytes 294920 | tf_op jit(solution)/shard_map/ppermute | solution.py:422
  58.1 4.3 %collective-permute-start.14 = (bf16[2,32,512]{2,1,0:T(8,128)(2,1)S(1)}, bf16[2,32,512]{2,1,0:T(8,128)(2,1)S(1)}, u32[]{:S(2)}, u32[]{:S(2)}) collective-permute-start(bf16[2,32,512]{2,1,0:T(8,128)(2,1)S(1)} %get-tuple-element.91), channel_id=1, source_target_pairs={{0,8},{4,12},{8,0},{12,4},{16,24},{20,28},{24,16},{28,20},{1,9},{5... | collective-permute-start | bytes 196616 | tf_op jit(solution)/shard_map/ppermute | solution.py:422
  58.5 4.3 %collective-permute-start.16 = (bf16[4,16,512]{2,1,0:T(8,128)(2,1)S(1)}, bf16[4,16,512]{2,1,0:T(8,128)(2,1)S(1)}, u32[]{:S(2)}, u32[]{:S(2)}) collective-permute-start(bf16[4,16,512]{2,1,0:T(8,128)(2,1)S(1)} %get-tuple-element.95), channel_id=1, source_target_pairs={{0,2},{1,3},{2,0},{3,1},{4,6},{5,7},{6,4},{7,5},{8,10},{9,11},{10,... | collective-permute-start | bytes 196616 | tf_op jit(solution)/shard_map/ppermute | solution.py:422
  63.0 15.9 %copy-start.7 = (f32[512]{0:T(512)S(1)}, f32[512]{0:T(512)}, u32[]{:S(2)}) copy-start(f32[512]{0:T(512)} %param.16) | copy-start | bytes 6148
  63.0 6.9 %collective-permute-start.20 = (bf16[2,16,1792]{2,1,0:T(8,128)(2,1)S(1)}, bf16[2,16,1792]{2,1,0:T(8,128)(2,1)S(1)}, u32[]{:S(2)}, u32[]{:S(2)}) collective-permute-start(bf16[2,16,1792]{2,1,0:T(8,128)(2,1)S(1)} %get-tuple-element.103), channel_id=1, source_target_pairs={{0,4},{4,0},{8,12},{12,8},{16,20},{20,16},{24,28},{28,24},{1,5},{5... | collective-permute-start | bytes 344072 | tf_op jit(solution)/shard_map/ppermute | solution.py:422
  64.4 14.5 %collective-permute-start.25 = (bf16[128,512]{1,0:T(8,128)(2,1)S(1)}, bf16[128,512]{1,0:T(8,128)(2,1)S(1)}, u32[]{:S(2)}, u32[]{:S(2)}) collective-permute-start(bf16[128,512]{1,0:T(8,128)(2,1)S(1)} %get-tuple-element.110), channel_id=1, source_target_pairs={{0,4},{4,8},{8,12},{12,16},{16,20},{20,24},{24,28},{28,0},{1,5},{5... | collective-permute-start | bytes 393224 | tf_op jit(solution)/shard_map/ppermute | solution.py:504
  65.1 13.8 %collective-permute-start.26 = (bf16[128,512]{1,0:T(8,128)(2,1)S(1)}, bf16[128,512]{1,0:T(8,128)(2,1)S(1)}, u32[]{:S(2)}, u32[]{:S(2)}) collective-permute-start(bf16[128,512]{1,0:T(8,128)(2,1)S(1)} %get-tuple-element.111), channel_id=1, source_target_pairs={{4,0},{8,4},{12,8},{16,12},{20,16},{24,20},{28,24},{0,28},{5,1},{9... | collective-permute-start | bytes 393224 | tf_op jit(solution)/shard_map/ppermute | solution.py:505
  70.1 6.2 %collective-permute-start.21 = (bf16[1,16,1792]{2,1,0:T(8,128)(2,1)S(1)}, bf16[1,16,1792]{2,1,0:T(8,128)(2,1)S(1)}, u32[]{:S(2)}, u32[]{:S(2)}) collective-permute-start(bf16[1,16,1792]{2,1,0:T(8,128)(2,1)S(1)} %get-tuple-element.105), channel_id=1, source_target_pairs={{0,16},{4,20},{8,24},{12,28},{16,0},{20,4},{24,8},{28,12},{1,17},{... | collective-permute-start | bytes 172040 | tf_op jit(solution)/shard_map/ppermute | solution.py:422
  76.4 3.7 %collective-permute-start.24 = (bf16[16,1792]{1,0:T(8,128)(2,1)S(1)}, bf16[16,1792]{1,0:T(8,128)(2,1)S(1)}, u32[]{:S(2)}, u32[]{:S(2)}) collective-permute-start(bf16[16,1792]{1,0:T(8,128)(2,1)S(1)} %bitcast.51), channel_id=1, source_target_pairs={{0,3},{1,2},{2,1},{3,0},{4,7},{5,6},{6,5},{7,4},{8,11},{9,10},{10,... | collective-permute-start | bytes 172040 | tf_op jit(solution)/shard_map/ppermute | solution.py:422
  76.4 4.8 %collective-permute-start.23 = (bf16[16,1792]{1,0:T(8,128)(2,1)S(1)}, bf16[16,1792]{1,0:T(8,128)(2,1)S(1)}, u32[]{:S(2)}, u32[]{:S(2)}) collective-permute-start(bf16[16,1792]{1,0:T(8,128)(2,1)S(1)} %bitcast.52), channel_id=1, source_target_pairs={{0,2},{1,3},{2,0},{3,1},{4,6},{5,7},{6,4},{7,5},{8,10},{9,11},{10,... | collective-permute-start | bytes 172040 | tf_op jit(solution)/shard_map/ppermute | solution.py:422
  77.1 4.1 %collective-permute-start.22 = (bf16[16,1792]{1,0:T(8,128)(2,1)S(1)}, bf16[16,1792]{1,0:T(8,128)(2,1)S(1)}, u32[]{:S(2)}, u32[]{:S(2)}) collective-permute-start(bf16[16,1792]{1,0:T(8,128)(2,1)S(1)} %bitcast.53), channel_id=1, source_target_pairs={{0,1},{1,0},{2,3},{3,2},{4,5},{5,4},{6,7},{7,6},{8,9},{9,8},{10,11... | collective-permute-start | bytes 172040 | tf_op jit(solution)/shard_map/ppermute | solution.py:422

commit v5 on v4

--- a/solution.py
+++ b/solution.py
@@ -203,19 +203,22 @@
 
 
 def score_kernel(state_ref, target_ref, area_ref, var_ref, mix_ref, *refs, points):
-    grad_ref, head_ref, tail_ref, loss_ref = refs[-4:]
-    table_refs = refs[:-4]
+    grad_ref, head_ref, tail_ref, loss_ref, stack_ref = refs[-5:]
+    table_refs = refs[:-5]
     members = len(table_refs) // 2
     fair = 1.0 - (1.0 - ALPHA) / members
     pair = fair / (2.0 * members * (members - 1))
-    mix = mix_ref[...]
-    nodes = table_refs[0].shape[1]
+    variables, nodes = table_refs[0].shape
+    step = stack_ref.shape[0] // members
+    for n in range(members):
+        stack_ref[n * step : n * step + variables, :nodes] = table_refs[n][...]
+        stack_ref[n * step : n * step + variables, nodes:] = table_refs[members + n][...]
+    changes = nn(stack_ref[...], mix_ref[...])
 
     def change(n):
-        return nn(table_refs[n][...], mix[:nodes]) + nn(table_refs[members + n][...], mix[nodes:])
+        return changes[n * step : n * step + variables]
 
     own = change(0)
-    variables = own.shape[0]
     spread = jnp.zeros_like(own)
     slope = jnp.zeros_like(own)
     for n in range(members):
@@ -282,9 +285,8 @@
     rounded = total.astype(BF16)
     mixed = nt(rounded, w_out_ref[...]).astype(BF16)
     mixed_ref[...] = mixed
-    mixed = mixed.astype(F32)
     for e in range(edges):
-        edge_ref[e * nodes : (e + 1) * nodes, :] = (shares_ref[e].astype(F32) * mixed).astype(BF16)
+        edge_ref[e * nodes : (e + 1) * nodes, :] = shares_ref[e] * mixed
     grad_value = nn(hot_ref[...], edge_ref[...]).astype(BF16)
     grad_value_ref[...] = grad_value
     features = features_ref[...]
@@ -315,27 +317,29 @@
     squeeze = head_map(width, columns, head_size, edges)
     expand = head_map(columns, width, edges, head_size)
     lane = iota((nodes, columns), 1) & (edges - 1)
-    mixed = mixed_ref[...].astype(F32)
+    mixed = mixed_ref[...]
     probs = probs_ref[...]
     grad_probs = jnp.zeros((nodes, columns), F32)
     for e in range(edges):
-        part = nn((mixed * values_ref[e].astype(F32)).astype(BF16), squeeze)
+        part = nn(mixed * values_ref[e], squeeze)
         grad_probs = jnp.where(lane == e, part, grad_probs)
     grad_scores = probs * (grad_probs - group_reduce(probs * grad_probs, edges, jnp.add))
-    query = q_ref[...].astype(F32) * inv_root
+    query = q_ref[...]
     total = jnp.zeros((nodes, width), F32)
     for e in range(edges):
         share = nn(jnp.where(lane == e, grad_scores, 0.0).astype(BF16), expand)
         total += share * keys_ref[e].astype(F32)
-        edge_ref[e * nodes : (e + 1) * nodes, :] = (share * query).astype(BF16)
+        edge_ref[e * nodes : (e + 1) * nodes, :] = share.astype(BF16) * query
     grad_query_ref[...] = (total * inv_root).astype(BF16)
 
 
-def query_back_kernel(edge_ref, hot_ref, grad_value_ref, w_ref, grad_key_ref, head_ref, tail_ref):
+def query_back_kernel(
+    edge_ref, hot_ref, grad_value_ref, w_ref, grad_key_ref, head_ref, tail_ref, *, inv_root
+):
     width = edge_ref.shape[1]
     rim = head_ref.shape[0]
     nodes = hot_ref.shape[0] - 2 * rim
-    grad_key = nn(hot_ref[...], edge_ref[...]).astype(BF16)
+    grad_key = (nn(hot_ref[...], edge_ref[...]) * inv_root).astype(BF16)
     grad_key_ref[...] = grad_key
     rows = nt(grad_key[nodes:], w_ref[:, width : 2 * width])
     rows += nt(grad_value_ref[nodes:, :], w_ref[:, 2 * width :])
@@ -588,6 +592,7 @@
         functools.partial(score_kernel, points=total_points),
         [((variables, points), BF16), rim_columns, rim_columns, ((1, LANES), F32)],
         state, target, area[None], var_weight[None], mix, *own_tables, *rim_tables,
+        scratch=[pltpu.VMEM((members * (-(-variables // 16) * 16), table_rows), BF16)],
     )
     back_left, back_right = swap_rims(head, tail)
     grad_own, hot = on_core(
@@ -619,7 +624,7 @@
         grad_mixed, probs, values, queries, keys,
     )
     grad_key, head, tail = on_core(
-        query_back_kernel,
+        functools.partial(query_back_kernel, inv_root=1.0 / math.sqrt(width // (columns // edges))),
         [((table_rows, width), BF16), rim_rows, rim_rows],
         key_edges, hot, grad_value, w_qkv,
     )

time: 82.4 us -> 82.2 us (level)
  no operation moved by 1% of the time
where the time goes in v5:
time: 82.2 us; the launch traced here: 81.9 us
  starting transfers between devices  35.6 us (43%)
  Pallas kernels  22.9 us (28%)
  waiting for transfers between devices  21.8 us (27%)
  between operations  1.58 us (2%)
    pallas_call x21, Pallas kernels, on_core(): pl.pallas_call(kernel, out_shape=[jax.ShapeDtypeStruct(s, d) for s, d in...  22.9 us
    ppermute x19, waiting for transfers between devices, swapped(): return lax.ppermute(array, axis, [(i, i ^ bit) for i in range(count)])  20.4 us
    ppermute x4, starting transfers between devices, swap_rims(): lax.ppermute(head, 'region', [((i + 1) % count, i) for i in range(count)])  15.8 us
    ppermute x19, starting transfers between devices, swapped(): return lax.ppermute(array, axis, [(i, i ^ bit) for i in range(count)])  14.7 us
    ppermute x4, starting transfers between devices, swap_rims(): lax.ppermute(tail, 'region', [(i, (i + 1) % count) for i in range(count)])  5.02 us
  transfers between devices with their start and end apart: 27, of which 15 were waited for; matrix products, arithmetic and copies ran while one was open for 0% of the time, Pallas kernels for 9%

profile of v5, /device:TPU:0, one launch (start us, length us, event | category | flops | bytes accessed | tf_op | source)
XLA Modules:
  0.0 81.9 jit_solution(10086007796922694489)
XLA Ops:
  0.7 1.5 %shard_map.182 = (bf16[256,512]{1,0:T(8,128)(2,1)S(1)}, bf16[128,512]{1,0:T(8,128)(2,1)S(1)}, bf16[128,512]{1,0:T(8,128)(2,1)S(1)}) custom-call(bf16[256,512]{1,0:T(8,128)(2,1)} %bitcast.37, f32[1,512]{1,0:T(1,128)} %bitcast.68, s32[1,256]{1,0:T(1,128)} %border_ref.5), custom_call_target="tpu_custom_call" | custom-call | tf_op jit(solution)/shard_map/pallas_call | solution.py:34
  2.1 3.0 %collective-permute-start = (bf16[128,512]{1,0:T(8,128)(2,1)S(1)}, bf16[128,512]{1,0:T(8,128)(2,1)S(1)}, u32[]{:S(2)}, u32[]{:S(2)}) collective-permute-start(bf16[128,512]{1,0:T(8,128)(2,1)S(1)} %get-tuple-element.60), channel_id=1, source_target_pairs={{0,4},{4,8},{8,12},{12,16},{16,20},{20,24},{24,28},{28,0},{1,5},{5... | collective-permute-start | bytes 393224 | tf_op jit(solution)/shard_map/ppermute | solution.py:508
  5.2 3.1 %collective-permute-start.1 = (bf16[128,512]{1,0:T(8,128)(2,1)S(1)}, bf16[128,512]{1,0:T(8,128)(2,1)S(1)}, u32[]{:S(2)}, u32[]{:S(2)}) collective-permute-start(bf16[128,512]{1,0:T(8,128)(2,1)S(1)} %get-tuple-element.61), channel_id=1, source_target_pairs={{4,0},{8,4},{12,8},{16,12},{20,16},{24,20},{28,24},{0,28},{5,1},{9... | collective-permute-start | bytes 393224 | tf_op jit(solution)/shard_map/ppermute | solution.py:509
  9.0 3.6 %shard_map.183 = (bf16[256,512]{1,0:T(8,128)(2,1)S(1)}, bf16[8,256,1024]{2,1,0:T(8,128)(2,1)S(1)}, bf16[512,1024]{1,0:T(8,128)(2,1)S(1)}, bf16[512,1536]{1,0:T(8,128)(2,1)S(1)}) custom-call(bf16[512,1536]{1,0:T(8,128)(2,1)} %w_hbm.1, s32[3,1024]{1,0:T(4,128)} %src_hbm.1, f32[3,1024]{1,0:T(4,128)} %weight_hbm.1, s32[8,256]{1,0:T(8,128)} %bitcast.63, ...), custom_call_target="tpu_custom_call" | custom-call | tf_op jit(solution)/shard_map/pallas_call | solution.py:34
  12.6 0.4 collective-permute-done.1.right_ref
  13.0 4.4 %shard_map.184 = (bf16[256,512]{1,0:T(8,128)(2,1)S(1)}, bf16[98,256]{1,0:T(8,128)(2,1)S(1)}, bf16[98,128]{1,0:T(8,128)(2,1)S(1)}, bf16[98,128]{1,0:T(8,128)(2,1)...) custom-call(bf16[512,512]{1,0:T(8,128)(2,1)} %w_out_ref.1, ...), custom_call_target="tpu_custom_call" | custom-call | tf_op jit(solution)/shard_map/pallas_call | solution.py:34
  17.4 0.4 collective-permute-start.4
  17.9 4.7 %collective-permute-start.6 = (bf16[98,128]{1,0:T(8,128)(2,1)S(1)}, bf16[98,128]{1,0:T(8,128)(2,1)S(1)}, u32[]{:S(2)}, u32[]{:S(2)}) collective-permute-start(bf16[98,128]{1,0:T(8,128)(2,1)S(1)} %get-tuple-element.68), channel_id=1, source_target_pairs={{4,0},{8,4},{12,8},{16,12},{20,16},{24,20},{28,24},{0,28},{5,1},{9... | collective-permute-start | bytes 75272 | tf_op jit(solution)/shard_map/ppermute | solution.py:509
  22.5 1.3 %collective-permute-start.3 = (bf16[98,256]{1,0:T(8,128)(2,1)S(1)}, bf16[98,256]{1,0:T(8,128)(2,1)S(1)}, u32[]{:S(2)}, u32[]{:S(2)}) collective-permute-start(bf16[98,256]{1,0:T(8,128)(2,1)S(1)} %get-tuple-element.66.refs_0_), channel_id=1, source_target_pairs={{0,2},{1,3},{2,0},{3,1},{4,6},{5,7},{6,4},{7,5},{8,10},{9,11},{10,... | collective-permute-start | bytes 150536 | tf_op jit(solution)/shard_map/ppermute | solution.py:426
  23.8 0.6 collective-permute-done.5.left_ref
  24.4 0.4 collective-permute-start.9
  24.7 1.5 %collective-permute-start.8 = (bf16[98,256]{1,0:T(8,128)(2,1)S(1)}, bf16[98,256]{1,0:T(8,128)(2,1)S(1)}, u32[]{:S(2)}, u32[]{:S(2)}) collective-permute-start(bf16[98,256]{1,0:T(8,128)(2,1)S(1)} %shard_map.185.refs_4_), channel_id=1, source_target_pairs={{0,2},{1,3},{2,0},{3,1},{4,6},{5,7},{6,4},{7,5},{8,10},{9,11},{10,... | collective-permute-start | bytes 150536 | tf_op jit(solution)/shard_map/ppermute | solution.py:426
  26.3 0.7 collective-permute-done.3.refs_2_
  27.0 1.2 %collective-permute-done.9.refs_7_ = bf16[98,256]{1,0:T(8,128)(2,1)S(1)} collective-permute-done((bf16[98,256]{1,0:T(8,128)(2,1)S(1)}, bf16[98,256]{1,0:T(8,128)(2,1)S(1)}, u32[]{:S(2)}, u32[]{:S(2)}) %collective-permute-start.9) | collective-permute-done | bytes 50208 | tf_op jit(solution)/shard_map/ppermute | solution.py:426
  28.2 1.5 %collective-permute-done.8.refs_6_ = bf16[98,256]{1,0:T(8,128)(2,1)S(1)} collective-permute-done((bf16[98,256]{1,0:T(8,128)(2,1)S(1)}, bf16[98,256]{1,0:T(8,128)(2,1)S(1)}, u32[]{:S(2)}, u32[]{:S(2)}) %collective-permute-start.8) | collective-permute-done | bytes 50208 | tf_op jit(solution)/shard_map/ppermute | solution.py:426
  29.7 1.4 %shard_map.186 = (bf16[98,1024]{1,0:T(8,128)(2,1)S(1)}, bf16[98,128]{1,0:T(8,128)(2,1)S(1)}, bf16[98,128]{1,0:T(8,128)(2,1)S(1)}, f32[1,128]{1,0:T(1,128)S(1)}) custom-call(f32[98,1024]{1,0:T(8,128)S(1)} %copy-done.3, f32[98,1024]{1,0:T(8,128)S(1)} %copy-done.4, f32[1,1024]{1,0:T(1,128)S(1)} %bitcast.70, f32[1,98]{1,0:T(1,128)S(1)} %bitcast.71, ...), custom_call_target="tpu_custom_call" | custom-call | tf_op jit(solution)/shard_map/pallas_call | solution.py:34
  31.2 1.2 %collective-permute-start.10 = (bf16[98,128]{1,0:T(8,128)(2,1)S(1)}, bf16[98,128]{1,0:T(8,128)(2,1)S(1)}, u32[]{:S(2)}, u32[]{:S(2)}) collective-permute-start(bf16[98,128]{1,0:T(8,128)(2,1)S(1)} %get-tuple-element.71), channel_id=1, source_target_pairs={{0,4},{4,8},{8,12},{12,16},{16,20},{20,24},{24,28},{28,0},{1,5},{5... | collective-permute-start | bytes 75272 | tf_op jit(solution)/shard_map/ppermute | solution.py:508
  32.4 4.0 %collective-permute-start.11 = (bf16[98,128]{1,0:T(8,128)(2,1)S(1)}, bf16[98,128]{1,0:T(8,128)(2,1)S(1)}, u32[]{:S(2)}, u32[]{:S(2)}) collective-permute-start(bf16[98,128]{1,0:T(8,128)(2,1)S(1)} %get-tuple-element.72), channel_id=1, source_target_pairs={{4,0},{8,4},{12,8},{16,12},{20,16},{24,20},{28,24},{0,28},{5,1},{9... | collective-permute-start | bytes 75272 | tf_op jit(solution)/shard_map/ppermute | solution.py:509
  36.4 1.1 %shard_map.187 = (f32[98,256]{1,0:T(8,128)S(1)}, bf16[512,2048]{1,0:T(8,128)(2,1)S(1)}) custom-call(bf16[512,1024]{1,0:T(8,128)(2,1)S(1)} %get-tuple-element.62.mix_ref, bf16[98,1024]{1,0:T(8,128)(2,1)S(1)} %get-tuple-element.69.grad_ref, s32[8,256]{1,0:T(8,128)S(1)} %bitcast.65), custom_call_target="tpu_custom_call" | custom-call | tf_op jit(solution)/shard_map/pallas_call | solution.py:34
  37.5 0.5 collective-permute-done.10.from_left_ref
  38.0 2.8 %shard_map.188 = (f32[256,512]{1,0:T(8,128)S(1)}, bf16[256,512]{1,0:T(8,128)(2,1)S(1)}, bf16[512,512]{1,0:T(8,128)(2,1)S(1)}, bf16[16,16,768]{2,1,0:T(8,128)(2,1)S(1)}, f32[16,16,768]{2,1,0:T(8,128)S(1)}) custom-call(s32[1,1]{1,0:T(1,128)} %bitcast.34.count_ref, f32[98,256]{1,0:T(8,128)S(1)} %get-tuple-element.70.own_ref, ...), custom_call_target="tpu_custom_call" | custom-call | tf_op jit(solution)/shard_map/pallas_call | solution.py:34
  40.8 1.8 %shard_map.189 = (bf16[256,512]{1,0:T(8,128)(2,1)S(1)}, bf16[2048,512]{1,0:T(8,128)(2,1)S(1)}) custom-call(bf16[256,512]{1,0:T(8,128)(2,1)S(1)} %get-tuple-element.78.mixed_ref, f32[256,128]{1,0:T(8,128)S(1)} %get-tuple-element.79.probs_ref, bf16[8,256,512]{2,1,0:T(8,128)(2,1)S(1)} %get-tuple-element.80.values_ref, ...), custom_call_target="tpu_custom_call" | custom-call | tf_op jit(solution)/shard_map/pallas_call | solution.py:34
  42.6 1.5 %shard_map.190 = (bf16[512,512]{1,0:T(8,128)(2,1)S(1)}, bf16[128,512]{1,0:T(8,128)(2,1)S(1)}, bf16[128,512]{1,0:T(8,128)(2,1)S(1)}) custom-call(bf16[2048,512]{1,0:T(8,128)(2,1)S(1)} %get-tuple-element.83.edge_ref, bf16[512,2048]{1,0:T(8,128)(2,1)S(1)} %get-tuple-element.76.hot_ref, bf16[512,512]{1,0:T(8,128)(2,1)S(1)} %get-tuple-element.84.grad_value_ref, ...), custom_call_target="tpu_custom_call" | custom-call | tf_op jit(solution)/shard_map/pallas_call | solution.py:34
  44.2 1.0 %shard_map.191 = (bf16[16,16,1024]{2,1,0:T(8,128)(2,1)S(1)}, f32[16,16,1024]{2,1,0:T(8,128)S(1)}) custom-call(bf16[256,512]{1,0:T(8,128)(2,1)S(1)} %get-tuple-element.59.features_ref, bf16[128,512]{1,0:T(8,128)(2,1)S(1)} %collective-permute-done.left_ref, bf16[128,512]{1,0:T(8,128)(2,1)S(1)} %collective-permute-done.1.right_ref, ...), custom_call_target="tpu_custom_call" | custom-call | tf_op jit(solution)/shard_map/pallas_call | solution.py:34
  45.3 0.5 collective-permute-start.17
  45.8 2.0 %collective-permute-done.17 = bf16[16,16,768]{2,1,0:T(8,128)(2,1)S(1)} collective-permute-done((bf16[16,16,768]{2,1,0:T(8,128)(2,1)S(1)}, bf16[16,16,768]{2,1,0:T(8,128)(2,1)S(1)}, u32[]{:S(2)}, u32[]{:S(2)}) %collective-permute-start.17) | collective-permute-done | bytes 393248 | tf_op jit(solution)/shard_map/ppermute | solution.py:426
  47.7 0.2 shard_map.195
  48.0 0.7 collective-permute-start.18
  48.8 1.4 %collective-permute-start.13 = (bf16[8,16,512]{2,1,0:T(8,128)(2,1)S(1)}, bf16[8,16,512]{2,1,0:T(8,128)(2,1)S(1)}, u32[]{:S(2)}, u32[]{:S(2)}) collective-permute-start(bf16[8,16,512]{2,1,0:T(8,128)(2,1)S(1)} %get-tuple-element.89), channel_id=1, source_target_pairs={{0,2},{1,3},{2,0},{3,1},{4,6},{5,7},{6,4},{7,5},{8,10},{9,11},{10,... | collective-permute-start | bytes 393224 | tf_op jit(solution)/shard_map/ppermute | solution.py:426
  50.3 5.6 %collective-permute-done.18 = bf16[8,16,768]{2,1,0:T(8,128)(2,1)S(1)} collective-permute-done((bf16[8,16,768]{2,1,0:T(8,128)(2,1)S(1)}, bf16[8,16,768]{2,1,0:T(8,128)(2,1)S(1)}, u32[]{:S(2)}, u32[]{:S(2)}) %collective-permute-start.18) | collective-permute-done | bytes 196640 | tf_op jit(solution)/shard_map/ppermute | solution.py:426
  56.1 1.7 %collective-permute-done.13 = bf16[8,16,512]{2,1,0:T(8,128)(2,1)S(1)} collective-permute-done((bf16[8,16,512]{2,1,0:T(8,128)(2,1)S(1)}, bf16[8,16,512]{2,1,0:T(8,128)(2,1)S(1)}, u32[]{:S(2)}, u32[]{:S(2)}) %collective-permute-start.13) | collective-permute-done | bytes 131104 | tf_op jit(solution)/shard_map/ppermute | solution.py:426
  57.8 0.4 collective-permute-start.14
  58.3 0.7 collective-permute-start.16
  59.0 2.4 %collective-permute-done.19 = bf16[2,32,768]{2,1,0:T(8,128)(2,1)S(1)} collective-permute-done((bf16[2,32,768]{2,1,0:T(8,128)(2,1)S(1)}, bf16[2,32,768]{2,1,0:T(8,128)(2,1)S(1)}, u32[]{:S(2)}, u32[]{:S(2)}) %collective-permute-start.19) | collective-permute-done | bytes 98336 | tf_op jit(solution)/shard_map/ppermute | solution.py:426
  61.4 0.8 collective-permute-done.14
  62.2 0.4 collective-permute-done.16
  62.8 1.4 %collective-permute-start.20 = (bf16[2,16,1792]{2,1,0:T(8,128)(2,1)S(1)}, bf16[2,16,1792]{2,1,0:T(8,128)(2,1)S(1)}, u32[]{:S(2)}, u32[]{:S(2)}) collective-permute-start(bf16[2,16,1792]{2,1,0:T(8,128)(2,1)S(1)} %get-tuple-element.103), channel_id=1, source_target_pairs={{0,4},{4,0},{8,12},{12,8},{16,20},{20,16},{24,28},{28,24},{1,5},{5... | collective-permute-start | bytes 344072 | tf_op jit(solution)/shard_map/ppermute | solution.py:426
  64.2 0.7 collective-permute-start.25
  64.9 4.0 %collective-permute-start.26 = (bf16[128,512]{1,0:T(8,128)(2,1)S(1)}, bf16[128,512]{1,0:T(8,128)(2,1)S(1)}, u32[]{:S(2)}, u32[]{:S(2)}) collective-permute-start(bf16[128,512]{1,0:T(8,128)(2,1)S(1)} %get-tuple-element.111), channel_id=1, source_target_pairs={{4,0},{8,4},{12,8},{16,12},{20,16},{24,20},{28,24},{0,28},{5,1},{9... | collective-permute-start | bytes 393224 | tf_op jit(solution)/shard_map/ppermute | solution.py:509
  68.9 0.8 collective-permute-done.20
  69.8 4.0 %collective-permute-start.21 = (bf16[1,16,1792]{2,1,0:T(8,128)(2,1)S(1)}, bf16[1,16,1792]{2,1,0:T(8,128)(2,1)S(1)}, u32[]{:S(2)}, u32[]{:S(2)}) collective-permute-start(bf16[1,16,1792]{2,1,0:T(8,128)(2,1)S(1)} %get-tuple-element.105), channel_id=1, source_target_pairs={{0,16},{4,20},{8,24},{12,28},{16,0},{20,4},{24,8},{28,12},{1,17},{... | collective-permute-start | bytes 172040 | tf_op jit(solution)/shard_map/ppermute | solution.py:426
  73.9 2.2 %collective-permute-done.21.arrived_ref = bf16[1,16,1792]{2,1,0:T(8,128)(2,1)S(1)} collective-permute-done((bf16[1,16,1792]{2,1,0:T(8,128)(2,1)S(1)}, bf16[1,16,1792]{2,1,0:T(8,128)(2,1)S(1)}, u32[]{:S(2)}, u32[]{:S(2)}) %collective-permute-start.21) | collective-permute-done | bytes 57376 | tf_op jit(solution)/shard_map/ppermute | solution.py:426
  76.2 0.7 collective-permute-start.23
  76.9 1.2 %collective-permute-start.22 = (bf16[16,1792]{1,0:T(8,128)(2,1)S(1)}, bf16[16,1792]{1,0:T(8,128)(2,1)S(1)}, u32[]{:S(2)}, u32[]{:S(2)}) collective-permute-start(bf16[16,1792]{1,0:T(8,128)(2,1)S(1)} %bitcast.53), channel_id=1, source_target_pairs={{0,1},{1,0},{2,3},{3,2},{4,5},{5,4},{6,7},{7,6},{8,9},{9,8},{10,11... | collective-permute-start | bytes 172040 | tf_op jit(solution)/shard_map/ppermute | solution.py:426
  78.1 0.6 shard_map.201.own_ref
  78.7 1.2 %shard_map.202 = bf16[256,512]{1,0:T(8,128)(2,1)} custom-call(bf16[256,512]{1,0:T(8,128)(2,1)S(1)} %bitcast.39, f32[1,512]{1,0:T(1,128)S(1)} %bitcast.69, f32[256,512]{1,0:T(8,128)S(1)} %shard_map.201.own_ref, bf16[128,512]{1,0:T(8,128)(2,1)S(1)} %collective-permute-done.25.from_left_ref, bf16[128,512]{1,0:T(8,128)(2,1)S(1)} %collective-permute-done.26.from_right_ref, ...), custom_call_target="tpu_custom_call" | custom-call | tf_op jit(solution)/shard_map/pallas_call | solution.py:34
  79.8 1.2 %collective-permute-done.23.refs_2_ = bf16[16,1792]{1,0:T(8,128)(2,1)S(1)} collective-permute-done((bf16[16,1792]{1,0:T(8,128)(2,1)S(1)}, bf16[16,1792]{1,0:T(8,128)(2,1)S(1)}, u32[]{:S(2)}, u32[]{:S(2)}) %collective-permute-start.23) | collective-permute-done | bytes 57376 | tf_op jit(solution)/shard_map/ppermute | solution.py:426
  81.0 0.9 %shard_map.200 = (f32[4,16,1536]{2,1,0:T(8,128)}, f32[4,16,512]{2,1,0:T(8,128)}, f32[4,16,98]{2,1,0:T(8,128)}, f32[1,1]{1,0:T(1,128)}) custom-call(bf16[98,512]{1,0:T(8,128)(2,1)S(1)} %bitcast.44, bf16[16,1792]{1,0:T(8,128)(2,1)S(1)} %bitcast.54, bf16[16,1792]{1,0:T(8,128)(2,1)S(1)} %collective-permute-done.22.refs_1_, ...), custom_call_target="tpu_custom_call" | custom-call | tf_op jit(solution)/shard_map/pallas_call | solution.py:34
  (47 shorter events, 1.2 us)
Async XLA Ops:
  0.6 12.3 %copy-start.6 = (s32[1,256]{1,0:T(1,128)S(1)}, s32[1,256]{1,0:T(1,128)}, u32[]{:S(2)}) copy-start(s32[1,256]{1,0:T(1,128)} %border_ref.5) | copy-start | bytes 3076
  0.6 12.3 %copy-start = (bf16[1,256,512]{2,1,0:T(8,128)(2,1)S(1)}, bf16[1,256,512]{2,1,0:T(8,128)(2,1)}, u32[]{:S(2)}) copy-start(bf16[1,256,512]{2,1,0:T(8,128)(2,1)} %param.15) | copy-start | bytes 786436
  0.7 12.3 %copy-start.5 = (s32[256,8]{0,1:T(8,128)S(1)}, s32[256,8]{0,1:T(8,128)}, u32[]{:S(2)}) copy-start(s32[256,8]{0,1:T(8,128)} %param.20) | copy-start | bytes 24580
  2.1 10.4 %collective-permute-start = (bf16[128,512]{1,0:T(8,128)(2,1)S(1)}, bf16[128,512]{1,0:T(8,128)(2,1)S(1)}, u32[]{:S(2)}, u32[]{:S(2)}) collective-permute-start(bf16[128,512]{1,0:T(8,128)(2,1)S(1)} %get-tuple-element.60), channel_id=1, source_target_pairs={{0,4},{4,8},{8,12},{12,16},{16,20},{20,24},{24,28},{28,0},{1,5},{5... | collective-permute-start | bytes 393224 | tf_op jit(solution)/shard_map/ppermute | solution.py:508
  5.2 7.8 %collective-permute-start.1 = (bf16[128,512]{1,0:T(8,128)(2,1)S(1)}, bf16[128,512]{1,0:T(8,128)(2,1)S(1)}, u32[]{:S(2)}, u32[]{:S(2)}) collective-permute-start(bf16[128,512]{1,0:T(8,128)(2,1)S(1)} %get-tuple-element.61), channel_id=1, source_target_pairs={{4,0},{8,4},{12,8},{16,12},{20,16},{24,20},{28,24},{0,28},{5,1},{9... | collective-permute-start | bytes 393224 | tf_op jit(solution)/shard_map/ppermute | solution.py:509
  13.0 16.7 %copy-start.3 = (f32[98,1024]{1,0:T(8,128)S(1)}, f32[98,1024]{1,0:T(8,128)}, u32[]{:S(2)}) copy-start(f32[98,1024]{1,0:T(8,128)} %state_ref.1) | copy-start | bytes 1204228
  13.0 16.7 %copy-start.4 = (f32[98,1024]{1,0:T(8,128)S(1)}, f32[98,1024]{1,0:T(8,128)}, u32[]{:S(2)}) copy-start(f32[98,1024]{1,0:T(8,128)} %target_ref.1) | copy-start | bytes 1204228
  13.0 16.7 %copy-start.8 = (f32[1024]{0:T(1024)S(1)}, f32[1024]{0:T(1024)}, u32[]{:S(2)}) copy-start(f32[1024]{0:T(1024)} %param.28) | copy-start | bytes 12292
  13.0 16.7 %copy-start.9 = (f32[98]{0:T(128)S(1)}, f32[98]{0:T(128)}, u32[]{:S(2)}) copy-start(f32[98]{0:T(128)} %param.29) | copy-start | bytes 1180
  17.4 20.6 %copy-start.1 = (bf16[512,512]{1,0:T(8,128)(2,1)S(1)}, bf16[512,512]{1,0:T(8,128)(2,1)}, u32[]{:S(2)}) copy-start(bf16[512,512]{1,0:T(8,128)(2,1)} %w_out_ref.1) | copy-start | bytes 1572868
  17.4 20.6 %copy-start.2 = (bf16[512,98]{0,1:T(8,128)(2,1)S(1)}, bf16[512,98]{0,1:T(8,128)(2,1)}, u32[]{:S(2)}) copy-start(bf16[512,98]{0,1:T(8,128)(2,1)} %param.23) | copy-start | bytes 301060
  17.4 8.8 %collective-permute-start.4 = (bf16[98,256]{1,0:T(8,128)(2,1)S(1)}, bf16[98,256]{1,0:T(8,128)(2,1)S(1)}, u32[]{:S(2)}, u32[]{:S(2)}) collective-permute-start(bf16[98,256]{1,0:T(8,128)(2,1)S(1)} %get-tuple-element.66.refs_0_), channel_id=1, source_target_pairs={{0,3},{1,2},{2,1},{3,0},{4,7},{5,6},{6,5},{7,4},{8,11},{9,10},{10,... | collective-permute-start | bytes 150536 | tf_op jit(solution)/shard_map/ppermute | solution.py:426
  17.8 6.5 %collective-permute-start.5 = (bf16[98,128]{1,0:T(8,128)(2,1)S(1)}, bf16[98,128]{1,0:T(8,128)(2,1)S(1)}, u32[]{:S(2)}, u32[]{:S(2)}) collective-permute-start(bf16[98,128]{1,0:T(8,128)(2,1)S(1)} %get-tuple-element.67), channel_id=1, source_target_pairs={{0,4},{4,8},{8,12},{12,16},{16,20},{20,24},{24,28},{28,0},{1,5},{5... | collective-permute-start | bytes 75272 | tf_op jit(solution)/shard_map/ppermute | solution.py:508
  17.9 6.5 %collective-permute-start.6 = (bf16[98,128]{1,0:T(8,128)(2,1)S(1)}, bf16[98,128]{1,0:T(8,128)(2,1)S(1)}, u32[]{:S(2)}, u32[]{:S(2)}) collective-permute-start(bf16[98,128]{1,0:T(8,128)(2,1)S(1)} %get-tuple-element.68), channel_id=1, source_target_pairs={{4,0},{8,4},{12,8},{16,12},{20,16},{24,20},{28,24},{0,28},{5,1},{9... | collective-permute-start | bytes 75272 | tf_op jit(solution)/shard_map/ppermute | solution.py:509
  22.5 4.5 %collective-permute-start.3 = (bf16[98,256]{1,0:T(8,128)(2,1)S(1)}, bf16[98,256]{1,0:T(8,128)(2,1)S(1)}, u32[]{:S(2)}, u32[]{:S(2)}) collective-permute-start(bf16[98,256]{1,0:T(8,128)(2,1)S(1)} %get-tuple-element.66.refs_0_), channel_id=1, source_target_pairs={{0,2},{1,3},{2,0},{3,1},{4,6},{5,7},{6,4},{7,5},{8,10},{9,11},{10,... | collective-permute-start | bytes 150536 | tf_op jit(solution)/shard_map/ppermute | solution.py:426
  23.8 3.2 %collective-permute-start.2 = (bf16[98,256]{1,0:T(8,128)(2,1)S(1)}, bf16[98,256]{1,0:T(8,128)(2,1)S(1)}, u32[]{:S(2)}, u32[]{:S(2)}) collective-permute-start(bf16[98,256]{1,0:T(8,128)(2,1)S(1)} %get-tuple-element.66.refs_0_), channel_id=1, source_target_pairs={{0,1},{1,0},{2,3},{3,2},{4,5},{5,4},{6,7},{7,6},{8,9},{9,8},{10,11... | collective-permute-start | bytes 150536 | tf_op jit(solution)/shard_map/ppermute | solution.py:426
  24.4 3.8 %collective-permute-start.9 = (bf16[98,256]{1,0:T(8,128)(2,1)S(1)}, bf16[98,256]{1,0:T(8,128)(2,1)S(1)}, u32[]{:S(2)}, u32[]{:S(2)}) collective-permute-start(bf16[98,256]{1,0:T(8,128)(2,1)S(1)} %shard_map.185.refs_4_), channel_id=1, source_target_pairs={{0,3},{1,2},{2,1},{3,0},{4,7},{5,6},{6,5},{7,4},{8,11},{9,10},{10,... | collective-permute-start | bytes 150536 | tf_op jit(solution)/shard_map/ppermute | solution.py:426
  24.7 4.9 %collective-permute-start.8 = (bf16[98,256]{1,0:T(8,128)(2,1)S(1)}, bf16[98,256]{1,0:T(8,128)(2,1)S(1)}, u32[]{:S(2)}, u32[]{:S(2)}) collective-permute-start(bf16[98,256]{1,0:T(8,128)(2,1)S(1)} %shard_map.185.refs_4_), channel_id=1, source_target_pairs={{0,2},{1,3},{2,0},{3,1},{4,6},{5,7},{6,4},{7,5},{8,10},{9,11},{10,... | collective-permute-start | bytes 150536 | tf_op jit(solution)/shard_map/ppermute | solution.py:426
  26.2 3.5 %collective-permute-start.7 = (bf16[98,256]{1,0:T(8,128)(2,1)S(1)}, bf16[98,256]{1,0:T(8,128)(2,1)S(1)}, u32[]{:S(2)}, u32[]{:S(2)}) collective-permute-start(bf16[98,256]{1,0:T(8,128)(2,1)S(1)} %shard_map.185.refs_4_), channel_id=1, source_target_pairs={{0,1},{1,0},{2,3},{3,2},{4,5},{5,4},{6,7},{7,6},{8,9},{9,8},{10,11... | collective-permute-start | bytes 150536 | tf_op jit(solution)/shard_map/ppermute | solution.py:426
  31.2 6.8 %collective-permute-start.10 = (bf16[98,128]{1,0:T(8,128)(2,1)S(1)}, bf16[98,128]{1,0:T(8,128)(2,1)S(1)}, u32[]{:S(2)}, u32[]{:S(2)}) collective-permute-start(bf16[98,128]{1,0:T(8,128)(2,1)S(1)} %get-tuple-element.71), channel_id=1, source_target_pairs={{0,4},{4,8},{8,12},{12,16},{16,20},{20,24},{24,28},{28,0},{1,5},{5... | collective-permute-start | bytes 75272 | tf_op jit(solution)/shard_map/ppermute | solution.py:508
  32.4 5.6 %collective-permute-start.11 = (bf16[98,128]{1,0:T(8,128)(2,1)S(1)}, bf16[98,128]{1,0:T(8,128)(2,1)S(1)}, u32[]{:S(2)}, u32[]{:S(2)}) collective-permute-start(bf16[98,128]{1,0:T(8,128)(2,1)S(1)} %get-tuple-element.72), channel_id=1, source_target_pairs={{4,0},{8,4},{12,8},{16,12},{20,16},{24,20},{28,24},{0,28},{5,1},{9... | collective-permute-start | bytes 75272 | tf_op jit(solution)/shard_map/ppermute | solution.py:509
  45.2 3.5 %collective-permute-start.12 = (bf16[16,16,1024]{2,1,0:T(8,128)(2,1)S(1)}, bf16[16,16,1024]{2,1,0:T(8,128)(2,1)S(1)}, u32[]{:S(2)}, u32[]{:S(2)}) collective-permute-start(bf16[16,16,1024]{2,1,0:T(8,128)(2,1)S(1)} %get-tuple-element.87), channel_id=1, source_target_pairs={{0,1},{1,0},{2,3},{3,2},{4,5},{5,4},{6,7},{7,6},{8,9},{9,8},{10,11... | collective-permute-start | bytes 1572872 | tf_op jit(solution)/shard_map/ppermute | solution.py:426
  45.3 2.5 %collective-permute-start.17 = (bf16[16,16,768]{2,1,0:T(8,128)(2,1)S(1)}, bf16[16,16,768]{2,1,0:T(8,128)(2,1)S(1)}, u32[]{:S(2)}, u32[]{:S(2)}) collective-permute-start(bf16[16,16,768]{2,1,0:T(8,128)(2,1)S(1)} %get-tuple-element.97), channel_id=1, source_target_pairs={{0,1},{1,0},{2,3},{3,2},{4,5},{5,4},{6,7},{7,6},{8,9},{9,8},{10,11... | collective-permute-start | bytes 1179656 | tf_op jit(solution)/shard_map/ppermute | solution.py:426
  48.0 7.8 %collective-permute-start.18 = (bf16[8,16,768]{2,1,0:T(8,128)(2,1)S(1)}, bf16[8,16,768]{2,1,0:T(8,128)(2,1)S(1)}, u32[]{:S(2)}, u32[]{:S(2)}) collective-permute-start(bf16[8,16,768]{2,1,0:T(8,128)(2,1)S(1)} %get-tuple-element.99), channel_id=1, source_target_pairs={{0,2},{1,3},{2,0},{3,1},{4,6},{5,7},{6,4},{7,5},{8,10},{9,11},{10,... | collective-permute-start | bytes 589832 | tf_op jit(solution)/shard_map/ppermute | solution.py:426
  48.8 9.0 %collective-permute-start.13 = (bf16[8,16,512]{2,1,0:T(8,128)(2,1)S(1)}, bf16[8,16,512]{2,1,0:T(8,128)(2,1)S(1)}, u32[]{:S(2)}, u32[]{:S(2)}) collective-permute-start(bf16[8,16,512]{2,1,0:T(8,128)(2,1)S(1)} %get-tuple-element.89), channel_id=1, source_target_pairs={{0,2},{1,3},{2,0},{3,1},{4,6},{5,7},{6,4},{7,5},{8,10},{9,11},{10,... | collective-permute-start | bytes 393224 | tf_op jit(solution)/shard_map/ppermute | solution.py:426
  50.3 8.0 %collective-permute-start.15 = (bf16[2,64,512]{2,1,0:T(8,128)(2,1)S(1)}, bf16[2,64,512]{2,1,0:T(8,128)(2,1)S(1)}, u32[]{:S(2)}, u32[]{:S(2)}) collective-permute-start(bf16[2,64,512]{2,1,0:T(8,128)(2,1)S(1)} %get-tuple-element.93), channel_id=1, source_target_pairs={{0,8},{4,12},{8,0},{12,4},{16,24},{20,28},{24,16},{28,20},{1,9},{5... | collective-permute-start | bytes 393224 | tf_op jit(solution)/shard_map/ppermute | solution.py:426
  56.0 5.4 %collective-permute-start.19 = (bf16[2,32,768]{2,1,0:T(8,128)(2,1)S(1)}, bf16[2,32,768]{2,1,0:T(8,128)(2,1)S(1)}, u32[]{:S(2)}, u32[]{:S(2)}) collective-permute-start(bf16[2,32,768]{2,1,0:T(8,128)(2,1)S(1)} %get-tuple-element.101), channel_id=1, source_target_pairs={{0,8},{4,12},{8,0},{12,4},{16,24},{20,28},{24,16},{28,20},{1,9},{5... | collective-permute-start | bytes 294920 | tf_op jit(solution)/shard_map/ppermute | solution.py:426
  57.8 4.3 %collective-permute-start.14 = (bf16[2,32,512]{2,1,0:T(8,128)(2,1)S(1)}, bf16[2,32,512]{2,1,0:T(8,128)(2,1)S(1)}, u32[]{:S(2)}, u32[]{:S(2)}) collective-permute-start(bf16[2,32,512]{2,1,0:T(8,128)(2,1)S(1)} %get-tuple-element.91), channel_id=1, source_target_pairs={{0,8},{4,12},{8,0},{12,4},{16,24},{20,28},{24,16},{28,20},{1,9},{5... | collective-permute-start | bytes 196616 | tf_op jit(solution)/shard_map/ppermute | solution.py:426
  58.3 4.3 %collective-permute-start.16 = (bf16[4,16,512]{2,1,0:T(8,128)(2,1)S(1)}, bf16[4,16,512]{2,1,0:T(8,128)(2,1)S(1)}, u32[]{:S(2)}, u32[]{:S(2)}) collective-permute-start(bf16[4,16,512]{2,1,0:T(8,128)(2,1)S(1)} %get-tuple-element.95), channel_id=1, source_target_pairs={{0,2},{1,3},{2,0},{3,1},{4,6},{5,7},{6,4},{7,5},{8,10},{9,11},{10,... | collective-permute-start | bytes 196616 | tf_op jit(solution)/shard_map/ppermute | solution.py:426
  62.8 15.9 %copy-start.7 = (f32[512]{0:T(512)S(1)}, f32[512]{0:T(512)}, u32[]{:S(2)}) copy-start(f32[512]{0:T(512)} %param.16) | copy-start | bytes 6148
  62.8 6.9 %collective-permute-start.20 = (bf16[2,16,1792]{2,1,0:T(8,128)(2,1)S(1)}, bf16[2,16,1792]{2,1,0:T(8,128)(2,1)S(1)}, u32[]{:S(2)}, u32[]{:S(2)}) collective-permute-start(bf16[2,16,1792]{2,1,0:T(8,128)(2,1)S(1)} %get-tuple-element.103), channel_id=1, source_target_pairs={{0,4},{4,0},{8,12},{12,8},{16,20},{20,16},{24,28},{28,24},{1,5},{5... | collective-permute-start | bytes 344072 | tf_op jit(solution)/shard_map/ppermute | solution.py:426
  64.2 14.5 %collective-permute-start.25 = (bf16[128,512]{1,0:T(8,128)(2,1)S(1)}, bf16[128,512]{1,0:T(8,128)(2,1)S(1)}, u32[]{:S(2)}, u32[]{:S(2)}) collective-permute-start(bf16[128,512]{1,0:T(8,128)(2,1)S(1)} %get-tuple-element.110), channel_id=1, source_target_pairs={{0,4},{4,8},{8,12},{12,16},{16,20},{20,24},{24,28},{28,0},{1,5},{5... | collective-permute-start | bytes 393224 | tf_op jit(solution)/shard_map/ppermute | solution.py:508
  64.9 13.8 %collective-permute-start.26 = (bf16[128,512]{1,0:T(8,128)(2,1)S(1)}, bf16[128,512]{1,0:T(8,128)(2,1)S(1)}, u32[]{:S(2)}, u32[]{:S(2)}) collective-permute-start(bf16[128,512]{1,0:T(8,128)(2,1)S(1)} %get-tuple-element.111), channel_id=1, source_target_pairs={{4,0},{8,4},{12,8},{16,12},{20,16},{24,20},{28,24},{0,28},{5,1},{9... | collective-permute-start | bytes 393224 | tf_op jit(solution)/shard_map/ppermute | solution.py:509
  69.8 6.2 %collective-permute-start.21 = (bf16[1,16,1792]{2,1,0:T(8,128)(2,1)S(1)}, bf16[1,16,1792]{2,1,0:T(8,128)(2,1)S(1)}, u32[]{:S(2)}, u32[]{:S(2)}) collective-permute-start(bf16[1,16,1792]{2,1,0:T(8,128)(2,1)S(1)} %get-tuple-element.105), channel_id=1, source_target_pairs={{0,16},{4,20},{8,24},{12,28},{16,0},{20,4},{24,8},{28,12},{1,17},{... | collective-permute-start | bytes 172040 | tf_op jit(solution)/shard_map/ppermute | solution.py:426
  76.2 3.7 %collective-permute-start.24 = (bf16[16,1792]{1,0:T(8,128)(2,1)S(1)}, bf16[16,1792]{1,0:T(8,128)(2,1)S(1)}, u32[]{:S(2)}, u32[]{:S(2)}) collective-permute-start(bf16[16,1792]{1,0:T(8,128)(2,1)S(1)} %bitcast.51), channel_id=1, source_target_pairs={{0,3},{1,2},{2,1},{3,0},{4,7},{5,6},{6,5},{7,4},{8,11},{9,10},{10,... | collective-permute-start | bytes 172040 | tf_op jit(solution)/shard_map/ppermute | solution.py:426
  76.2 4.8 %collective-permute-start.23 = (bf16[16,1792]{1,0:T(8,128)(2,1)S(1)}, bf16[16,1792]{1,0:T(8,128)(2,1)S(1)}, u32[]{:S(2)}, u32[]{:S(2)}) collective-permute-start(bf16[16,1792]{1,0:T(8,128)(2,1)S(1)} %bitcast.52), channel_id=1, source_target_pairs={{0,2},{1,3},{2,0},{3,1},{4,6},{5,7},{6,4},{7,5},{8,10},{9,11},{10,... | collective-permute-start | bytes 172040 | tf_op jit(solution)/shard_map/ppermute | solution.py:426
  76.9 4.1 %collective-permute-start.22 = (bf16[16,1792]{1,0:T(8,128)(2,1)S(1)}, bf16[16,1792]{1,0:T(8,128)(2,1)S(1)}, u32[]{:S(2)}, u32[]{:S(2)}) collective-permute-start(bf16[16,1792]{1,0:T(8,128)(2,1)S(1)} %bitcast.53), channel_id=1, source_target_pairs={{0,1},{1,0},{2,3},{3,2},{4,5},{5,4},{6,7},{7,6},{8,9},{9,8},{10,11... | collective-permute-start | bytes 172040 | tf_op jit(solution)/shard_map/ppermute | solution.py:426

commit v6 on v5

--- a/solution.py
+++ b/solution.py
@@ -460,8 +460,8 @@
 
 
 def unpack_kernel(w_dec_ref, *refs):
-    sum_refs = refs[:-4]
-    qkv_ref, out_ref, dec_ref, loss_ref = refs[-4:]
+    sum_refs = refs[:-5]
+    qkv_ref, out_ref, dec_ref, loss_ref, stack_ref = refs[-5:]
     width = out_ref.shape[-1]
     variables = dec_ref.shape[-1]
     step = padded(variables)
@@ -470,8 +470,15 @@
     for away, ref in enumerate(sum_refs):
         at = place ^ away
         qkv_ref[at] = ref[:, :start].astype(F32)
-        out_ref[at] = nn(ref[:, start : start + variables], w_dec_ref[...])
+        stack_ref[at] = ref[:, start : start + variables]
         dec_ref[at] = ref[:, start + step : start + step + variables].astype(F32)
+    members, rows, _ = out_ref.shape
+    if rows % 16 == 0:
+        stacked = stack_ref[...].reshape(members * rows, variables)
+        out_ref[...] = nn(stacked, w_dec_ref[...]).reshape(out_ref.shape)
+    else:
+        for n in range(members):
+            out_ref[n] = nn(stack_ref[n], w_dec_ref[...])
     start += 2 * step
     last = sum_refs[0][0:1, start : start + 2].astype(F32)
     loss_ref[...] = last[:, 0:1] + last[:, 1:2]
@@ -685,6 +692,7 @@
             ((members, rows, variables), F32), ((1, 1), F32),
         ],
         w_decoder, *sums,
+        scratch=[pltpu.VMEM((members, rows, variables), BF16)],
     )
     held = members * rows
     return (

time: 82.2 us -> 82.1 us (level)
  no operation moved by 1% of the time
where the time goes in v6:
time: 82.1 us; the launch traced here: 81.9 us
  starting transfers between devices  35.6 us (43%)
  Pallas kernels  22.9 us (28%)
  waiting for transfers between devices  21.8 us (27%)
  between operations  1.58 us (2%)
    pallas_call x21, Pallas kernels, on_core(): pl.pallas_call(kernel, out_shape=[jax.ShapeDtypeStruct(s, d) for s, d in...  22.9 us
    ppermute x19, waiting for transfers between devices, swapped(): return lax.ppermute(array, axis, [(i, i ^ bit) for i in range(count)])  20.4 us
    ppermute x4, starting transfers between devices, swap_rims(): lax.ppermute(head, 'region', [((i + 1) % count, i) for i in range(count)])  15.8 us
    ppermute x19, starting transfers between devices, swapped(): return lax.ppermute(array, axis, [(i, i ^ bit) for i in range(count)])  14.7 us
    ppermute x4, starting transfers between devices, swap_rims(): lax.ppermute(tail, 'region', [(i, (i + 1) % count) for i in range(count)])  5.02 us
  transfers between devices with their start and end apart: 27, of which 15 were waited for; matrix products, arithmetic and copies ran while one was open for 0% of the time, Pallas kernels for 9%

profile of v6, /device:TPU:0, one launch (start us, length us, event | category | flops | bytes accessed | tf_op | source)
XLA Modules:
  0.0 81.9 jit_solution(8708999031739627654)
XLA Ops:
  0.7 1.5 %shard_map.182 = (bf16[256,512]{1,0:T(8,128)(2,1)S(1)}, bf16[128,512]{1,0:T(8,128)(2,1)S(1)}, bf16[128,512]{1,0:T(8,128)(2,1)S(1)}) custom-call(bf16[256,512]{1,0:T(8,128)(2,1)} %bitcast.37, f32[1,512]{1,0:T(1,128)} %bitcast.68, s32[1,256]{1,0:T(1,128)} %border_ref.5), custom_call_target="tpu_custom_call" | custom-call | tf_op jit(solution)/shard_map/pallas_call | solution.py:34
  2.1 3.0 %collective-permute-start = (bf16[128,512]{1,0:T(8,128)(2,1)S(1)}, bf16[128,512]{1,0:T(8,128)(2,1)S(1)}, u32[]{:S(2)}, u32[]{:S(2)}) collective-permute-start(bf16[128,512]{1,0:T(8,128)(2,1)S(1)} %get-tuple-element.60), channel_id=1, source_target_pairs={{0,4},{4,8},{8,12},{12,16},{16,20},{20,24},{24,28},{28,0},{1,5},{5... | collective-permute-start | bytes 393224 | tf_op jit(solution)/shard_map/ppermute | solution.py:515
  5.2 3.1 %collective-permute-start.1 = (bf16[128,512]{1,0:T(8,128)(2,1)S(1)}, bf16[128,512]{1,0:T(8,128)(2,1)S(1)}, u32[]{:S(2)}, u32[]{:S(2)}) collective-permute-start(bf16[128,512]{1,0:T(8,128)(2,1)S(1)} %get-tuple-element.61), channel_id=1, source_target_pairs={{4,0},{8,4},{12,8},{16,12},{20,16},{24,20},{28,24},{0,28},{5,1},{9... | collective-permute-start | bytes 393224 | tf_op jit(solution)/shard_map/ppermute | solution.py:516
  9.0 3.6 %shard_map.183 = (bf16[256,512]{1,0:T(8,128)(2,1)S(1)}, bf16[8,256,1024]{2,1,0:T(8,128)(2,1)S(1)}, bf16[512,1024]{1,0:T(8,128)(2,1)S(1)}, bf16[512,1536]{1,0:T(8,128)(2,1)S(1)}) custom-call(bf16[512,1536]{1,0:T(8,128)(2,1)} %w_hbm.1, s32[3,1024]{1,0:T(4,128)} %src_hbm.1, f32[3,1024]{1,0:T(4,128)} %weight_hbm.1, s32[8,256]{1,0:T(8,128)} %bitcast.63, ...), custom_call_target="tpu_custom_call" | custom-call | tf_op jit(solution)/shard_map/pallas_call | solution.py:34
  12.6 0.4 collective-permute-done.1.right_ref
  13.0 4.4 %shard_map.184 = (bf16[256,512]{1,0:T(8,128)(2,1)S(1)}, bf16[98,256]{1,0:T(8,128)(2,1)S(1)}, bf16[98,128]{1,0:T(8,128)(2,1)S(1)}, bf16[98,128]{1,0:T(8,128)(2,1)...) custom-call(bf16[512,512]{1,0:T(8,128)(2,1)} %w_out_ref.1, ...), custom_call_target="tpu_custom_call" | custom-call | tf_op jit(solution)/shard_map/pallas_call | solution.py:34
  17.4 0.4 collective-permute-start.4
  17.9 4.7 %collective-permute-start.6 = (bf16[98,128]{1,0:T(8,128)(2,1)S(1)}, bf16[98,128]{1,0:T(8,128)(2,1)S(1)}, u32[]{:S(2)}, u32[]{:S(2)}) collective-permute-start(bf16[98,128]{1,0:T(8,128)(2,1)S(1)} %get-tuple-element.68), channel_id=1, source_target_pairs={{4,0},{8,4},{12,8},{16,12},{20,16},{24,20},{28,24},{0,28},{5,1},{9... | collective-permute-start | bytes 75272 | tf_op jit(solution)/shard_map/ppermute | solution.py:516
  22.5 1.3 %collective-permute-start.3 = (bf16[98,256]{1,0:T(8,128)(2,1)S(1)}, bf16[98,256]{1,0:T(8,128)(2,1)S(1)}, u32[]{:S(2)}, u32[]{:S(2)}) collective-permute-start(bf16[98,256]{1,0:T(8,128)(2,1)S(1)} %get-tuple-element.66.refs_0_), channel_id=1, source_target_pairs={{0,2},{1,3},{2,0},{3,1},{4,6},{5,7},{6,4},{7,5},{8,10},{9,11},{10,... | collective-permute-start | bytes 150536 | tf_op jit(solution)/shard_map/ppermute | solution.py:426
  23.8 0.6 collective-permute-done.5.left_ref
  24.4 0.4 collective-permute-start.9
  24.7 1.5 %collective-permute-start.8 = (bf16[98,256]{1,0:T(8,128)(2,1)S(1)}, bf16[98,256]{1,0:T(8,128)(2,1)S(1)}, u32[]{:S(2)}, u32[]{:S(2)}) collective-permute-start(bf16[98,256]{1,0:T(8,128)(2,1)S(1)} %shard_map.185.refs_4_), channel_id=1, source_target_pairs={{0,2},{1,3},{2,0},{3,1},{4,6},{5,7},{6,4},{7,5},{8,10},{9,11},{10,... | collective-permute-start | bytes 150536 | tf_op jit(solution)/shard_map/ppermute | solution.py:426
  26.3 0.7 collective-permute-done.3.refs_2_
  27.0 1.2 %collective-permute-done.9.refs_7_ = bf16[98,256]{1,0:T(8,128)(2,1)S(1)} collective-permute-done((bf16[98,256]{1,0:T(8,128)(2,1)S(1)}, bf16[98,256]{1,0:T(8,128)(2,1)S(1)}, u32[]{:S(2)}, u32[]{:S(2)}) %collective-permute-start.9) | collective-permute-done | bytes 50208 | tf_op jit(solution)/shard_map/ppermute | solution.py:426
  28.2 1.5 %collective-permute-done.8.refs_6_ = bf16[98,256]{1,0:T(8,128)(2,1)S(1)} collective-permute-done((bf16[98,256]{1,0:T(8,128)(2,1)S(1)}, bf16[98,256]{1,0:T(8,128)(2,1)S(1)}, u32[]{:S(2)}, u32[]{:S(2)}) %collective-permute-start.8) | collective-permute-done | bytes 50208 | tf_op jit(solution)/shard_map/ppermute | solution.py:426
  29.7 1.4 %shard_map.186 = (bf16[98,1024]{1,0:T(8,128)(2,1)S(1)}, bf16[98,128]{1,0:T(8,128)(2,1)S(1)}, bf16[98,128]{1,0:T(8,128)(2,1)S(1)}, f32[1,128]{1,0:T(1,128)S(1)}) custom-call(f32[98,1024]{1,0:T(8,128)S(1)} %copy-done.3, f32[98,1024]{1,0:T(8,128)S(1)} %copy-done.4, f32[1,1024]{1,0:T(1,128)S(1)} %bitcast.70, f32[1,98]{1,0:T(1,128)S(1)} %bitcast.71, ...), custom_call_target="tpu_custom_call" | custom-call | tf_op jit(solution)/shard_map/pallas_call | solution.py:34
  31.2 1.2 %collective-permute-start.10 = (bf16[98,128]{1,0:T(8,128)(2,1)S(1)}, bf16[98,128]{1,0:T(8,128)(2,1)S(1)}, u32[]{:S(2)}, u32[]{:S(2)}) collective-permute-start(bf16[98,128]{1,0:T(8,128)(2,1)S(1)} %get-tuple-element.71), channel_id=1, source_target_pairs={{0,4},{4,8},{8,12},{12,16},{16,20},{20,24},{24,28},{28,0},{1,5},{5... | collective-permute-start | bytes 75272 | tf_op jit(solution)/shard_map/ppermute | solution.py:515
  32.4 4.0 %collective-permute-start.11 = (bf16[98,128]{1,0:T(8,128)(2,1)S(1)}, bf16[98,128]{1,0:T(8,128)(2,1)S(1)}, u32[]{:S(2)}, u32[]{:S(2)}) collective-permute-start(bf16[98,128]{1,0:T(8,128)(2,1)S(1)} %get-tuple-element.72), channel_id=1, source_target_pairs={{4,0},{8,4},{12,8},{16,12},{20,16},{24,20},{28,24},{0,28},{5,1},{9... | collective-permute-start | bytes 75272 | tf_op jit(solution)/shard_map/ppermute | solution.py:516
  36.4 1.1 %shard_map.187 = (f32[98,256]{1,0:T(8,128)S(1)}, bf16[512,2048]{1,0:T(8,128)(2,1)S(1)}) custom-call(bf16[512,1024]{1,0:T(8,128)(2,1)S(1)} %get-tuple-element.62.mix_ref, bf16[98,1024]{1,0:T(8,128)(2,1)S(1)} %get-tuple-element.69.grad_ref, s32[8,256]{1,0:T(8,128)S(1)} %bitcast.65), custom_call_target="tpu_custom_call" | custom-call | tf_op jit(solution)/shard_map/pallas_call | solution.py:34
  37.5 0.5 collective-permute-done.10.from_left_ref
  38.0 2.8 %shard_map.188 = (f32[256,512]{1,0:T(8,128)S(1)}, bf16[256,512]{1,0:T(8,128)(2,1)S(1)}, bf16[512,512]{1,0:T(8,128)(2,1)S(1)}, bf16[16,16,768]{2,1,0:T(8,128)(2,1)S(1)}, f32[16,16,768]{2,1,0:T(8,128)S(1)}) custom-call(s32[1,1]{1,0:T(1,128)} %bitcast.34.count_ref, f32[98,256]{1,0:T(8,128)S(1)} %get-tuple-element.70.own_ref, ...), custom_call_target="tpu_custom_call" | custom-call | tf_op jit(solution)/shard_map/pallas_call | solution.py:34
  40.8 1.8 %shard_map.189 = (bf16[256,512]{1,0:T(8,128)(2,1)S(1)}, bf16[2048,512]{1,0:T(8,128)(2,1)S(1)}) custom-call(bf16[256,512]{1,0:T(8,128)(2,1)S(1)} %get-tuple-element.78.mixed_ref, f32[256,128]{1,0:T(8,128)S(1)} %get-tuple-element.79.probs_ref, bf16[8,256,512]{2,1,0:T(8,128)(2,1)S(1)} %get-tuple-element.80.values_ref, ...), custom_call_target="tpu_custom_call" | custom-call | tf_op jit(solution)/shard_map/pallas_call | solution.py:34
  42.6 1.5 %shard_map.190 = (bf16[512,512]{1,0:T(8,128)(2,1)S(1)}, bf16[128,512]{1,0:T(8,128)(2,1)S(1)}, bf16[128,512]{1,0:T(8,128)(2,1)S(1)}) custom-call(bf16[2048,512]{1,0:T(8,128)(2,1)S(1)} %get-tuple-element.83.edge_ref, bf16[512,2048]{1,0:T(8,128)(2,1)S(1)} %get-tuple-element.76.hot_ref, bf16[512,512]{1,0:T(8,128)(2,1)S(1)} %get-tuple-element.84.grad_value_ref, ...), custom_call_target="tpu_custom_call" | custom-call | tf_op jit(solution)/shard_map/pallas_call | solution.py:34
  44.2 1.0 %shard_map.191 = (bf16[16,16,1024]{2,1,0:T(8,128)(2,1)S(1)}, f32[16,16,1024]{2,1,0:T(8,128)S(1)}) custom-call(bf16[256,512]{1,0:T(8,128)(2,1)S(1)} %get-tuple-element.59.features_ref, bf16[128,512]{1,0:T(8,128)(2,1)S(1)} %collective-permute-done.left_ref, bf16[128,512]{1,0:T(8,128)(2,1)S(1)} %collective-permute-done.1.right_ref, ...), custom_call_target="tpu_custom_call" | custom-call | tf_op jit(solution)/shard_map/pallas_call | solution.py:34
  45.3 0.5 collective-permute-start.17
  45.8 2.0 %collective-permute-done.17 = bf16[16,16,768]{2,1,0:T(8,128)(2,1)S(1)} collective-permute-done((bf16[16,16,768]{2,1,0:T(8,128)(2,1)S(1)}, bf16[16,16,768]{2,1,0:T(8,128)(2,1)S(1)}, u32[]{:S(2)}, u32[]{:S(2)}) %collective-permute-start.17) | collective-permute-done | bytes 393248 | tf_op jit(solution)/shard_map/ppermute | solution.py:426
  47.7 0.2 shard_map.195
  48.0 0.7 collective-permute-start.18
  48.8 1.4 %collective-permute-start.13 = (bf16[8,16,512]{2,1,0:T(8,128)(2,1)S(1)}, bf16[8,16,512]{2,1,0:T(8,128)(2,1)S(1)}, u32[]{:S(2)}, u32[]{:S(2)}) collective-permute-start(bf16[8,16,512]{2,1,0:T(8,128)(2,1)S(1)} %get-tuple-element.89), channel_id=1, source_target_pairs={{0,2},{1,3},{2,0},{3,1},{4,6},{5,7},{6,4},{7,5},{8,10},{9,11},{10,... | collective-permute-start | bytes 393224 | tf_op jit(solution)/shard_map/ppermute | solution.py:426
  50.3 5.6 %collective-permute-done.18 = bf16[8,16,768]{2,1,0:T(8,128)(2,1)S(1)} collective-permute-done((bf16[8,16,768]{2,1,0:T(8,128)(2,1)S(1)}, bf16[8,16,768]{2,1,0:T(8,128)(2,1)S(1)}, u32[]{:S(2)}, u32[]{:S(2)}) %collective-permute-start.18) | collective-permute-done | bytes 196640 | tf_op jit(solution)/shard_map/ppermute | solution.py:426
  56.1 1.7 %collective-permute-done.13 = bf16[8,16,512]{2,1,0:T(8,128)(2,1)S(1)} collective-permute-done((bf16[8,16,512]{2,1,0:T(8,128)(2,1)S(1)}, bf16[8,16,512]{2,1,0:T(8,128)(2,1)S(1)}, u32[]{:S(2)}, u32[]{:S(2)}) %collective-permute-start.13) | collective-permute-done | bytes 131104 | tf_op jit(solution)/shard_map/ppermute | solution.py:426
  57.8 0.4 collective-permute-start.14
  58.3 0.7 collective-permute-start.16
  59.0 2.4 %collective-permute-done.19 = bf16[2,32,768]{2,1,0:T(8,128)(2,1)S(1)} collective-permute-done((bf16[2,32,768]{2,1,0:T(8,128)(2,1)S(1)}, bf16[2,32,768]{2,1,0:T(8,128)(2,1)S(1)}, u32[]{:S(2)}, u32[]{:S(2)}) %collective-permute-start.19) | collective-permute-done | bytes 98336 | tf_op jit(solution)/shard_map/ppermute | solution.py:426
  61.4 0.8 collective-permute-done.14
  62.2 0.4 collective-permute-done.16
  62.8 1.4 %collective-permute-start.20 = (bf16[2,16,1792]{2,1,0:T(8,128)(2,1)S(1)}, bf16[2,16,1792]{2,1,0:T(8,128)(2,1)S(1)}, u32[]{:S(2)}, u32[]{:S(2)}) collective-permute-start(bf16[2,16,1792]{2,1,0:T(8,128)(2,1)S(1)} %get-tuple-element.103), channel_id=1, source_target_pairs={{0,4},{4,0},{8,12},{12,8},{16,20},{20,16},{24,28},{28,24},{1,5},{5... | collective-permute-start | bytes 344072 | tf_op jit(solution)/shard_map/ppermute | solution.py:426
  64.2 0.7 collective-permute-start.25
  64.9 4.0 %collective-permute-start.26 = (bf16[128,512]{1,0:T(8,128)(2,1)S(1)}, bf16[128,512]{1,0:T(8,128)(2,1)S(1)}, u32[]{:S(2)}, u32[]{:S(2)}) collective-permute-start(bf16[128,512]{1,0:T(8,128)(2,1)S(1)} %get-tuple-element.111), channel_id=1, source_target_pairs={{4,0},{8,4},{12,8},{16,12},{20,16},{24,20},{28,24},{0,28},{5,1},{9... | collective-permute-start | bytes 393224 | tf_op jit(solution)/shard_map/ppermute | solution.py:516
  68.9 0.8 collective-permute-done.20
  69.8 4.0 %collective-permute-start.21 = (bf16[1,16,1792]{2,1,0:T(8,128)(2,1)S(1)}, bf16[1,16,1792]{2,1,0:T(8,128)(2,1)S(1)}, u32[]{:S(2)}, u32[]{:S(2)}) collective-permute-start(bf16[1,16,1792]{2,1,0:T(8,128)(2,1)S(1)} %get-tuple-element.105), channel_id=1, source_target_pairs={{0,16},{4,20},{8,24},{12,28},{16,0},{20,4},{24,8},{28,12},{1,17},{... | collective-permute-start | bytes 172040 | tf_op jit(solution)/shard_map/ppermute | solution.py:426
  73.9 2.2 %collective-permute-done.21.arrived_ref = bf16[1,16,1792]{2,1,0:T(8,128)(2,1)S(1)} collective-permute-done((bf16[1,16,1792]{2,1,0:T(8,128)(2,1)S(1)}, bf16[1,16,1792]{2,1,0:T(8,128)(2,1)S(1)}, u32[]{:S(2)}, u32[]{:S(2)}) %collective-permute-start.21) | collective-permute-done | bytes 57376 | tf_op jit(solution)/shard_map/ppermute | solution.py:426
  76.2 0.7 collective-permute-start.23
  76.9 1.2 %collective-permute-start.22 = (bf16[16,1792]{1,0:T(8,128)(2,1)S(1)}, bf16[16,1792]{1,0:T(8,128)(2,1)S(1)}, u32[]{:S(2)}, u32[]{:S(2)}) collective-permute-start(bf16[16,1792]{1,0:T(8,128)(2,1)S(1)} %bitcast.53), channel_id=1, source_target_pairs={{0,1},{1,0},{2,3},{3,2},{4,5},{5,4},{6,7},{7,6},{8,9},{9,8},{10,11... | collective-permute-start | bytes 172040 | tf_op jit(solution)/shard_map/ppermute | solution.py:426
  78.1 0.6 shard_map.201.own_ref
  78.7 1.2 %shard_map.202 = bf16[256,512]{1,0:T(8,128)(2,1)} custom-call(bf16[256,512]{1,0:T(8,128)(2,1)S(1)} %bitcast.39, f32[1,512]{1,0:T(1,128)S(1)} %bitcast.69, f32[256,512]{1,0:T(8,128)S(1)} %shard_map.201.own_ref, bf16[128,512]{1,0:T(8,128)(2,1)S(1)} %collective-permute-done.25.from_left_ref, bf16[128,512]{1,0:T(8,128)(2,1)S(1)} %collective-permute-done.26.from_right_ref, ...), custom_call_target="tpu_custom_call" | custom-call | tf_op jit(solution)/shard_map/pallas_call | solution.py:34
  79.8 1.2 %collective-permute-done.23.refs_2_ = bf16[16,1792]{1,0:T(8,128)(2,1)S(1)} collective-permute-done((bf16[16,1792]{1,0:T(8,128)(2,1)S(1)}, bf16[16,1792]{1,0:T(8,128)(2,1)S(1)}, u32[]{:S(2)}, u32[]{:S(2)}) %collective-permute-start.23) | collective-permute-done | bytes 57376 | tf_op jit(solution)/shard_map/ppermute | solution.py:426
  81.0 0.8 %shard_map.200 = (f32[4,16,1536]{2,1,0:T(8,128)}, f32[4,16,512]{2,1,0:T(8,128)}, f32[4,16,98]{2,1,0:T(8,128)}, f32[1,1]{1,0:T(1,128)}) custom-call(bf16[98,512]{1,0:T(8,128)(2,1)S(1)} %bitcast.44, bf16[16,1792]{1,0:T(8,128)(2,1)S(1)} %bitcast.54, bf16[16,1792]{1,0:T(8,128)(2,1)S(1)} %collective-permute-done.22.refs_1_, ...), custom_call_target="tpu_custom_call" | custom-call | tf_op jit(solution)/shard_map/pallas_call | solution.py:34
  (47 shorter events, 1.2 us)
Async XLA Ops:
  0.6 12.3 %copy-start.6 = (s32[1,256]{1,0:T(1,128)S(1)}, s32[1,256]{1,0:T(1,128)}, u32[]{:S(2)}) copy-start(s32[1,256]{1,0:T(1,128)} %border_ref.5) | copy-start | bytes 3076
  0.6 12.3 %copy-start = (bf16[1,256,512]{2,1,0:T(8,128)(2,1)S(1)}, bf16[1,256,512]{2,1,0:T(8,128)(2,1)}, u32[]{:S(2)}) copy-start(bf16[1,256,512]{2,1,0:T(8,128)(2,1)} %param.15) | copy-start | bytes 786436
  0.7 12.3 %copy-start.5 = (s32[256,8]{0,1:T(8,128)S(1)}, s32[256,8]{0,1:T(8,128)}, u32[]{:S(2)}) copy-start(s32[256,8]{0,1:T(8,128)} %param.20) | copy-start | bytes 24580
  2.1 10.4 %collective-permute-start = (bf16[128,512]{1,0:T(8,128)(2,1)S(1)}, bf16[128,512]{1,0:T(8,128)(2,1)S(1)}, u32[]{:S(2)}, u32[]{:S(2)}) collective-permute-start(bf16[128,512]{1,0:T(8,128)(2,1)S(1)} %get-tuple-element.60), channel_id=1, source_target_pairs={{0,4},{4,8},{8,12},{12,16},{16,20},{20,24},{24,28},{28,0},{1,5},{5... | collective-permute-start | bytes 393224 | tf_op jit(solution)/shard_map/ppermute | solution.py:515
  5.2 7.8 %collective-permute-start.1 = (bf16[128,512]{1,0:T(8,128)(2,1)S(1)}, bf16[128,512]{1,0:T(8,128)(2,1)S(1)}, u32[]{:S(2)}, u32[]{:S(2)}) collective-permute-start(bf16[128,512]{1,0:T(8,128)(2,1)S(1)} %get-tuple-element.61), channel_id=1, source_target_pairs={{4,0},{8,4},{12,8},{16,12},{20,16},{24,20},{28,24},{0,28},{5,1},{9... | collective-permute-start | bytes 393224 | tf_op jit(solution)/shard_map/ppermute | solution.py:516
  13.0 16.7 %copy-start.3 = (f32[98,1024]{1,0:T(8,128)S(1)}, f32[98,1024]{1,0:T(8,128)}, u32[]{:S(2)}) copy-start(f32[98,1024]{1,0:T(8,128)} %state_ref.1) | copy-start | bytes 1204228
  13.0 16.7 %copy-start.4 = (f32[98,1024]{1,0:T(8,128)S(1)}, f32[98,1024]{1,0:T(8,128)}, u32[]{:S(2)}) copy-start(f32[98,1024]{1,0:T(8,128)} %target_ref.1) | copy-start | bytes 1204228
  13.0 16.7 %copy-start.8 = (f32[1024]{0:T(1024)S(1)}, f32[1024]{0:T(1024)}, u32[]{:S(2)}) copy-start(f32[1024]{0:T(1024)} %param.28) | copy-start | bytes 12292
  13.0 16.7 %copy-start.9 = (f32[98]{0:T(128)S(1)}, f32[98]{0:T(128)}, u32[]{:S(2)}) copy-start(f32[98]{0:T(128)} %param.29) | copy-start | bytes 1180
  17.4 20.6 %copy-start.1 = (bf16[512,512]{1,0:T(8,128)(2,1)S(1)}, bf16[512,512]{1,0:T(8,128)(2,1)}, u32[]{:S(2)}) copy-start(bf16[512,512]{1,0:T(8,128)(2,1)} %w_out_ref.1) | copy-start | bytes 1572868
  17.4 20.6 %copy-start.2 = (bf16[512,98]{0,1:T(8,128)(2,1)S(1)}, bf16[512,98]{0,1:T(8,128)(2,1)}, u32[]{:S(2)}) copy-start(bf16[512,98]{0,1:T(8,128)(2,1)} %param.23) | copy-start | bytes 301060
  17.4 8.8 %collective-permute-start.4 = (bf16[98,256]{1,0:T(8,128)(2,1)S(1)}, bf16[98,256]{1,0:T(8,128)(2,1)S(1)}, u32[]{:S(2)}, u32[]{:S(2)}) collective-permute-start(bf16[98,256]{1,0:T(8,128)(2,1)S(1)} %get-tuple-element.66.refs_0_), channel_id=1, source_target_pairs={{0,3},{1,2},{2,1},{3,0},{4,7},{5,6},{6,5},{7,4},{8,11},{9,10},{10,... | collective-permute-start | bytes 150536 | tf_op jit(solution)/shard_map/ppermute | solution.py:426
  17.8 6.5 %collective-permute-start.5 = (bf16[98,128]{1,0:T(8,128)(2,1)S(1)}, bf16[98,128]{1,0:T(8,128)(2,1)S(1)}, u32[]{:S(2)}, u32[]{:S(2)}) collective-permute-start(bf16[98,128]{1,0:T(8,128)(2,1)S(1)} %get-tuple-element.67), channel_id=1, source_target_pairs={{0,4},{4,8},{8,12},{12,16},{16,20},{20,24},{24,28},{28,0},{1,5},{5... | collective-permute-start | bytes 75272 | tf_op jit(solution)/shard_map/ppermute | solution.py:515
  17.9 6.5 %collective-permute-start.6 = (bf16[98,128]{1,0:T(8,128)(2,1)S(1)}, bf16[98,128]{1,0:T(8,128)(2,1)S(1)}, u32[]{:S(2)}, u32[]{:S(2)}) collective-permute-start(bf16[98,128]{1,0:T(8,128)(2,1)S(1)} %get-tuple-element.68), channel_id=1, source_target_pairs={{4,0},{8,4},{12,8},{16,12},{20,16},{24,20},{28,24},{0,28},{5,1},{9... | collective-permute-start | bytes 75272 | tf_op jit(solution)/shard_map/ppermute | solution.py:516
  22.5 4.5 %collective-permute-start.3 = (bf16[98,256]{1,0:T(8,128)(2,1)S(1)}, bf16[98,256]{1,0:T(8,128)(2,1)S(1)}, u32[]{:S(2)}, u32[]{:S(2)}) collective-permute-start(bf16[98,256]{1,0:T(8,128)(2,1)S(1)} %get-tuple-element.66.refs_0_), channel_id=1, source_target_pairs={{0,2},{1,3},{2,0},{3,1},{4,6},{5,7},{6,4},{7,5},{8,10},{9,11},{10,... | collective-permute-start | bytes 150536 | tf_op jit(solution)/shard_map/ppermute | solution.py:426
  23.8 3.2 %collective-permute-start.2 = (bf16[98,256]{1,0:T(8,128)(2,1)S(1)}, bf16[98,256]{1,0:T(8,128)(2,1)S(1)}, u32[]{:S(2)}, u32[]{:S(2)}) collective-permute-start(bf16[98,256]{1,0:T(8,128)(2,1)S(1)} %get-tuple-element.66.refs_0_), channel_id=1, source_target_pairs={{0,1},{1,0},{2,3},{3,2},{4,5},{5,4},{6,7},{7,6},{8,9},{9,8},{10,11... | collective-permute-start | bytes 150536 | tf_op jit(solution)/shard_map/ppermute | solution.py:426
  24.4 3.8 %collective-permute-start.9 = (bf16[98,256]{1,0:T(8,128)(2,1)S(1)}, bf16[98,256]{1,0:T(8,128)(2,1)S(1)}, u32[]{:S(2)}, u32[]{:S(2)}) collective-permute-start(bf16[98,256]{1,0:T(8,128)(2,1)S(1)} %shard_map.185.refs_4_), channel_id=1, source_target_pairs={{0,3},{1,2},{2,1},{3,0},{4,7},{5,6},{6,5},{7,4},{8,11},{9,10},{10,... | collective-permute-start | bytes 150536 | tf_op jit(solution)/shard_map/ppermute | solution.py:426
  24.7 4.9 %collective-permute-start.8 = (bf16[98,256]{1,0:T(8,128)(2,1)S(1)}, bf16[98,256]{1,0:T(8,128)(2,1)S(1)}, u32[]{:S(2)}, u32[]{:S(2)}) collective-permute-start(bf16[98,256]{1,0:T(8,128)(2,1)S(1)} %shard_map.185.refs_4_), channel_id=1, source_target_pairs={{0,2},{1,3},{2,0},{3,1},{4,6},{5,7},{6,4},{7,5},{8,10},{9,11},{10,... | collective-permute-start | bytes 150536 | tf_op jit(solution)/shard_map/ppermute | solution.py:426
  26.2 3.5 %collective-permute-start.7 = (bf16[98,256]{1,0:T(8,128)(2,1)S(1)}, bf16[98,256]{1,0:T(8,128)(2,1)S(1)}, u32[]{:S(2)}, u32[]{:S(2)}) collective-permute-start(bf16[98,256]{1,0:T(8,128)(2,1)S(1)} %shard_map.185.refs_4_), channel_id=1, source_target_pairs={{0,1},{1,0},{2,3},{3,2},{4,5},{5,4},{6,7},{7,6},{8,9},{9,8},{10,11... | collective-permute-start | bytes 150536 | tf_op jit(solution)/shard_map/ppermute | solution.py:426
  31.2 6.8 %collective-permute-start.10 = (bf16[98,128]{1,0:T(8,128)(2,1)S(1)}, bf16[98,128]{1,0:T(8,128)(2,1)S(1)}, u32[]{:S(2)}, u32[]{:S(2)}) collective-permute-start(bf16[98,128]{1,0:T(8,128)(2,1)S(1)} %get-tuple-element.71), channel_id=1, source_target_pairs={{0,4},{4,8},{8,12},{12,16},{16,20},{20,24},{24,28},{28,0},{1,5},{5... | collective-permute-start | bytes 75272 | tf_op jit(solution)/shard_map/ppermute | solution.py:515
  32.4 5.6 %collective-permute-start.11 = (bf16[98,128]{1,0:T(8,128)(2,1)S(1)}, bf16[98,128]{1,0:T(8,128)(2,1)S(1)}, u32[]{:S(2)}, u32[]{:S(2)}) collective-permute-start(bf16[98,128]{1,0:T(8,128)(2,1)S(1)} %get-tuple-element.72), channel_id=1, source_target_pairs={{4,0},{8,4},{12,8},{16,12},{20,16},{24,20},{28,24},{0,28},{5,1},{9... | collective-permute-start | bytes 75272 | tf_op jit(solution)/shard_map/ppermute | solution.py:516
  45.2 3.5 %collective-permute-start.12 = (bf16[16,16,1024]{2,1,0:T(8,128)(2,1)S(1)}, bf16[16,16,1024]{2,1,0:T(8,128)(2,1)S(1)}, u32[]{:S(2)}, u32[]{:S(2)}) collective-permute-start(bf16[16,16,1024]{2,1,0:T(8,128)(2,1)S(1)} %get-tuple-element.87), channel_id=1, source_target_pairs={{0,1},{1,0},{2,3},{3,2},{4,5},{5,4},{6,7},{7,6},{8,9},{9,8},{10,11... | collective-permute-start | bytes 1572872 | tf_op jit(solution)/shard_map/ppermute | solution.py:426
  45.3 2.5 %collective-permute-start.17 = (bf16[16,16,768]{2,1,0:T(8,128)(2,1)S(1)}, bf16[16,16,768]{2,1,0:T(8,128)(2,1)S(1)}, u32[]{:S(2)}, u32[]{:S(2)}) collective-permute-start(bf16[16,16,768]{2,1,0:T(8,128)(2,1)S(1)} %get-tuple-element.97), channel_id=1, source_target_pairs={{0,1},{1,0},{2,3},{3,2},{4,5},{5,4},{6,7},{7,6},{8,9},{9,8},{10,11... | collective-permute-start | bytes 1179656 | tf_op jit(solution)/shard_map/ppermute | solution.py:426
  48.0 7.8 %collective-permute-start.18 = (bf16[8,16,768]{2,1,0:T(8,128)(2,1)S(1)}, bf16[8,16,768]{2,1,0:T(8,128)(2,1)S(1)}, u32[]{:S(2)}, u32[]{:S(2)}) collective-permute-start(bf16[8,16,768]{2,1,0:T(8,128)(2,1)S(1)} %get-tuple-element.99), channel_id=1, source_target_pairs={{0,2},{1,3},{2,0},{3,1},{4,6},{5,7},{6,4},{7,5},{8,10},{9,11},{10,... | collective-permute-start | bytes 589832 | tf_op jit(solution)/shard_map/ppermute | solution.py:426
  48.8 9.0 %collective-permute-start.13 = (bf16[8,16,512]{2,1,0:T(8,128)(2,1)S(1)}, bf16[8,16,512]{2,1,0:T(8,128)(2,1)S(1)}, u32[]{:S(2)}, u32[]{:S(2)}) collective-permute-start(bf16[8,16,512]{2,1,0:T(8,128)(2,1)S(1)} %get-tuple-element.89), channel_id=1, source_target_pairs={{0,2},{1,3},{2,0},{3,1},{4,6},{5,7},{6,4},{7,5},{8,10},{9,11},{10,... | collective-permute-start | bytes 393224 | tf_op jit(solution)/shard_map/ppermute | solution.py:426
  50.3 8.0 %collective-permute-start.15 = (bf16[2,64,512]{2,1,0:T(8,128)(2,1)S(1)}, bf16[2,64,512]{2,1,0:T(8,128)(2,1)S(1)}, u32[]{:S(2)}, u32[]{:S(2)}) collective-permute-start(bf16[2,64,512]{2,1,0:T(8,128)(2,1)S(1)} %get-tuple-element.93), channel_id=1, source_target_pairs={{0,8},{4,12},{8,0},{12,4},{16,24},{20,28},{24,16},{28,20},{1,9},{5... | collective-permute-start | bytes 393224 | tf_op jit(solution)/shard_map/ppermute | solution.py:426
  56.0 5.4 %collective-permute-start.19 = (bf16[2,32,768]{2,1,0:T(8,128)(2,1)S(1)}, bf16[2,32,768]{2,1,0:T(8,128)(2,1)S(1)}, u32[]{:S(2)}, u32[]{:S(2)}) collective-permute-start(bf16[2,32,768]{2,1,0:T(8,128)(2,1)S(1)} %get-tuple-element.101), channel_id=1, source_target_pairs={{0,8},{4,12},{8,0},{12,4},{16,24},{20,28},{24,16},{28,20},{1,9},{5... | collective-permute-start | bytes 294920 | tf_op jit(solution)/shard_map/ppermute | solution.py:426
  57.8 4.3 %collective-permute-start.14 = (bf16[2,32,512]{2,1,0:T(8,128)(2,1)S(1)}, bf16[2,32,512]{2,1,0:T(8,128)(2,1)S(1)}, u32[]{:S(2)}, u32[]{:S(2)}) collective-permute-start(bf16[2,32,512]{2,1,0:T(8,128)(2,1)S(1)} %get-tuple-element.91), channel_id=1, source_target_pairs={{0,8},{4,12},{8,0},{12,4},{16,24},{20,28},{24,16},{28,20},{1,9},{5... | collective-permute-start | bytes 196616 | tf_op jit(solution)/shard_map/ppermute | solution.py:426
  58.3 4.3 %collective-permute-start.16 = (bf16[4,16,512]{2,1,0:T(8,128)(2,1)S(1)}, bf16[4,16,512]{2,1,0:T(8,128)(2,1)S(1)}, u32[]{:S(2)}, u32[]{:S(2)}) collective-permute-start(bf16[4,16,512]{2,1,0:T(8,128)(2,1)S(1)} %get-tuple-element.95), channel_id=1, source_target_pairs={{0,2},{1,3},{2,0},{3,1},{4,6},{5,7},{6,4},{7,5},{8,10},{9,11},{10,... | collective-permute-start | bytes 196616 | tf_op jit(solution)/shard_map/ppermute | solution.py:426
  62.8 15.9 %copy-start.7 = (f32[512]{0:T(512)S(1)}, f32[512]{0:T(512)}, u32[]{:S(2)}) copy-start(f32[512]{0:T(512)} %param.16) | copy-start | bytes 6148
  62.8 6.9 %collective-permute-start.20 = (bf16[2,16,1792]{2,1,0:T(8,128)(2,1)S(1)}, bf16[2,16,1792]{2,1,0:T(8,128)(2,1)S(1)}, u32[]{:S(2)}, u32[]{:S(2)}) collective-permute-start(bf16[2,16,1792]{2,1,0:T(8,128)(2,1)S(1)} %get-tuple-element.103), channel_id=1, source_target_pairs={{0,4},{4,0},{8,12},{12,8},{16,20},{20,16},{24,28},{28,24},{1,5},{5... | collective-permute-start | bytes 344072 | tf_op jit(solution)/shard_map/ppermute | solution.py:426
  64.2 14.5 %collective-permute-start.25 = (bf16[128,512]{1,0:T(8,128)(2,1)S(1)}, bf16[128,512]{1,0:T(8,128)(2,1)S(1)}, u32[]{:S(2)}, u32[]{:S(2)}) collective-permute-start(bf16[128,512]{1,0:T(8,128)(2,1)S(1)} %get-tuple-element.110), channel_id=1, source_target_pairs={{0,4},{4,8},{8,12},{12,16},{16,20},{20,24},{24,28},{28,0},{1,5},{5... | collective-permute-start | bytes 393224 | tf_op jit(solution)/shard_map/ppermute | solution.py:515
  64.9 13.8 %collective-permute-start.26 = (bf16[128,512]{1,0:T(8,128)(2,1)S(1)}, bf16[128,512]{1,0:T(8,128)(2,1)S(1)}, u32[]{:S(2)}, u32[]{:S(2)}) collective-permute-start(bf16[128,512]{1,0:T(8,128)(2,1)S(1)} %get-tuple-element.111), channel_id=1, source_target_pairs={{4,0},{8,4},{12,8},{16,12},{20,16},{24,20},{28,24},{0,28},{5,1},{9... | collective-permute-start | bytes 393224 | tf_op jit(solution)/shard_map/ppermute | solution.py:516
  69.8 6.2 %collective-permute-start.21 = (bf16[1,16,1792]{2,1,0:T(8,128)(2,1)S(1)}, bf16[1,16,1792]{2,1,0:T(8,128)(2,1)S(1)}, u32[]{:S(2)}, u32[]{:S(2)}) collective-permute-start(bf16[1,16,1792]{2,1,0:T(8,128)(2,1)S(1)} %get-tuple-element.105), channel_id=1, source_target_pairs={{0,16},{4,20},{8,24},{12,28},{16,0},{20,4},{24,8},{28,12},{1,17},{... | collective-permute-start | bytes 172040 | tf_op jit(solution)/shard_map/ppermute | solution.py:426
  76.2 3.7 %collective-permute-start.24 = (bf16[16,1792]{1,0:T(8,128)(2,1)S(1)}, bf16[16,1792]{1,0:T(8,128)(2,1)S(1)}, u32[]{:S(2)}, u32[]{:S(2)}) collective-permute-start(bf16[16,1792]{1,0:T(8,128)(2,1)S(1)} %bitcast.51), channel_id=1, source_target_pairs={{0,3},{1,2},{2,1},{3,0},{4,7},{5,6},{6,5},{7,4},{8,11},{9,10},{10,... | collective-permute-start | bytes 172040 | tf_op jit(solution)/shard_map/ppermute | solution.py:426
  76.2 4.8 %collective-permute-start.23 = (bf16[16,1792]{1,0:T(8,128)(2,1)S(1)}, bf16[16,1792]{1,0:T(8,128)(2,1)S(1)}, u32[]{:S(2)}, u32[]{:S(2)}) collective-permute-start(bf16[16,1792]{1,0:T(8,128)(2,1)S(1)} %bitcast.52), channel_id=1, source_target_pairs={{0,2},{1,3},{2,0},{3,1},{4,6},{5,7},{6,4},{7,5},{8,10},{9,11},{10,... | collective-permute-start | bytes 172040 | tf_op jit(solution)/shard_map/ppermute | solution.py:426
  76.9 4.1 %collective-permute-start.22 = (bf16[16,1792]{1,0:T(8,128)(2,1)S(1)}, bf16[16,1792]{1,0:T(8,128)(2,1)S(1)}, u32[]{:S(2)}, u32[]{:S(2)}) collective-permute-start(bf16[16,1792]{1,0:T(8,128)(2,1)S(1)} %bitcast.53), channel_id=1, source_target_pairs={{0,1},{1,0},{2,3},{3,2},{4,5},{5,4},{6,7},{7,6},{8,9},{9,8},{10,11... | collective-permute-start | bytes 172040 | tf_op jit(solution)/shard_map/ppermute | solution.py:426
